TPU v7x, 32 devices: a whole 2x2x4 slice. The times are simulated.
32 devices in a mesh: seq: 16 (over z, y, core), dp: 2 (over x).
Axes of the slice: x: 2, y: 2, z: 4, core: 2. Of those that a mesh axis runs over, the one named last changes fastest.
Arguments:
- queries: bfloat16 [2, 2048, 1024], P('dp', 'seq'), may hold values from -6 to 6
- keys: bfloat16 [2, 2048, 1024], P('dp', 'seq'), may hold values from -6 to 6
- values: bfloat16 [2, 2048, 1024], P('dp', 'seq'), may hold values from -6 to 6
- d_out: bfloat16 [2, 2048, 1024], P('dp', 'seq'), may hold values from -6 to 6
- segment_ids: int32 [2, 2048], P('dp', 'seq'), may hold values from 0 to 2, never falling along the last dimension, each value on 1 to 1536 neighbouring positions
- block_bucket: int32 [2, 16], P('dp', 'seq'), may hold values from 0 to 63
- block_mask: int32 [2, 16, 5, 1], P('dp', 'seq'), may hold values 0 or 1
- bias_table: bfloat16 [16, 64, 64], replicated, may hold values from -4 to 4
Outputs:
- attention_out: bfloat16 [2, 2048, 1024], P('dp', 'seq')
- d_queries: bfloat16 [2, 2048, 1024], P('dp', 'seq')
- d_keys: bfloat16 [2, 2048, 1024], P('dp', 'seq')
- d_values: bfloat16 [2, 2048, 1024], P('dp', 'seq')
- d_table: float32 [16, 64, 64], replicated
Inputs may be any that keep to these rules, and one draw needn't show every extreme that they name: `segment_ids`: each document is a run of consecutive tokens of one sequence.
All inputs are finite; a program needn't handle non-finite values. No bound on the sum of `block_mask` on one device may be relied on, other than what follows from the above.
Results may differ from a plain program's by a relative error of at most 0.024.
Values may be sent and summed in bfloat16 or wider, within the bound.
No kernel may reach another device: no remote copies, remote signals or barrier semaphores. Data moves between devices by JAX's collectives and lax.ppermute only.
A program may use at most 64 MiB of HBM per device.

v0:
```python
import jax
import jax.numpy as jnp
from jax import lax
from jax.sharding import PartitionSpec as P

H = 16
DH = 64
NB = 64
BLK = 128


masked_value = -1e30


def from_partner(value, axis, apart):
    mask = 2**apart
    pairs = [(source, source ^ mask) for source in range(lax.axis_size(axis))]
    return lax.ppermute(value, axis, pairs)


def expand_blocks(bias_block, row_count, col_count):
    leading = bias_block.shape[:-2]
    row_blocks = bias_block.shape[-2]
    col_blocks = bias_block.shape[-1]
    widened = jnp.broadcast_to(
        bias_block[..., :, None, :, None],
        leading + (row_blocks, row_count // row_blocks, col_blocks, col_count // col_blocks),
    )
    return widened.reshape(leading + (row_count, col_count))


def one_hot_rows(buckets):
    levels_all = jnp.arange(NB, dtype=jnp.float32)
    return (buckets.astype(jnp.float32)[:, None] == levels_all[None, :]).astype(jnp.bfloat16)


def bias_tile(bias_table, row_hot, col_hot):
    picked = jnp.einsum(
        "bn,hnm->hbm", row_hot, bias_table, preferred_element_type=jnp.float32
    ).astype(jnp.bfloat16)
    return jnp.einsum("hbm,cm->hbc", picked, col_hot, preferred_element_type=jnp.float32)


def allowed_pairs(seg_rows, seg_cols, block_ok):
    same_doc = seg_rows.astype(jnp.float32)[:, None] == seg_cols.astype(jnp.float32)[None, :]
    return same_doc & expand_blocks(block_ok, seg_rows.shape[0], seg_cols.shape[0])


def masked_scores(query_heads, key_heads, bias_block, allowed):
    products = jnp.einsum(
        "thd,uhd->htu", query_heads, key_heads, preferred_element_type=jnp.float32
    )
    shifted = products * 0.125 + expand_blocks(bias_block, query_heads.shape[0], key_heads.shape[0])
    return jnp.where(allowed[None], shifted, masked_value)


def grad_terms(scores, allowed, lse, row_delta, grad_heads, value_heads):
    probs = jnp.where(allowed[None], jnp.exp(scores - lse[:, :, None]), 0.0)
    dprob = jnp.einsum("thd,uhd->htu", grad_heads, value_heads, preferred_element_type=jnp.float32)
    dscore = probs * (dprob - row_delta[:, :, None])
    return (probs.astype(jnp.bfloat16), dscore)


def local(queries, keys, values, d_out, segment_ids, block_bucket, block_mask, bias_table):
    row_count = queries.shape[1]
    block_count = row_count // BLK
    level_count = lax.axis_size("seq").bit_length() - 1
    query_heads = queries[0].reshape(row_count, H, DH)
    grad_heads = d_out[0].reshape(row_count, H, DH)
    own_keys = keys[0]
    own_values = values[0]
    own_seg = segment_ids[0]
    own_bucket = block_bucket[0]
    own_mask = block_mask[0] != 0
    own_hot = one_hot_rows(own_bucket)
    own_hot_wide = own_hot.astype(jnp.float32)
    section_list = list(range(level_count + 1))
    stored = {}
    run_max = jnp.full((H, row_count), masked_value, jnp.float32)
    run_sum = jnp.zeros((H, row_count), jnp.float32)
    run_acc = jnp.zeros((row_count, H, DH), jnp.float32)
    for section_num in section_list:
        if section_num == 0:
            key_rows, value_rows, seg_cols, bucket_cols = (
                own_keys,
                own_values,
                own_seg,
                own_bucket,
            )
            block_ok = own_mask[:, 0, :] | jnp.eye(block_count, dtype=bool)
        else:
            key_rows, value_rows, seg_cols, bucket_cols = from_partner(
                (
                    own_keys,
                    own_values,
                    own_seg.astype(jnp.bfloat16),
                    own_bucket.astype(jnp.bfloat16),
                ),
                "seq",
                section_num - 1,
            )
            block_ok = own_mask[:, section_num, :]
        key_heads = key_rows.reshape(row_count, H, DH)
        value_heads = value_rows.reshape(row_count, H, DH)
        col_hot = one_hot_rows(bucket_cols)
        bias_block = bias_tile(bias_table, own_hot, col_hot)
        allowed = allowed_pairs(own_seg, seg_cols, block_ok)
        stored[section_num] = (key_heads, value_heads, seg_cols, col_hot, bias_block, allowed)
        scores = masked_scores(query_heads, key_heads, bias_block, allowed)
        fresh_max = jnp.maximum(run_max, jnp.max(scores, axis=-1))
        rescale = jnp.exp(run_max - fresh_max)
        weights = jnp.where(allowed[None], jnp.exp(scores - fresh_max[:, :, None]), 0.0)
        run_sum = run_sum * rescale + jnp.sum(weights, axis=-1)
        run_acc = run_acc * rescale.T[:, :, None] + jnp.einsum(
            "htu,uhd->thd",
            weights.astype(jnp.bfloat16),
            value_heads,
            preferred_element_type=jnp.float32,
        )
        run_max = fresh_max
    out_heads = (run_acc / run_sum.T[:, :, None]).astype(jnp.bfloat16)
    lse = run_max + jnp.log(run_sum)
    row_delta = jnp.sum(out_heads.astype(jnp.float32) * grad_heads.astype(jnp.float32), axis=-1).T
    out_rows = out_heads.reshape(row_count, H * DH)
    query_acc = jnp.zeros((row_count, H, DH), jnp.float32)
    key_acc = jnp.zeros((row_count, H, DH), jnp.float32)
    value_acc = jnp.zeros((row_count, H, DH), jnp.float32)
    table_acc = jnp.zeros((H, NB, NB), jnp.float32)
    for section_num in section_list:
        key_heads, value_heads, seg_cols, col_hot, bias_block, allowed = stored[section_num]
        scores = masked_scores(query_heads, key_heads, bias_block, allowed)
        probs_low, dscore = grad_terms(scores, allowed, lse, row_delta, grad_heads, value_heads)
        dscore_low = dscore.astype(jnp.bfloat16)
        query_acc = (
            query_acc
            + jnp.einsum("htu,uhd->thd", dscore_low, key_heads, preferred_element_type=jnp.float32)
            * 0.125
        )
        block_sums = dscore.reshape(H, block_count, BLK, block_count, BLK).sum(axis=(2, 4))
        table_acc = table_acc + jnp.einsum(
            "bn,hbc,cm->hnm",
            own_hot_wide,
            block_sums,
            col_hot.astype(jnp.float32),
            precision=lax.Precision.HIGHEST,
        )
        if section_num == 0:
            key_acc = (
                jnp.einsum(
                    "htu,thd->uhd", dscore_low, query_heads, preferred_element_type=jnp.float32
                )
                * 0.125
            )
            value_acc = jnp.einsum(
                "htu,thd->uhd", probs_low, grad_heads, preferred_element_type=jnp.float32
            )
        else:
            key_term = (
                jnp.einsum(
                    "htu,thd->uhd", dscore_low, query_heads, preferred_element_type=jnp.float32
                )
                * 0.125
            ).astype(jnp.bfloat16)
            value_term = jnp.einsum(
                "htu,thd->uhd", probs_low, grad_heads, preferred_element_type=jnp.float32
            ).astype(jnp.bfloat16)
            back_keys, back_values = from_partner(
                (key_term.reshape(row_count, H * DH), value_term.reshape(row_count, H * DH)),
                "seq",
                section_num - 1,
            )
            key_acc = key_acc + back_keys.reshape(row_count, H, DH).astype(jnp.float32)
            value_acc = value_acc + back_values.reshape(row_count, H, DH).astype(jnp.float32)
    table_total = lax.psum(table_acc, ("seq", "dp"))
    feature_count = H * DH
    return (
        out_rows.reshape(1, row_count, feature_count),
        query_acc.astype(jnp.bfloat16).reshape(1, row_count, feature_count),
        key_acc.astype(jnp.bfloat16).reshape(1, row_count, feature_count),
        value_acc.astype(jnp.bfloat16).reshape(1, row_count, feature_count),
        table_total,
    )


def solution(mesh):
    in_specs = (
        P("dp", "seq", None),
        P("dp", "seq", None),
        P("dp", "seq", None),
        P("dp", "seq", None),
        P("dp", "seq"),
        P("dp", "seq"),
        P("dp", "seq", None, None),
        P(),
    )
    out_specs = (
        P("dp", "seq", None),
        P("dp", "seq", None),
        P("dp", "seq", None),
        P("dp", "seq", None),
        P(),
    )
    return jax.shard_map(local, mesh=mesh, in_specs=in_specs, out_specs=out_specs, check_vma=False)
```

profile of v0, /device:TPU:0, one launch (start us, length us, event | category | flops | bytes accessed | tf_op | source)
XLA Modules:
  0.0 256.8 jit_solution(7733567742736410515)
XLA Ops:
  8.0 3.0 %collective-permute-start.4 = (bf16[128]{0:T(256)(128)(2,1)S(1)}, bf16[128]{0:T(256)(128)(2,1)S(1)}, u32[]{:S(2)}, u32[]{:S(2)}) collective-permute-start(bf16[128]{0:T(256)(128)(2,1)S(1)} %get-tuple-element.40), channel_id=1, source_target_pairs={{0,4},{2,6},{4,0},{6,2},{8,12},{10,14},{12,8},{14,10},{16,20},{18,... | collective-permute-start | bytes 776 | tf_op jit(solution)/shard_map/ppermute | solution.py:18
  10.9 1.6 collective-permute-start.8
  12.5 2.6 %collective-permute-start.12 = (bf16[128]{0:T(256)(128)(2,1)S(1)}, bf16[128]{0:T(256)(128)(2,1)S(1)}, u32[]{:S(2)}, u32[]{:S(2)}) collective-permute-start(bf16[128]{0:T(256)(128)(2,1)S(1)} %get-tuple-element.40), channel_id=1, source_target_pairs={{0,16},{2,18},{4,20},{6,22},{8,24},{10,26},{12,28},{14,30},{16,0},... | collective-permute-start | bytes 776 | tf_op jit(solution)/shard_map/ppermute | solution.py:18
  15.8 1.7 collective-permute-start.14
  23.2 1.8 collective-permute-start.10
  26.7 1.8 collective-permute-start.6
  31.8 2.6 %collective-permute-start.13 = (bf16[128,1024]{1,0:T(8,128)(2,1)}, bf16[128,1024]{1,0:T(8,128)(2,1)S(1)}, u32[]{:S(2)}, u32[]{:S(2)}) collective-permute-start(bf16[128,1024]{1,0:T(8,128)(2,1)} %bitcast.15), channel_id=1, source_target_pairs={{0,16},{2,18},{4,20},{6,22},{8,24},{10,26},{12,28},{14,30},{16,0},... | collective-permute-start | bytes 786440 | tf_op jit(solution)/shard_map/ppermute | solution.py:18
  38.0 2.6 %broadcast_compare_fusion = (pred[128,128]{0,1:T(8,128)(4,1)S(1)}, pred[128,128]{0,1:T(8,128)(4,1)S(1)}, pred[128,128]{0,1:T(8,128)(4,1)S(1)}, pred[128,128]{0,1:T(8,128)(4,1)S(1)}, pred[128,128]{0,1:T(8,128)(4,1)S(1)}) fusion(f32[128]{0:T(128)S(1)} %get-tuple-element.41, pred[]{:T(512)} %bitcast.25, f32[128]{0:T(128)S(1)} %convert_element_type.245, ...), kind=kLoop, calls=%fused_computation.151 | loop fusion | flops 147456 | bytes 84484 | tf_op jit(solution)/shard_map/eq | solution.py:45
  41.1 6.8 %collective-permute-done.13 = bf16[128,1024]{1,0:T(8,128)(2,1)S(1)} collective-permute-done((bf16[128,1024]{1,0:T(8,128)(2,1)}, bf16[128,1024]{1,0:T(8,128)(2,1)S(1)}, u32[]{:S(2)}, u32[]{:S(2)}) %collective-permute-start.13) | collective-permute-done | bytes 262176 | tf_op jit(solution)/shard_map/ppermute | solution.py:18
  51.4 1.8 copy.75
  53.2 2.3 fusion.151
  55.5 1.8 copy.72
  57.3 2.3 fusion.152
  59.6 1.8 copy.69
  61.4 1.5 fusion.153
  66.0 1.8 copy.79
  67.8 2.0 convolution_bitcast_fusion
  69.9 1.8 copy.76
  71.7 2.4 convolution_bitcast_fusion.1
  74.1 1.8 copy.73
  75.8 2.4 convolution_bitcast_fusion.2
  78.3 1.8 copy.70
  80.8 3.1 %multiply_reduce_fusion = (f32[128,16]{0,1:T(8,128)S(1)}, bf16[128,16,64]{0,2,1:T(8,128)(2,1)}) fusion(bf16[128,16,64]{0,2,1:T(8,128)(2,1)S(1)} %bitcast.299, f32[128,16]{0,1:T(8,128)S(1)} %copy-done.24, f32[128,16,64]{0,2,1:T(8,128)} %convolution_bitcast_fusion, f32[128,16]{0,1:T(8,128)S(1)} %copy-done.27, f32[128,16,64]{0,2,1:T(8,128)} %convolution_bitcast_fusion.1, ...), kind=kOutput, calls=%fused_computation.103 | convolution fusion | flops 36042752 | bytes 3997696 | tf_op jit(solution)/shard_map/htu,uhd->thd/dot_general | solution.py:114
  99.8 1.9 copy.102
  106.1 1.9 copy.103
  108.0 2.9 %collective-permute-start.19 = (bf16[128,1024]{0,1:T(8,128)(2,1)}, bf16[128,1024]{0,1:T(8,128)(2,1)}, u32[]{:S(2)}, u32[]{:S(2)}) collective-permute-start(bf16[128,1024]{0,1:T(8,128)(2,1)} %bitcast.353), channel_id=1, source_target_pairs={{0,16},{2,18},{4,20},{6,22},{8,24},{10,26},{12,28},{14,30},{16,0},... | collective-permute-start | bytes 786440 | tf_op jit(solution)/shard_map/ppermute | solution.py:18
  111.7 2.0 collective-permute-start.23
  113.8 1.5 multiply_add_fusion
  115.9 8.2 %collective-permute-done.19 = bf16[128,1024]{0,1:T(8,128)(2,1)} collective-permute-done((bf16[128,1024]{0,1:T(8,128)(2,1)}, bf16[128,1024]{0,1:T(8,128)(2,1)}, u32[]{:S(2)}, u32[]{:S(2)}) %collective-permute-start.19) | collective-permute-done | bytes 262176 | tf_op jit(solution)/shard_map/ppermute | solution.py:18
  127.2 9.0 %collective-permute-done.23 = bf16[128,1024]{0,1:T(8,128)(2,1)S(1)} collective-permute-done((bf16[128,1024]{0,1:T(8,128)(2,1)}, bf16[128,1024]{0,1:T(8,128)(2,1)S(1)}, u32[]{:S(2)}, u32[]{:S(2)}) %collective-permute-start.23) | collective-permute-done | bytes 262176 | tf_op jit(solution)/shard_map/ppermute | solution.py:18
  139.2 108.9 %all-reduce.2.cloned.1.call-done = f32[16,64,64]{2,1,0:T(8,128)} async-done(((f32[16,64,64]{2,1,0:T(8,128)}), f32[16,64,64]{2,1,0:T(8,128)}) %all-reduce.2.cloned.1.call-update) | async-done | bytes 262160 | tf_op jit(solution)/shard_map/psum | solution.py:174
  248.1 1.9 copy.134
  (162 shorter events, 48.1 us)
Async XLA Ops:
  7.2 12.0 %copy-start = (bf16[16,64,64]{2,1,0:T(8,128)(2,1)S(1)}, bf16[16,64,64]{2,1,0:T(8,128)(2,1)}, u32[]{:S(2)}) copy-start(bf16[16,64,64]{2,1,0:T(8,128)(2,1)} %param.15) | copy-start | bytes 393220
  7.2 240.9 %all-reduce.2.cloned.1.call-start = ((), (), s32[]{:S(2)}) async-start(), calls=%async_computation | async-start | bytes 1048576 | tf_op jit(solution)/shard_map/psum | solution.py:174
  8.0 27.9 %collective-permute-start.4 = (bf16[128]{0:T(256)(128)(2,1)S(1)}, bf16[128]{0:T(256)(128)(2,1)S(1)}, u32[]{:S(2)}, u32[]{:S(2)}) collective-permute-start(bf16[128]{0:T(256)(128)(2,1)S(1)} %get-tuple-element.40), channel_id=1, source_target_pairs={{0,4},{2,6},{4,0},{6,2},{8,12},{10,14},{12,8},{14,10},{16,20},{18,... | collective-permute-start | bytes 776 | tf_op jit(solution)/shard_map/ppermute | solution.py:18
  10.9 25.5 %collective-permute-start.8 = (bf16[128]{0:T(256)(128)(2,1)S(1)}, bf16[128]{0:T(256)(128)(2,1)S(1)}, u32[]{:S(2)}, u32[]{:S(2)}) collective-permute-start(bf16[128]{0:T(256)(128)(2,1)S(1)} %get-tuple-element.40), channel_id=1, source_target_pairs={{0,8},{2,10},{4,12},{6,14},{8,0},{10,2},{12,4},{14,6},{16,24},{18,... | collective-permute-start | bytes 776 | tf_op jit(solution)/shard_map/ppermute | solution.py:18
  12.5 25.1 %collective-permute-start.12 = (bf16[128]{0:T(256)(128)(2,1)S(1)}, bf16[128]{0:T(256)(128)(2,1)S(1)}, u32[]{:S(2)}, u32[]{:S(2)}) collective-permute-start(bf16[128]{0:T(256)(128)(2,1)S(1)} %get-tuple-element.40), channel_id=1, source_target_pairs={{0,16},{2,18},{4,20},{6,22},{8,24},{10,26},{12,28},{14,30},{16,0},... | collective-permute-start | bytes 776 | tf_op jit(solution)/shard_map/ppermute | solution.py:18
  15.1 22.5 %collective-permute-start = (bf16[128]{0:T(256)(128)(2,1)S(1)}, bf16[128]{0:T(256)(128)(2,1)S(1)}, u32[]{:S(2)}, u32[]{:S(2)}) collective-permute-start(bf16[128]{0:T(256)(128)(2,1)S(1)} %get-tuple-element.40), channel_id=1, source_target_pairs={{0,2},{2,0},{4,6},{6,4},{8,10},{10,8},{12,14},{14,12},{16,18},{18,... | collective-permute-start | bytes 776 | tf_op jit(solution)/shard_map/ppermute | solution.py:18
  15.8 7.4 %collective-permute-start.14 = (bf16[1]{0:T(256)(128)(2,1)}, bf16[1]{0:T(256)(128)(2,1)}, u32[]{:S(2)}, u32[]{:S(2)}) collective-permute-start(bf16[1]{0:T(256)(128)(2,1)} %bitcast.17), channel_id=1, source_target_pairs={{0,16},{2,18},{4,20},{6,22},{8,24},{10,26},{12,28},{14,30},{16,0},... | collective-permute-start | bytes 14 | tf_op jit(solution)/shard_map/ppermute | solution.py:18
  23.2 3.6 %collective-permute-start.10 = (bf16[1]{0:T(256)(128)(2,1)}, bf16[1]{0:T(256)(128)(2,1)}, u32[]{:S(2)}, u32[]{:S(2)}) collective-permute-start(bf16[1]{0:T(256)(128)(2,1)} %bitcast.17), channel_id=1, source_target_pairs={{0,8},{2,10},{4,12},{6,14},{8,0},{10,2},{12,4},{14,6},{16,24},{18,... | collective-permute-start | bytes 14 | tf_op jit(solution)/shard_map/ppermute | solution.py:18
  26.7 3.5 %collective-permute-start.6 = (bf16[1]{0:T(256)(128)(2,1)}, bf16[1]{0:T(256)(128)(2,1)}, u32[]{:S(2)}, u32[]{:S(2)}) collective-permute-start(bf16[1]{0:T(256)(128)(2,1)} %bitcast.17), channel_id=1, source_target_pairs={{0,4},{2,6},{4,0},{6,2},{8,12},{10,14},{12,8},{14,10},{16,20},{18,... | collective-permute-start | bytes 14 | tf_op jit(solution)/shard_map/ppermute | solution.py:18
  30.2 1.6 collective-permute-start.2
  31.8 16.0 %collective-permute-start.13 = (bf16[128,1024]{1,0:T(8,128)(2,1)}, bf16[128,1024]{1,0:T(8,128)(2,1)S(1)}, u32[]{:S(2)}, u32[]{:S(2)}) collective-permute-start(bf16[128,1024]{1,0:T(8,128)(2,1)} %bitcast.15), channel_id=1, source_target_pairs={{0,16},{2,18},{4,20},{6,22},{8,24},{10,26},{12,28},{14,30},{16,0},... | collective-permute-start | bytes 786440 | tf_op jit(solution)/shard_map/ppermute | solution.py:18
  35.8 14.4 %collective-permute-start.9 = (bf16[128,1024]{1,0:T(8,128)(2,1)}, bf16[128,1024]{1,0:T(8,128)(2,1)}, u32[]{:S(2)}, u32[]{:S(2)}) collective-permute-start(bf16[128,1024]{1,0:T(8,128)(2,1)} %bitcast.15), channel_id=1, source_target_pairs={{0,8},{2,10},{4,12},{6,14},{8,0},{10,2},{12,4},{14,6},{16,24},{18,... | collective-permute-start | bytes 786440 | tf_op jit(solution)/shard_map/ppermute | solution.py:18
  36.4 19.1 %collective-permute-start.5 = (bf16[128,1024]{1,0:T(8,128)(2,1)}, bf16[128,1024]{1,0:T(8,128)(2,1)}, u32[]{:S(2)}, u32[]{:S(2)}) collective-permute-start(bf16[128,1024]{1,0:T(8,128)(2,1)} %bitcast.15), channel_id=1, source_target_pairs={{0,4},{2,6},{4,0},{6,2},{8,12},{10,14},{12,8},{14,10},{16,20},{18,... | collective-permute-start | bytes 786440 | tf_op jit(solution)/shard_map/ppermute | solution.py:18
  37.6 22.0 %collective-permute-start.1 = (bf16[128,1024]{1,0:T(8,128)(2,1)}, bf16[128,1024]{1,0:T(8,128)(2,1)}, u32[]{:S(2)}, u32[]{:S(2)}) collective-permute-start(bf16[128,1024]{1,0:T(8,128)(2,1)} %bitcast.15), channel_id=1, source_target_pairs={{0,2},{2,0},{4,6},{6,4},{8,10},{10,8},{12,14},{14,12},{16,18},{18,... | collective-permute-start | bytes 786440 | tf_op jit(solution)/shard_map/ppermute | solution.py:18
  37.6 28.4 %collective-permute-start.15 = (bf16[128,1024]{1,0:T(8,128)(2,1)}, bf16[128,1024]{1,0:T(8,128)(2,1)}, u32[]{:S(2)}, u32[]{:S(2)}) collective-permute-start(bf16[128,1024]{1,0:T(8,128)(2,1)} %bitcast.22), channel_id=1, source_target_pairs={{0,16},{2,18},{4,20},{6,22},{8,24},{10,26},{12,28},{14,30},{16,0},... | collective-permute-start | bytes 786440 | tf_op jit(solution)/shard_map/ppermute | solution.py:18
  47.8 22.0 %collective-permute-start.11 = (bf16[128,1024]{1,0:T(8,128)(2,1)}, bf16[128,1024]{1,0:T(8,128)(2,1)}, u32[]{:S(2)}, u32[]{:S(2)}) collective-permute-start(bf16[128,1024]{1,0:T(8,128)(2,1)} %bitcast.22), channel_id=1, source_target_pairs={{0,8},{2,10},{4,12},{6,14},{8,0},{10,2},{12,4},{14,6},{16,24},{18,... | collective-permute-start | bytes 786440 | tf_op jit(solution)/shard_map/ppermute | solution.py:18
  50.2 23.9 %collective-permute-start.7 = (bf16[128,1024]{1,0:T(8,128)(2,1)}, bf16[128,1024]{1,0:T(8,128)(2,1)}, u32[]{:S(2)}, u32[]{:S(2)}) collective-permute-start(bf16[128,1024]{1,0:T(8,128)(2,1)} %bitcast.22), channel_id=1, source_target_pairs={{0,4},{2,6},{4,0},{6,2},{8,12},{10,14},{12,8},{14,10},{16,20},{18,... | collective-permute-start | bytes 786440 | tf_op jit(solution)/shard_map/ppermute | solution.py:18
  55.5 22.8 %collective-permute-start.3 = (bf16[128,1024]{1,0:T(8,128)(2,1)}, bf16[128,1024]{1,0:T(8,128)(2,1)}, u32[]{:S(2)}, u32[]{:S(2)}) collective-permute-start(bf16[128,1024]{1,0:T(8,128)(2,1)} %bitcast.22), channel_id=1, source_target_pairs={{0,2},{2,0},{4,6},{6,4},{8,10},{10,8},{12,14},{14,12},{16,18},{18,... | collective-permute-start | bytes 786440 | tf_op jit(solution)/shard_map/ppermute | solution.py:18
  105.1 8.7 %copy-start.30 = (f32[64]{0:T(128)S(1)}, f32[64]{0:T(128)}, u32[]{:S(2)}) copy-start(f32[64]{0:T(128)} %get-tuple-element.69) | copy-start | bytes 772
  105.1 8.7 %copy-start.31 = (f32[64]{0:T(128)S(1)}, f32[64]{0:T(128)}, u32[]{:S(2)}) copy-start(f32[64]{0:T(128)} %get-tuple-element.70) | copy-start | bytes 772
  105.1 8.7 %copy-start.32 = (f32[64]{0:T(128)S(1)}, f32[64]{0:T(128)}, u32[]{:S(2)}) copy-start(f32[64]{0:T(128)} %get-tuple-element.71) | copy-start | bytes 772
  106.1 9.3 %copy-start.7 = (f32[16,128,128]{1,2,0:T(8,128)S(1)}, f32[16,128,128]{1,2,0:T(8,128)}, u32[]{:S(2)}) copy-start(f32[16,128,128]{1,2,0:T(8,128)} %copy-done.5) | copy-start | bytes 3145732
  108.0 16.1 %collective-permute-start.19 = (bf16[128,1024]{0,1:T(8,128)(2,1)}, bf16[128,1024]{0,1:T(8,128)(2,1)}, u32[]{:S(2)}, u32[]{:S(2)}) collective-permute-start(bf16[128,1024]{0,1:T(8,128)(2,1)} %bitcast.353), channel_id=1, source_target_pairs={{0,16},{2,18},{4,20},{6,22},{8,24},{10,26},{12,28},{14,30},{16,0},... | collective-permute-start | bytes 786440 | tf_op jit(solution)/shard_map/ppermute | solution.py:18
  110.9 13.7 %collective-permute-start.18 = (bf16[128,1024]{0,1:T(8,128)(2,1)}, bf16[128,1024]{0,1:T(8,128)(2,1)}, u32[]{:S(2)}, u32[]{:S(2)}) collective-permute-start(bf16[128,1024]{0,1:T(8,128)(2,1)} %bitcast.352), channel_id=1, source_target_pairs={{0,8},{2,10},{4,12},{6,14},{8,0},{10,2},{12,4},{14,6},{16,24},{18,... | collective-permute-start | bytes 786440 | tf_op jit(solution)/shard_map/ppermute | solution.py:18
  110.9 15.0 %collective-permute-start.17 = (bf16[128,1024]{0,1:T(8,128)(2,1)}, bf16[128,1024]{0,1:T(8,128)(2,1)}, u32[]{:S(2)}, u32[]{:S(2)}) collective-permute-start(bf16[128,1024]{0,1:T(8,128)(2,1)} %bitcast.355), channel_id=1, source_target_pairs={{0,4},{2,6},{4,0},{6,2},{8,12},{10,14},{12,8},{14,10},{16,20},{18,... | collective-permute-start | bytes 786440 | tf_op jit(solution)/shard_map/ppermute | solution.py:18
  111.7 14.1 %collective-permute-start.16 = (bf16[128,1024]{0,1:T(8,128)(2,1)}, bf16[128,1024]{0,1:T(8,128)(2,1)}, u32[]{:S(2)}, u32[]{:S(2)}) collective-permute-start(bf16[128,1024]{0,1:T(8,128)(2,1)} %bitcast.354), channel_id=1, source_target_pairs={{0,2},{2,0},{4,6},{6,4},{8,10},{10,8},{12,14},{14,12},{16,18},{18,... | collective-permute-start | bytes 786440 | tf_op jit(solution)/shard_map/ppermute | solution.py:18
  111.7 24.5 %collective-permute-start.23 = (bf16[128,1024]{0,1:T(8,128)(2,1)}, bf16[128,1024]{0,1:T(8,128)(2,1)S(1)}, u32[]{:S(2)}, u32[]{:S(2)}) collective-permute-start(bf16[128,1024]{0,1:T(8,128)(2,1)} %bitcast.343), channel_id=1, source_target_pairs={{0,16},{2,18},{4,20},{6,22},{8,24},{10,26},{12,28},{14,30},{16,0},... | collective-permute-start | bytes 786440 | tf_op jit(solution)/shard_map/ppermute | solution.py:18
  115.4 8.7 %copy-start.21 = (bf16[16,128,64]{1,2,0:T(8,128)(2,1)S(1)}, bf16[16,128,64]{1,2,0:T(8,128)(2,1)}, u32[]{:S(2)}) copy-start(bf16[16,128,64]{1,2,0:T(8,128)(2,1)} %convolution_convert_fusion.1) | copy-start | bytes 786436
  115.4 9.2 %copy-start.20 = (bf16[16,128,64]{1,2,0:T(8,128)(2,1)S(1)}, bf16[16,128,64]{1,2,0:T(8,128)(2,1)}, u32[]{:S(2)}) copy-start(bf16[16,128,64]{1,2,0:T(8,128)(2,1)} %convolution_convert_fusion.2) | copy-start | bytes 786436
  124.1 13.2 %collective-permute-start.22 = (bf16[128,1024]{0,1:T(8,128)(2,1)S(1)}, bf16[128,1024]{0,1:T(8,128)(2,1)S(1)}, u32[]{:S(2)}, u32[]{:S(2)}) collective-permute-start(bf16[128,1024]{0,1:T(8,128)(2,1)S(1)} %bitcast.342), channel_id=1, source_target_pairs={{0,8},{2,10},{4,12},{6,14},{8,0},{10,2},{12,4},{14,6},{16,24},{18,... | collective-permute-start | bytes 786440 | tf_op jit(solution)/shard_map/ppermute | solution.py:18
  124.6 12.7 %collective-permute-start.21 = (bf16[128,1024]{0,1:T(8,128)(2,1)S(1)}, bf16[128,1024]{0,1:T(8,128)(2,1)S(1)}, u32[]{:S(2)}, u32[]{:S(2)}) collective-permute-start(bf16[128,1024]{0,1:T(8,128)(2,1)S(1)} %bitcast.341), channel_id=1, source_target_pairs={{0,4},{2,6},{4,0},{6,2},{8,12},{10,14},{12,8},{14,10},{16,20},{18,... | collective-permute-start | bytes 786440 | tf_op jit(solution)/shard_map/ppermute | solution.py:18
  125.8 11.5 %collective-permute-start.20 = (bf16[128,1024]{0,1:T(8,128)(2,1)S(1)}, bf16[128,1024]{0,1:T(8,128)(2,1)S(1)}, u32[]{:S(2)}, u32[]{:S(2)}) collective-permute-start(bf16[128,1024]{0,1:T(8,128)(2,1)S(1)} %bitcast.345), channel_id=1, source_target_pairs={{0,2},{2,0},{4,6},{6,4},{8,10},{10,8},{12,14},{14,12},{16,18},{18,... | collective-permute-start | bytes 786440 | tf_op jit(solution)/shard_map/ppermute | solution.py:18
  (27 other events, 52.6 us)
Sparse Core Ops, SparseCore 0:
  115.5 132.5 all-reduce.1
where the time goes:
time: 258 us; the launch traced here: 257 us
  waiting for transfers between devices  136 us (53%)
  matrix products  38.1 us (15%)
  local copies, waits for them, and re-layouts  28.9 us (11%)
  starting transfers between devices  26.2 us (10%)
  between operations  17.7 us (7%)
  other arithmetic  9.98 us (4%)
    psum x1, waiting for transfers between devices, local(): table_total = lax.psum(table_acc, ('seq', 'dp'))  109 us
    ppermute x24, waiting for transfers between devices, from_partner(): return lax.ppermute(value, axis, pairs)  27.1 us
    ppermute x24, starting transfers between devices, from_partner(): return lax.ppermute(value, axis, pairs)  26.2 us
    unnamed x77, local copies, waits for them, and re-layouts  14.8 us
    ppermute x8, local copies, waits for them, and re-layouts, from_partner(): return lax.ppermute(value, axis, pairs)  13.4 us
    dot_general x5, matrix products, local(): jnp.einsum('htu,uhd->thd', weights.astype(jnp.bfloat16), value_heads, pre...  11 us
    dot_general x5, matrix products, masked_scores(): jnp.einsum('thd,uhd->htu', query_heads, key_heads, preferred_element_type...  7.82 us
  transfers between devices with their start and end apart: 25, of which 9 were waited for; matrix products, arithmetic and copies ran while one was open for 17% of the time, Pallas kernels for 0%

commit v1 on v0

v1 whole, which is shorter than its diff:
```python
import functools

import jax
import jax.numpy as jnp
from jax import lax
from jax.experimental import pallas as pl
from jax.experimental.pallas import tpu as pltpu
from jax.sharding import PartitionSpec as P

H = 16
DH = 64
NB = 64
BLK = 128
HALVES = 2
INFO = 8
LANES = 128
PAIR_LANES = 2 * DH
BUCKET_LANE = 112
MASKED = -1e30

F32 = jnp.float32
BF16 = jnp.bfloat16


def contract(a, b, dim_a, dim_b):
    return lax.dot_general(a, b, (((dim_a,), (dim_b,)), ((), ())), preferred_element_type=F32)


def from_partner(value, axis, mask):
    pairs = [(source, source ^ mask) for source in range(lax.axis_size(axis))]
    return lax.ppermute(value, axis, pairs)


def lane_iota(shape):
    return lax.broadcasted_iota(jnp.int32, shape, len(shape) - 1)


def row_iota(shape):
    return lax.broadcasted_iota(jnp.int32, shape, len(shape) - 2)


def split_pair(pair, low):
    zero = jnp.zeros_like(pair)
    return jnp.concatenate([jnp.where(low, pair, zero), jnp.where(low, zero, pair)], axis=0)


def attention_body(section_count, half, first, *refs):
    level_count = section_count - 1
    refs = list(refs)

    def take(count):
        taken, refs[:] = refs[:count], refs[count:]
        return taken

    mask_ref, bucket_ref, seg_ref, table_ref = take(4)
    q_ref, do_ref, k_ref, v_ref = take(4)
    partner_refs = take(level_count)
    info_refs = partner_refs if first else take(level_count)
    if not first:
        pay_in_ref, _, _ = take(3)
    out_ref, dq_ref, own_ref, pay_ref = take(4)
    term_refs = take(level_count)
    masks, biases = take(2)
    pair = pl.program_id(0)
    half_heads = biases.shape[1]

    @pl.when(pair == 0)
    def _():
        seg_rows = seg_ref[...].astype(F32)
        own_bucket = bucket_ref[0]
        in_row = row_iota((half_heads, NB, LANES)) == own_bucket
        pay = jnp.zeros((1, LANES), F32) if first else pay_in_ref[...]
        for s in range(section_count):
            if s == 0:
                seg_cols = seg_rows
                bucket = jnp.full((1, LANES), own_bucket, jnp.int32).astype(F32)
            else:
                info = info_refs[s - 1][2 * BLK : 2 * BLK + INFO, :].astype(F32)
                seg_cols = info[0:1]
                bucket = info[1:2]
            cols = jnp.broadcast_to(seg_cols, (BLK, BLK)).T
            same = cols == seg_rows
            open_block = MASKED if s == 0 else jnp.where(mask_ref[s] != 0, 0.0, MASKED)
            masks[s * BLK : (s + 1) * BLK, :] = jnp.where(
                same, jnp.full((BLK, BLK), 0.0 if s == 0 else open_block, F32), MASKED
            )
            hot = (row_iota((NB, LANES)).astype(F32) == bucket).astype(BF16)
            picked = contract(table_ref[...], hot, 1, 0).reshape(half_heads, NB, LANES)
            biases[s] = jnp.sum(jnp.where(in_row, picked, 0.0), axis=1)
            if first:
                pay = jnp.where(lane_iota(pay.shape) == BUCKET_LANE + s, bucket, pay)
        pay_ref[...] = pay

    low = lane_iota((BLK, PAIR_LANES)) < DH
    q_stack = split_pair(q_ref[...] * jnp.asarray(0.125, BF16), low)
    key_list = [k_ref[...]] + [r[0:BLK, :] for r in partner_refs]
    value_list = [v_ref[...]] + [r[BLK : 2 * BLK, :] for r in partner_refs]
    shifts = []
    scores = []
    top = None
    for s in range(section_count):
        mask = masks[s * BLK : (s + 1) * BLK, :]
        score = contract(key_list[s], q_stack, 1, 1) + jnp.concatenate([mask, mask], axis=1)
        bias = jnp.concatenate(
            [biases[s, pl.ds(2 * pair, 1), :], biases[s, pl.ds(2 * pair + 1, 1), :]], axis=1
        )
        best = jnp.max(score, axis=0, keepdims=True) + bias
        top = best if top is None else jnp.maximum(top, best)
        scores.append(score)
        shifts.append(bias)
    weights = []
    weights_low = []
    total = None
    out_stack = None
    for s in range(section_count):
        weight = jnp.exp(scores[s] - (top - shifts[s]))
        weight_low = weight.astype(BF16)
        part = jnp.sum(weight, axis=0, keepdims=True)
        total = part if total is None else total + part
        term = contract(weight_low, value_list[s], 0, 0)
        out_stack = term if out_stack is None else out_stack + term
        weights.append(weight)
        weights_low.append(weight_low)
    inverse = 1.0 / total
    inverse_cols = jnp.broadcast_to(inverse, (BLK, 2 * BLK)).T
    scaled = out_stack * inverse_cols
    out_low = jnp.where(low, scaled[:BLK], scaled[BLK:]).astype(BF16)
    out_ref[...] = out_low
    grad = do_ref[...].astype(F32)
    products = (out_low.astype(F32) * grad).T
    delta = jnp.concatenate(
        [
            jnp.sum(products[:DH], axis=0, keepdims=True),
            jnp.sum(products[DH:], axis=0, keepdims=True),
        ],
        axis=1,
    )
    delta = delta * inverse
    grad_stack = jnp.concatenate(
        [
            jnp.where(low, grad * inverse_cols[:BLK], 0.0),
            jnp.where(low, 0.0, grad * inverse_cols[BLK:]),
        ],
        axis=0,
    ).astype(BF16)
    dq_stack = None
    pay = pay_ref[...]
    lanes = lane_iota((1, LANES))
    head = half * half_heads + 2 * pair
    for s in range(section_count):
        dprob = contract(value_list[s], grad_stack, 1, 1)
        dscore = weights[s] * (dprob - delta)
        dscore_low = dscore.astype(BF16)
        sums = jnp.sum(dscore, axis=0, keepdims=True)
        even = jnp.sum(sums[:, :BLK], axis=1, keepdims=True)
        odd = jnp.sum(sums[:, BLK:], axis=1, keepdims=True)
        pay = jnp.where(lanes == s * H + head, even, pay)
        pay = jnp.where(lanes == s * H + head + 1, odd, pay)
        term = contract(dscore_low, key_list[s], 0, 0)
        dq_stack = term if dq_stack is None else dq_stack + term
        key_term = contract(dscore_low, q_stack, 1, 0)
        value_term = contract(weights_low[s], grad_stack, 1, 0)
        if s == 0:
            own_ref[0:BLK, :] = key_term
            own_ref[BLK : 2 * BLK, :] = value_term
        else:
            term_refs[s - 1][0:BLK, :] = key_term.astype(BF16)
            term_refs[s - 1][BLK : 2 * BLK, :] = value_term.astype(BF16)
    pay_ref[...] = pay
    dq_ref[...] = (jnp.where(low, dq_stack[:BLK], dq_stack[BLK:]) * 0.125).astype(BF16)


def attention_half(half, scalars, table_rows, rows, partners, infos, previous):
    section_count = len(partners) + 1
    level_count = section_count - 1
    row_count, feature_count = rows[0].shape
    half_features = feature_count // HALVES
    pairs = half_features // PAIR_LANES
    half_heads = half_features // DH
    first = previous is None
    mask, bucket, seg = scalars

    def whole(shape):
        return pl.BlockSpec(shape, lambda j: (0,) * len(shape))

    row_spec = pl.BlockSpec((row_count, PAIR_LANES), lambda j: (0, half * pairs + j))

    def column_spec(array):
        return pl.BlockSpec((array.shape[0], PAIR_LANES), lambda j: (0, j))

    smem = pl.BlockSpec(memory_space=pltpu.SMEM)
    operands = [mask, bucket, seg, table_rows, *rows, *partners]
    in_specs = [
        smem,
        smem,
        whole(seg.shape),
        pl.BlockSpec((half_heads * NB, NB), lambda j: (half, 0)),
        *[row_spec] * 4,
        *[column_spec(p) for p in partners],
    ]
    aliases = {}
    if not first:
        operands += [*infos, previous[3], previous[0], previous[1]]
        in_specs += [pl.BlockSpec((p.shape[0], PAIR_LANES), lambda j: (0, 0)) for p in infos]
        in_specs += [whole((1, LANES))] + [pl.BlockSpec(memory_space=pl.ANY)] * 2
        aliases = {len(operands) - 2: 0, len(operands) - 1: 1}
    packed = jax.ShapeDtypeStruct((2 * row_count, half_features), BF16)
    out_shape = [
        jax.ShapeDtypeStruct((row_count, feature_count), BF16),
        jax.ShapeDtypeStruct((row_count, feature_count), BF16),
        jax.ShapeDtypeStruct((2 * row_count, half_features), F32),
        jax.ShapeDtypeStruct((1, LANES), F32),
        *[packed] * level_count,
    ]
    out_specs = [
        row_spec,
        row_spec,
        column_spec(out_shape[2]),
        whole((1, LANES)),
        *[column_spec(packed)] * level_count,
    ]
    return pl.pallas_call(
        functools.partial(attention_body, section_count, half, first),
        grid=(pairs,),
        in_specs=in_specs,
        out_specs=out_specs,
        out_shape=out_shape,
        scratch_shapes=[
            pltpu.VMEM((section_count * BLK, BLK), F32),
            pltpu.VMEM((section_count, half_heads, LANES), F32),
        ],
        input_output_aliases=aliases,
        compiler_params=pltpu.CompilerParams(dimension_semantics=("arbitrary",)),
        cost_estimate=pl.CostEstimate(
            flops=12 * section_count * half_heads * BLK * BLK * DH,
            bytes_accessed=4 * 2**20,
            transcendentals=section_count * half_heads * BLK * BLK,
        ),
        name="attention",
    )(*operands)


def finish_body(level_count, *refs):
    own_ref = refs[0]
    term_refs = refs[1 : 1 + level_count]
    key_ref, value_ref = refs[-2:]
    total = own_ref[...]
    for term in term_refs:
        total = total + term[...].astype(F32)
    total = total.astype(BF16)
    key_ref[...] = total[:BLK]
    value_ref[...] = total[BLK:]


def finish_half(half, own, terms, previous):
    row_count = own.shape[0] // 2
    half_features = own.shape[1]
    feature_count = half_features * HALVES
    step = 2 * PAIR_LANES
    steps = half_features // step
    column = pl.BlockSpec((2 * row_count, step), lambda j: (0, j))
    out_spec = pl.BlockSpec((row_count, step), lambda j: (0, half * steps + j))
    out = jax.ShapeDtypeStruct((row_count, feature_count), BF16)
    operands = [own, *terms]
    in_specs = [column] * len(operands)
    aliases = {}
    if previous is not None:
        operands += list(previous)
        in_specs += [pl.BlockSpec(memory_space=pl.ANY)] * 2
        aliases = {len(operands) - 2: 0, len(operands) - 1: 1}
    return pl.pallas_call(
        functools.partial(finish_body, len(terms)),
        grid=(steps,),
        in_specs=in_specs,
        out_specs=[out_spec, out_spec],
        out_shape=[out, out],
        input_output_aliases=aliases,
        compiler_params=pltpu.CompilerParams(dimension_semantics=("arbitrary",)),
        cost_estimate=pl.CostEstimate(flops=2**19, bytes_accessed=2**21, transcendentals=0),
        name="finish",
    )(*operands)


def table_body(section_count, gathered_ref, table_ref):
    gathered = gathered_ref[...]
    count = gathered.shape[0]
    lanes = lane_iota((count, PAIR_LANES))
    column = jnp.where(lanes < NB, lanes, lanes - NB).astype(F32)
    row_hot = (lane_iota((count, NB)).astype(F32) == gathered[:, BUCKET_LANE : BUCKET_LANE + 1]).astype(F32)
    rows = jnp.concatenate([row_hot] * section_count, axis=0)
    hots = [
        column == gathered[:, BUCKET_LANE + s : BUCKET_LANE + s + 1] for s in range(section_count)
    ]
    for pair in range(H // 2):
        parts = []
        for s in range(section_count):
            lane = s * H + 2 * pair
            value = jnp.where(lanes < NB, gathered[:, lane : lane + 1], gathered[:, lane + 1 : lane + 2])
            parts.append(jnp.where(hots[s], value, 0.0))
        tile = lax.dot_general(
            rows,
            jnp.concatenate(parts, axis=0),
            (((0,), (0,)), ((), ())),
            preferred_element_type=F32,
            precision=lax.Precision.HIGHEST,
        )
        table_ref[2 * pair] = tile[:, :NB]
        table_ref[2 * pair + 1] = tile[:, NB:]


def table_of(payload, section_count):
    gathered = payload
    for axis in ("dp", "seq"):
        mask = 1
        while mask < lax.axis_size(axis):
            gathered = jnp.concatenate([gathered, from_partner(gathered, axis, mask)], axis=0)
            mask *= 2
    return pl.pallas_call(
        functools.partial(table_body, section_count),
        out_shape=jax.ShapeDtypeStruct((H, NB, NB), F32),
        name="table",
    )(gathered)


def local(queries, keys, values, d_out, segment_ids, block_bucket, block_mask, bias_table):
    feature_count = queries.shape[2]
    half_features = feature_count // HALVES
    level_count = lax.axis_size("seq").bit_length() - 1
    section_count = level_count + 1
    rows = [queries[0], d_out[0], keys[0], values[0]]
    own_keys, own_values = rows[2], rows[3]
    scalars = (block_mask.reshape(-1), block_bucket.reshape(-1), segment_ids)
    table_rows = bias_table.reshape(H * NB, NB)
    seg_line = jnp.tile(segment_ids.astype(BF16), (1, half_features // BLK))
    bucket_line = jnp.broadcast_to(block_bucket.astype(BF16), (INFO - 1, half_features))
    info = jnp.concatenate([seg_line, bucket_line], axis=0)
    packs = []
    for half in range(HALVES):
        window = slice(half * half_features, (half + 1) * half_features)
        pieces = [own_keys[:, window], own_values[:, window]]
        packs.append(jnp.concatenate(pieces + ([info] if half == 0 else []), axis=0))
    arrived = [[None] * level_count for _ in range(HALVES)]
    for half in range(HALVES):
        for level in reversed(range(level_count)):
            arrived[half][level] = from_partner(packs[half], "seq", 1 << level)
    result = None
    finished = None
    for half in range(HALVES):
        result = attention_half(
            half, scalars, table_rows, rows, arrived[half], arrived[0], result
        )
        back = [None] * level_count
        for level in reversed(range(level_count)):
            back[level] = from_partner(result[4 + level], "seq", 1 << level)
        finished = finish_half(half, result[2], back, finished)
    table_total = table_of(result[3], section_count)
    return (result[0][None], result[1][None], finished[0][None], finished[1][None], table_total)


def solution(mesh):
    rows = P("dp", "seq", None)
    in_specs = (
        rows,
        rows,
        rows,
        rows,
        P("dp", "seq"),
        P("dp", "seq"),
        P("dp", "seq", None, None),
        P(),
    )
    return jax.shard_map(
        local, mesh=mesh, in_specs=in_specs, out_specs=(rows,) * 4 + (P(),), check_vma=False
    )
```

time: 258 us -> 94.9 us (0.37)
  waiting for transfers between devices: 136 us -> 31.9 us
  matrix products: 38.1 us -> 0 us
  Pallas kernels: 0 us -> 27 us
  local copies, waits for them, and re-layouts: 28.9 us -> 7.39 us
  between operations: 17.7 us -> 1.55 us
  other arithmetic: 9.98 us -> 0.16 us
    psum x1 -> x0, waiting for transfers between devices: 109 us -> none  [local(): table_total = lax.psum(table_acc, ('seq', 'dp'))]
    dot_general x36 -> x0, matrix products: 38.1 us -> none  [the longest x5 11 us: local(): jnp.einsum('htu,uhd->thd', weights.astype(jnp.bfloat16), value_heads, pre...]
    pallas_call x0 -> x5, Pallas kernels: none -> 27 us  [the longest x2 20.1 us: attention_half(): pl.pallas_call(functools.partial(attention_body, section_count, half, fir...]
    ppermute x8 -> x0, local copies, waits for them, and re-layouts: 13.4 us -> none  [from_partner(): return lax.ppermute(value, axis, pairs)]
    unnamed x77 -> x46, local copies, waits for them, and re-layouts: 14.8 us -> 4.36 us
    ppermute x24 -> x21, waiting for transfers between devices: 27.1 us -> 31.9 us  [from_partner(): return lax.ppermute(value, axis, pairs)]
    eq x1 -> x0, other arithmetic: 2.64 us -> none  [allowed_pairs(): seg_rows.astype(jnp.float32)[:, None]]
    ppermute x24 -> x21, starting transfers between devices: 26.2 us -> 26.6 us  [from_partner(): return lax.ppermute(value, axis, pairs)]
  transfers between devices with their start and end apart: 25 -> 21, of which waited for: 9 -> 7; matrix products, arithmetic and copies ran while one was open for 17% -> 2% of each run, Pallas kernels for 0% -> 16%
where the time goes in v1:
time: 94.9 us; the launch traced here: 94.5 us
  waiting for transfers between devices  31.9 us (34%)
  Pallas kernels  27 us (28%)
  starting transfers between devices  26.6 us (28%)
  local copies, waits for them, and re-layouts  7.39 us (8%)
  between operations  1.55 us (2%)
    ppermute x21, waiting for transfers between devices, from_partner(): return lax.ppermute(value, axis, pairs)  31.9 us
    ppermute x21, starting transfers between devices, from_partner(): return lax.ppermute(value, axis, pairs)  26.6 us
    pallas_call x2, Pallas kernels, attention_half(): pl.pallas_call(functools.partial(attention_body, section_count, half, fir...  20.1 us
    unnamed x46, local copies, waits for them, and re-layouts  4.36 us
    pallas_call x2, Pallas kernels, finish_half(): pl.pallas_call(functools.partial(finish_body, len(terms)), grid=(steps,),...  4.22 us
    pallas_call x1, Pallas kernels, table_of(): pl.pallas_call(functools.partial(table_body, section_count), out_shape=ja...  2.62 us
  transfers between devices with their start and end apart: 21, of which 7 were waited for; matrix products, arithmetic and copies ran while one was open for 2% of the time, Pallas kernels for 16%

profile of v1, /device:TPU:0, one launch (start us, length us, event | category | flops | bytes accessed | tf_op | source)
XLA Modules:
  0.0 94.5 jit_solution(16521957104803794493)
XLA Ops:
  1.3 0.6 copy-done.17
  2.0 1.1 %fusion = (bf16[128,512]{1,0:T(8,128)(2,1)S(1)}, bf16[128,512]{1,0:T(8,128)(2,1)S(1)}, bf16[128,512]{1,0:T(8,128)(2,1)S(1)}, bf16[128,512]{1,0:T(8,128)(2,1)S(1)}) fusion(bf16[128,1024]{1,0:T(8,128)(2,1)} %bitcast.22, bf16[128,1024]{1,0:T(8,128)(2,1)} %bitcast.25), kind=kLoop, calls=%fused_computation.8 | loop fusion | bytes 1048576 | tf_op jit(solution)/shard_map/slice | solution.py:340
  3.3 4.1 %collective-permute-start.7 = (bf16[264,512]{1,0:T(8,128)(2,1)S(1)}, bf16[264,512]{1,0:T(8,128)(2,1)S(1)}, u32[]{:S(2)}, u32[]{:S(2)}) collective-permute-start(bf16[264,512]{1,0:T(8,128)(2,1)S(1)} %maximum_maximum_fusion), channel_id=1, source_target_pairs={{0,16},{2,18},{4,20},{6,22},{8,24},{10,26},{12,28},{14,30},{16,0},... | collective-permute-start | bytes 811016 | tf_op jit(solution)/shard_map/ppermute | solution.py:31
  7.4 1.6 %collective-permute-start.6 = (bf16[264,512]{1,0:T(8,128)(2,1)S(1)}, bf16[264,512]{1,0:T(8,128)(2,1)S(1)}, u32[]{:S(2)}, u32[]{:S(2)}) collective-permute-start(bf16[264,512]{1,0:T(8,128)(2,1)S(1)} %maximum_maximum_fusion), channel_id=1, source_target_pairs={{0,8},{2,10},{4,12},{6,14},{8,0},{10,2},{12,4},{14,6},{16,24},{18,... | collective-permute-start | bytes 811016 | tf_op jit(solution)/shard_map/ppermute | solution.py:31
  9.0 1.5 %collective-permute-start.5 = (bf16[264,512]{1,0:T(8,128)(2,1)S(1)}, bf16[264,512]{1,0:T(8,128)(2,1)S(1)}, u32[]{:S(2)}, u32[]{:S(2)}) collective-permute-start(bf16[264,512]{1,0:T(8,128)(2,1)S(1)} %maximum_maximum_fusion), channel_id=1, source_target_pairs={{0,4},{2,6},{4,0},{6,2},{8,12},{10,14},{12,8},{14,10},{16,20},{18,... | collective-permute-start | bytes 811016 | tf_op jit(solution)/shard_map/ppermute | solution.py:31
  10.9 10.5 %collective-permute-done.7.refs_11_.refs_15_ = bf16[264,512]{1,0:T(8,128)(2,1)S(1)} collective-permute-done((bf16[264,512]{1,0:T(8,128)(2,1)S(1)}, bf16[264,512]{1,0:T(8,128)(2,1)S(1)}, u32[]{:S(2)}, u32[]{:S(2)}) %collective-permute-start.7) | collective-permute-done | bytes 270368 | tf_op jit(solution)/shard_map/ppermute | solution.py:31
  21.4 5.6 %collective-permute-start.1 = (bf16[256,512]{1,0:T(8,128)(2,1)S(1)}, bf16[256,512]{1,0:T(8,128)(2,1)S(1)}, u32[]{:S(2)}, u32[]{:S(2)}) collective-permute-start(bf16[256,512]{1,0:T(8,128)(2,1)S(1)} %pad_maximum_fusion), channel_id=1, source_target_pairs={{0,4},{2,6},{4,0},{6,2},{8,12},{10,14},{12,8},{14,10},{16,20},{18,... | collective-permute-start | bytes 786440 | tf_op jit(solution)/shard_map/ppermute | solution.py:31
  27.1 0.7 copy-done.2
  27.9 9.9 %attention.2 = (bf16[128,1024]{1,0:T(8,128)(2,1)}, bf16[128,1024]{1,0:T(8,128)(2,1)}, f32[256,512]{1,0:T(8,128)}, f32[1,128]{1,0:T(1,128)}, bf16[256,512]{1,0:T(...) custom-call(s32[5]{0:T(128)} %bitcast.39, s32[1]{0:T(128)} %bitcast.20.refs_1_, ...), custom_call_target="tpu_custom_call" | custom-call | flops 503316480 | bytes 4194304 | tf_op jit(solution)/shard_map/attention/pallas_call | solution.py:222
  37.9 0.6 copy-done.4
  38.8 10.2 %attention.3 = (bf16[128,1024]{1,0:T(8,128)(2,1)}, bf16[128,1024]{1,0:T(8,128)(2,1)}, f32[256,512]{1,0:T(8,128)}, f32[1,128]{1,0:T(1,128)}, bf16[256,512]{1,0:T(...) custom-call(s32[5]{0:T(128)} %bitcast.40, ...), custom_call_target="tpu_custom_call", output_to_operand_aliasing={{0}: (17, {}), {1}: (18, {})} | custom-call | flops 503316480 | bytes 4194304 | tf_op jit(solution)/shard_map/attention/pallas_call | solution.py:222
  49.0 0.6 copy-done.16
  49.6 1.5 %collective-permute-start.16 = (f32[1,128]{1,0:T(1,128)S(1)}, f32[1,128]{1,0:T(1,128)S(1)}, u32[]{:S(2)}, u32[]{:S(2)}) collective-permute-start(f32[1,128]{1,0:T(1,128)S(1)} %copy-done.16), channel_id=1, source_target_pairs={{0,1},{1,0},{2,3},{3,2},{4,5},{5,4},{6,7},{7,6},{8,9},{9,8},{10,11... | collective-permute-start | bytes 1544 | tf_op jit(solution)/shard_map/ppermute | solution.py:31
  51.2 0.5 collective-permute-start.13
  51.8 1.9 %collective-permute-start.14 = (bf16[256,512]{1,0:T(8,128)(2,1)S(1)}, bf16[256,512]{1,0:T(8,128)(2,1)S(1)}, u32[]{:S(2)}, u32[]{:S(2)}) collective-permute-start(bf16[256,512]{1,0:T(8,128)(2,1)S(1)} %copy-done.19), channel_id=1, source_target_pairs={{0,8},{2,10},{4,12},{6,14},{8,0},{10,2},{12,4},{14,6},{16,24},{18,... | collective-permute-start | bytes 786440 | tf_op jit(solution)/shard_map/ppermute | solution.py:31
  53.8 1.1 %collective-permute-done.17 = f32[2,128]{1,0:T(2,128)S(1)} collective-permute-done((f32[2,128]{1,0:T(2,128)S(1)}, f32[2,128]{1,0:T(2,128)S(1)}, u32[]{:S(2)}, u32[]{:S(2)}) %collective-permute-start.17) | collective-permute-done | bytes 1056 | tf_op jit(solution)/shard_map/ppermute | solution.py:31
  54.9 1.6 %collective-permute-start.18 = (f32[4,128]{1,0:T(4,128)S(1)}, f32[4,128]{1,0:T(4,128)S(1)}, u32[]{:S(2)}, u32[]{:S(2)}) collective-permute-start(f32[4,128]{1,0:T(4,128)S(1)} %pad_maximum_fusion.2), channel_id=1, source_target_pairs={{0,4},{2,6},{4,0},{6,2},{8,12},{10,14},{12,8},{14,10},{16,20},{18,... | collective-permute-start | bytes 6152 | tf_op jit(solution)/shard_map/ppermute | solution.py:31
  56.5 3.3 %collective-permute-done.18 = f32[4,128]{1,0:T(4,128)S(1)} collective-permute-done((f32[4,128]{1,0:T(4,128)S(1)}, f32[4,128]{1,0:T(4,128)S(1)}, u32[]{:S(2)}, u32[]{:S(2)}) %collective-permute-start.18) | collective-permute-done | bytes 2080 | tf_op jit(solution)/shard_map/ppermute | solution.py:31
  59.9 2.0 %collective-permute-start.19 = (f32[8,128]{1,0:T(8,128)S(1)}, f32[8,128]{1,0:T(8,128)S(1)}, u32[]{:S(2)}, u32[]{:S(2)}) collective-permute-start(f32[8,128]{1,0:T(8,128)S(1)} %pad_maximum_fusion.1), channel_id=1, source_target_pairs={{0,8},{2,10},{4,12},{6,14},{8,0},{10,2},{12,4},{14,6},{16,24},{18,... | collective-permute-start | bytes 12296 | tf_op jit(solution)/shard_map/ppermute | solution.py:31
  61.9 1.7 %collective-permute-done.19 = f32[8,128]{1,0:T(8,128)S(1)} collective-permute-done((f32[8,128]{1,0:T(8,128)S(1)}, f32[8,128]{1,0:T(8,128)S(1)}, u32[]{:S(2)}, u32[]{:S(2)}) %collective-permute-start.19) | collective-permute-done | bytes 4128 | tf_op jit(solution)/shard_map/ppermute | solution.py:31
  63.7 4.5 %collective-permute-done.20 = f32[16,128]{1,0:T(8,128)S(1)} collective-permute-done((f32[16,128]{1,0:T(8,128)S(1)}, f32[16,128]{1,0:T(8,128)S(1)}, u32[]{:S(2)}, u32[]{:S(2)}) %collective-permute-start.20) | collective-permute-done | bytes 8224 | tf_op jit(solution)/shard_map/ppermute | solution.py:31
  68.2 0.6 collective-permute-start.9
  68.8 2.1 %collective-permute-start.10 = (bf16[256,512]{1,0:T(8,128)(2,1)}, bf16[256,512]{1,0:T(8,128)(2,1)S(1)}, u32[]{:S(2)}, u32[]{:S(2)}) collective-permute-start(bf16[256,512]{1,0:T(8,128)(2,1)} %get-tuple-element.33), channel_id=1, source_target_pairs={{0,8},{2,10},{4,12},{6,14},{8,0},{10,2},{12,4},{14,6},{16,24},{18,... | collective-permute-start | bytes 786440 | tf_op jit(solution)/shard_map/ppermute | solution.py:31
  70.8 2.8 %collective-permute-start.11 = (bf16[256,512]{1,0:T(8,128)(2,1)}, bf16[256,512]{1,0:T(8,128)(2,1)S(1)}, u32[]{:S(2)}, u32[]{:S(2)}) collective-permute-start(bf16[256,512]{1,0:T(8,128)(2,1)} %get-tuple-element.34), channel_id=1, source_target_pairs={{0,16},{2,18},{4,20},{6,22},{8,24},{10,26},{12,28},{14,30},{16,0},... | collective-permute-start | bytes 786440 | tf_op jit(solution)/shard_map/ppermute | solution.py:31
  73.7 1.8 %concatenate.31.gathered_ref = f32[32,128]{1,0:T(8,128)} concatenate(f32[1,128]{1,0:T(1,128)S(1)} %copy-done.16, f32[1,128]{1,0:T(1,128)S(1)} %collective-permute-done.16, f32[2,128]{1,0:T(2,128)S(1)} %collective-permute-done.17, f32[4,128]{1,0:T(4,128)S(1)} %collective-permute-done.18, f32[8,128]{1,0:T(8,128)S(1)} %collective-permute-done.19, f32[16,128]{1,0:T(8,128)S(1)} %collective-permute-done.20), dimensions={0} | concatenate | bytes 32768 | tf_op jit(solution)/shard_map/concatenate | solution.py:316
  75.5 2.6 %table.1 = f32[16,64,64]{2,1,0:T(8,128)} custom-call(f32[32,128]{1,0:T(8,128)} %concatenate.31.gathered_ref), custom_call_target="tpu_custom_call" | custom-call | tf_op jit(solution)/shard_map/table/pallas_call | solution.py:318
  78.1 9.2 %collective-permute-done.15.refs_4_ = bf16[256,512]{1,0:T(8,128)(2,1)S(1)} collective-permute-done((bf16[256,512]{1,0:T(8,128)(2,1)S(1)}, bf16[256,512]{1,0:T(8,128)(2,1)S(1)}, u32[]{:S(2)}, u32[]{:S(2)}) %collective-permute-start.15) | collective-permute-done | bytes 262176 | tf_op jit(solution)/shard_map/ppermute | solution.py:31
  87.3 0.7 copy-done.11
  88.0 2.1 %finish.2 = (bf16[128,1024]{1,0:T(8,128)(2,1)}, bf16[128,1024]{1,0:T(8,128)(2,1)}) custom-call(f32[256,512]{1,0:T(8,128)} %get-tuple-element.35.refs_0_, bf16[256,512]{1,0:T(8,128)(2,1)} %copy-done.8, bf16[256,512]{1,0:T(8,128)(2,1)} %copy-done.9, bf16[256,512]{1,0:T(8,128)(2,1)} %copy-done.10, bf16[256,512]{1,0:T(8,128)(2,1)} %copy-done.11), custom_call_target="tpu_custom_call" | custom-call | flops 524288 | bytes 2097152 | tf_op jit(solution)/shard_map/finish/pallas_call | solution.py:271
  90.2 1.5 %collective-permute-done.11.refs_4_ = bf16[256,512]{1,0:T(8,128)(2,1)S(1)} collective-permute-done((bf16[256,512]{1,0:T(8,128)(2,1)}, bf16[256,512]{1,0:T(8,128)(2,1)S(1)}, u32[]{:S(2)}, u32[]{:S(2)}) %collective-permute-start.11) | collective-permute-done | bytes 262176 | tf_op jit(solution)/shard_map/ppermute | solution.py:31
  91.7 0.7 copy-done.15
  92.4 2.1 %finish.3 = (bf16[128,1024]{1,0:T(8,128)(2,1)}, bf16[128,1024]{1,0:T(8,128)(2,1)}) custom-call(f32[256,512]{1,0:T(8,128)} %get-tuple-element.30.refs_0_, bf16[256,512]{1,0:T(8,128)(2,1)} %copy-done.12, bf16[256,512]{1,0:T(8,128)(2,1)} %copy-done.13, bf16[256,512]{1,0:T(8,128)(2,1)} %copy-done.14, ...), custom_call_target="tpu_custom_call", output_to_operand_aliasing={{0}: (5, {}), {1}: (6, {})} | custom-call | flops 524288 | bytes 2097152 | tf_op jit(solution)/shard_map/finish/pallas_call | solution.py:271
  (72 shorter events, 1.5 us)
Async XLA Ops:
  3.3 18.1 %collective-permute-start.7 = (bf16[264,512]{1,0:T(8,128)(2,1)S(1)}, bf16[264,512]{1,0:T(8,128)(2,1)S(1)}, u32[]{:S(2)}, u32[]{:S(2)}) collective-permute-start(bf16[264,512]{1,0:T(8,128)(2,1)S(1)} %maximum_maximum_fusion), channel_id=1, source_target_pairs={{0,16},{2,18},{4,20},{6,22},{8,24},{10,26},{12,28},{14,30},{16,0},... | collective-permute-start | bytes 811016 | tf_op jit(solution)/shard_map/ppermute | solution.py:31
  7.4 14.0 %collective-permute-start.6 = (bf16[264,512]{1,0:T(8,128)(2,1)S(1)}, bf16[264,512]{1,0:T(8,128)(2,1)S(1)}, u32[]{:S(2)}, u32[]{:S(2)}) collective-permute-start(bf16[264,512]{1,0:T(8,128)(2,1)S(1)} %maximum_maximum_fusion), channel_id=1, source_target_pairs={{0,8},{2,10},{4,12},{6,14},{8,0},{10,2},{12,4},{14,6},{16,24},{18,... | collective-permute-start | bytes 811016 | tf_op jit(solution)/shard_map/ppermute | solution.py:31
  9.0 18.1 %collective-permute-start.5 = (bf16[264,512]{1,0:T(8,128)(2,1)S(1)}, bf16[264,512]{1,0:T(8,128)(2,1)S(1)}, u32[]{:S(2)}, u32[]{:S(2)}) collective-permute-start(bf16[264,512]{1,0:T(8,128)(2,1)S(1)} %maximum_maximum_fusion), channel_id=1, source_target_pairs={{0,4},{2,6},{4,0},{6,2},{8,12},{10,14},{12,8},{14,10},{16,20},{18,... | collective-permute-start | bytes 811016 | tf_op jit(solution)/shard_map/ppermute | solution.py:31
  10.5 16.6 %collective-permute-start.4 = (bf16[264,512]{1,0:T(8,128)(2,1)S(1)}, bf16[264,512]{1,0:T(8,128)(2,1)S(1)}, u32[]{:S(2)}, u32[]{:S(2)}) collective-permute-start(bf16[264,512]{1,0:T(8,128)(2,1)S(1)} %maximum_maximum_fusion), channel_id=1, source_target_pairs={{0,2},{2,0},{4,6},{6,4},{8,10},{10,8},{12,14},{14,12},{16,18},{18,... | collective-permute-start | bytes 811016 | tf_op jit(solution)/shard_map/ppermute | solution.py:31
  10.5 27.3 %collective-permute-start.3 = (bf16[256,512]{1,0:T(8,128)(2,1)S(1)}, bf16[256,512]{1,0:T(8,128)(2,1)S(1)}, u32[]{:S(2)}, u32[]{:S(2)}) collective-permute-start(bf16[256,512]{1,0:T(8,128)(2,1)S(1)} %pad_maximum_fusion), channel_id=1, source_target_pairs={{0,16},{2,18},{4,20},{6,22},{8,24},{10,26},{12,28},{14,30},{16,0},... | collective-permute-start | bytes 786440 | tf_op jit(solution)/shard_map/ppermute | solution.py:31
  21.4 5.7 %copy-start = (bf16[264,512]{1,0:T(8,128)(2,1)}, bf16[264,512]{1,0:T(8,128)(2,1)S(1)}, u32[]{:S(2)}) copy-start(bf16[264,512]{1,0:T(8,128)(2,1)S(1)} %collective-permute-done.7.refs_11_.refs_15_) | copy-start | bytes 811012
  21.4 16.4 %collective-permute-start.2 = (bf16[256,512]{1,0:T(8,128)(2,1)S(1)}, bf16[256,512]{1,0:T(8,128)(2,1)S(1)}, u32[]{:S(2)}, u32[]{:S(2)}) collective-permute-start(bf16[256,512]{1,0:T(8,128)(2,1)S(1)} %pad_maximum_fusion), channel_id=1, source_target_pairs={{0,8},{2,10},{4,12},{6,14},{8,0},{10,2},{12,4},{14,6},{16,24},{18,... | collective-permute-start | bytes 786440 | tf_op jit(solution)/shard_map/ppermute | solution.py:31
  21.4 5.7 %copy-start.1 = (bf16[264,512]{1,0:T(8,128)(2,1)}, bf16[264,512]{1,0:T(8,128)(2,1)S(1)}, u32[]{:S(2)}) copy-start(bf16[264,512]{1,0:T(8,128)(2,1)S(1)} %collective-permute-done.6.refs_10_.refs_14_) | copy-start | bytes 811012
  21.4 16.4 %collective-permute-start.1 = (bf16[256,512]{1,0:T(8,128)(2,1)S(1)}, bf16[256,512]{1,0:T(8,128)(2,1)S(1)}, u32[]{:S(2)}, u32[]{:S(2)}) collective-permute-start(bf16[256,512]{1,0:T(8,128)(2,1)S(1)} %pad_maximum_fusion), channel_id=1, source_target_pairs={{0,4},{2,6},{4,0},{6,2},{8,12},{10,14},{12,8},{14,10},{16,20},{18,... | collective-permute-start | bytes 786440 | tf_op jit(solution)/shard_map/ppermute | solution.py:31
  27.1 10.8 %collective-permute-start = (bf16[256,512]{1,0:T(8,128)(2,1)S(1)}, bf16[256,512]{1,0:T(8,128)(2,1)S(1)}, u32[]{:S(2)}, u32[]{:S(2)}) collective-permute-start(bf16[256,512]{1,0:T(8,128)(2,1)S(1)} %pad_maximum_fusion), channel_id=1, source_target_pairs={{0,2},{2,0},{4,6},{6,4},{8,10},{10,8},{12,14},{14,12},{16,18},{18,... | collective-permute-start | bytes 786440 | tf_op jit(solution)/shard_map/ppermute | solution.py:31
  38.8 12.3 %copy-start.21 = (bf16[256,512]{1,0:T(8,128)(2,1)S(1)}, bf16[256,512]{1,0:T(8,128)(2,1)}, u32[]{:S(2)}) copy-start(bf16[256,512]{1,0:T(8,128)(2,1)} %get-tuple-element.36) | copy-start | bytes 786436
  38.8 12.5 %copy-start.20 = (bf16[256,512]{1,0:T(8,128)(2,1)S(1)}, bf16[256,512]{1,0:T(8,128)(2,1)}, u32[]{:S(2)}) copy-start(bf16[256,512]{1,0:T(8,128)(2,1)} %get-tuple-element.37) | copy-start | bytes 786436
  38.8 13.0 %copy-start.19 = (bf16[256,512]{1,0:T(8,128)(2,1)S(1)}, bf16[256,512]{1,0:T(8,128)(2,1)}, u32[]{:S(2)}) copy-start(bf16[256,512]{1,0:T(8,128)(2,1)} %get-tuple-element.38) | copy-start | bytes 786436
  38.8 29.4 %copy-start.18 = (bf16[256,512]{1,0:T(8,128)(2,1)S(1)}, bf16[256,512]{1,0:T(8,128)(2,1)}, u32[]{:S(2)}) copy-start(bf16[256,512]{1,0:T(8,128)(2,1)} %get-tuple-element.39) | copy-start | bytes 786436
  49.6 4.1 %collective-permute-start.16 = (f32[1,128]{1,0:T(1,128)S(1)}, f32[1,128]{1,0:T(1,128)S(1)}, u32[]{:S(2)}, u32[]{:S(2)}) collective-permute-start(f32[1,128]{1,0:T(1,128)S(1)} %copy-done.16), channel_id=1, source_target_pairs={{0,1},{1,0},{2,3},{3,2},{4,5},{5,4},{6,7},{7,6},{8,9},{9,8},{10,11... | collective-permute-start | bytes 1544 | tf_op jit(solution)/shard_map/ppermute | solution.py:31
  51.1 17.1 %collective-permute-start.12 = (bf16[256,512]{1,0:T(8,128)(2,1)S(1)}, bf16[256,512]{1,0:T(8,128)(2,1)S(1)}, u32[]{:S(2)}, u32[]{:S(2)}) collective-permute-start(bf16[256,512]{1,0:T(8,128)(2,1)S(1)} %copy-done.21), channel_id=1, source_target_pairs={{0,2},{2,0},{4,6},{6,4},{8,10},{10,8},{12,14},{14,12},{16,18},{18,... | collective-permute-start | bytes 786440 | tf_op jit(solution)/shard_map/ppermute | solution.py:31
  51.2 17.5 %collective-permute-start.13 = (bf16[256,512]{1,0:T(8,128)(2,1)S(1)}, bf16[256,512]{1,0:T(8,128)(2,1)S(1)}, u32[]{:S(2)}, u32[]{:S(2)}) collective-permute-start(bf16[256,512]{1,0:T(8,128)(2,1)S(1)} %copy-done.20), channel_id=1, source_target_pairs={{0,4},{2,6},{4,0},{6,2},{8,12},{10,14},{12,8},{14,10},{16,20},{18,... | collective-permute-start | bytes 786440 | tf_op jit(solution)/shard_map/ppermute | solution.py:31
  51.8 19.1 %collective-permute-start.14 = (bf16[256,512]{1,0:T(8,128)(2,1)S(1)}, bf16[256,512]{1,0:T(8,128)(2,1)S(1)}, u32[]{:S(2)}, u32[]{:S(2)}) collective-permute-start(bf16[256,512]{1,0:T(8,128)(2,1)S(1)} %copy-done.19), channel_id=1, source_target_pairs={{0,8},{2,10},{4,12},{6,14},{8,0},{10,2},{12,4},{14,6},{16,24},{18,... | collective-permute-start | bytes 786440 | tf_op jit(solution)/shard_map/ppermute | solution.py:31
  53.7 1.2 %collective-permute-start.17 = (f32[2,128]{1,0:T(2,128)S(1)}, f32[2,128]{1,0:T(2,128)S(1)}, u32[]{:S(2)}, u32[]{:S(2)}) collective-permute-start(f32[2,128]{1,0:T(2,128)S(1)} %pad_maximum_fusion.3), channel_id=1, source_target_pairs={{0,2},{2,0},{4,6},{6,4},{8,10},{10,8},{12,14},{14,12},{16,18},{18,... | collective-permute-start | bytes 3080 | tf_op jit(solution)/shard_map/ppermute | solution.py:31
  54.9 4.9 %collective-permute-start.18 = (f32[4,128]{1,0:T(4,128)S(1)}, f32[4,128]{1,0:T(4,128)S(1)}, u32[]{:S(2)}, u32[]{:S(2)}) collective-permute-start(f32[4,128]{1,0:T(4,128)S(1)} %pad_maximum_fusion.2), channel_id=1, source_target_pairs={{0,4},{2,6},{4,0},{6,2},{8,12},{10,14},{12,8},{14,10},{16,20},{18,... | collective-permute-start | bytes 6152 | tf_op jit(solution)/shard_map/ppermute | solution.py:31
  59.9 3.7 %collective-permute-start.19 = (f32[8,128]{1,0:T(8,128)S(1)}, f32[8,128]{1,0:T(8,128)S(1)}, u32[]{:S(2)}, u32[]{:S(2)}) collective-permute-start(f32[8,128]{1,0:T(8,128)S(1)} %pad_maximum_fusion.1), channel_id=1, source_target_pairs={{0,8},{2,10},{4,12},{6,14},{8,0},{10,2},{12,4},{14,6},{16,24},{18,... | collective-permute-start | bytes 12296 | tf_op jit(solution)/shard_map/ppermute | solution.py:31
  63.6 4.6 %collective-permute-start.20 = (f32[16,128]{1,0:T(8,128)S(1)}, f32[16,128]{1,0:T(8,128)S(1)}, u32[]{:S(2)}, u32[]{:S(2)}) collective-permute-start(f32[16,128]{1,0:T(8,128)S(1)} %concatenate.30), channel_id=1, source_target_pairs={{0,16},{2,18},{4,20},{6,22},{8,24},{10,26},{12,28},{14,30},{16,0},... | collective-permute-start | bytes 24584 | tf_op jit(solution)/shard_map/ppermute | solution.py:31
  63.6 26.5 %collective-permute-start.8 = (bf16[256,512]{1,0:T(8,128)(2,1)}, bf16[256,512]{1,0:T(8,128)(2,1)S(1)}, u32[]{:S(2)}, u32[]{:S(2)}) collective-permute-start(bf16[256,512]{1,0:T(8,128)(2,1)} %get-tuple-element.31), channel_id=1, source_target_pairs={{0,2},{2,0},{4,6},{6,4},{8,10},{10,8},{12,14},{14,12},{16,18},{18,... | collective-permute-start | bytes 786440 | tf_op jit(solution)/shard_map/ppermute | solution.py:31
  68.2 19.2 %collective-permute-start.15 = (bf16[256,512]{1,0:T(8,128)(2,1)S(1)}, bf16[256,512]{1,0:T(8,128)(2,1)S(1)}, u32[]{:S(2)}, u32[]{:S(2)}) collective-permute-start(bf16[256,512]{1,0:T(8,128)(2,1)S(1)} %copy-done.18), channel_id=1, source_target_pairs={{0,16},{2,18},{4,20},{6,22},{8,24},{10,26},{12,28},{14,30},{16,0},... | collective-permute-start | bytes 786440 | tf_op jit(solution)/shard_map/ppermute | solution.py:31
  68.2 9.9 %copy-start.8 = (bf16[256,512]{1,0:T(8,128)(2,1)}, bf16[256,512]{1,0:T(8,128)(2,1)S(1)}, u32[]{:S(2)}) copy-start(bf16[256,512]{1,0:T(8,128)(2,1)S(1)} %collective-permute-done.12.refs_1_) | copy-start | bytes 786436
  68.2 22.0 %collective-permute-start.9 = (bf16[256,512]{1,0:T(8,128)(2,1)}, bf16[256,512]{1,0:T(8,128)(2,1)S(1)}, u32[]{:S(2)}, u32[]{:S(2)}) collective-permute-start(bf16[256,512]{1,0:T(8,128)(2,1)} %get-tuple-element.32), channel_id=1, source_target_pairs={{0,4},{2,6},{4,0},{6,2},{8,12},{10,14},{12,8},{14,10},{16,20},{18,... | collective-permute-start | bytes 786440 | tf_op jit(solution)/shard_map/ppermute | solution.py:31
  68.8 9.3 %copy-start.9 = (bf16[256,512]{1,0:T(8,128)(2,1)}, bf16[256,512]{1,0:T(8,128)(2,1)S(1)}, u32[]{:S(2)}) copy-start(bf16[256,512]{1,0:T(8,128)(2,1)S(1)} %collective-permute-done.13.refs_2_) | copy-start | bytes 786436
  68.8 21.4 %collective-permute-start.10 = (bf16[256,512]{1,0:T(8,128)(2,1)}, bf16[256,512]{1,0:T(8,128)(2,1)S(1)}, u32[]{:S(2)}, u32[]{:S(2)}) collective-permute-start(bf16[256,512]{1,0:T(8,128)(2,1)} %get-tuple-element.33), channel_id=1, source_target_pairs={{0,8},{2,10},{4,12},{6,14},{8,0},{10,2},{12,4},{14,6},{16,24},{18,... | collective-permute-start | bytes 786440 | tf_op jit(solution)/shard_map/ppermute | solution.py:31
  70.8 16.5 %copy-start.10 = (bf16[256,512]{1,0:T(8,128)(2,1)}, bf16[256,512]{1,0:T(8,128)(2,1)S(1)}, u32[]{:S(2)}) copy-start(bf16[256,512]{1,0:T(8,128)(2,1)S(1)} %collective-permute-done.14.refs_3_) | copy-start | bytes 786436
  70.8 20.9 %collective-permute-start.11 = (bf16[256,512]{1,0:T(8,128)(2,1)}, bf16[256,512]{1,0:T(8,128)(2,1)S(1)}, u32[]{:S(2)}, u32[]{:S(2)}) collective-permute-start(bf16[256,512]{1,0:T(8,128)(2,1)} %get-tuple-element.34), channel_id=1, source_target_pairs={{0,16},{2,18},{4,20},{6,22},{8,24},{10,26},{12,28},{14,30},{16,0},... | collective-permute-start | bytes 786440 | tf_op jit(solution)/shard_map/ppermute | solution.py:31
  90.2 1.6 %copy-start.12 = (bf16[256,512]{1,0:T(8,128)(2,1)}, bf16[256,512]{1,0:T(8,128)(2,1)S(1)}, u32[]{:S(2)}) copy-start(bf16[256,512]{1,0:T(8,128)(2,1)S(1)} %collective-permute-done.8.refs_1_) | copy-start | bytes 786436
  90.2 1.5 %copy-start.13 = (bf16[256,512]{1,0:T(8,128)(2,1)}, bf16[256,512]{1,0:T(8,128)(2,1)S(1)}, u32[]{:S(2)}) copy-start(bf16[256,512]{1,0:T(8,128)(2,1)S(1)} %collective-permute-done.9.refs_2_) | copy-start | bytes 786436
  (11 other events, 8.9 us)

commit v2 on v1

v2 whole, which is shorter than its diff:
```python
import functools

import jax
import jax.numpy as jnp
from jax import lax
from jax.experimental import pallas as pl
from jax.experimental.pallas import tpu as pltpu
from jax.sharding import PartitionSpec as P

H = 16
DH = 64
NB = 64
BLK = 128
HALVES = 2
INFO = 8
LANES = 128
PAIR_LANES = 2 * DH
BUCKET_LANE = 112
MASKED = -1e30
UNROLL = 4
VMEM_LIMIT = 24 * 2**20
FLOPS = 2 * 10**10

F32 = jnp.float32
BF16 = jnp.bfloat16


def contract(a, b, dim_a, dim_b):
    return lax.dot_general(a, b, (((dim_a,), (dim_b,)), ((), ())), preferred_element_type=F32)


def from_partner(value, axis, mask):
    pairs = [(source, source ^ mask) for source in range(lax.axis_size(axis))]
    return lax.ppermute(value, axis, pairs)


def lane_iota(shape):
    return lax.broadcasted_iota(jnp.int32, shape, len(shape) - 1)


def row_iota(shape):
    return lax.broadcasted_iota(jnp.int32, shape, len(shape) - 2)


def split_pair(pair, low):
    zero = jnp.zeros_like(pair)
    return jnp.concatenate([jnp.where(low, pair, zero), jnp.where(low, zero, pair)], axis=0)


def attention_body(near_count, far_count, half, *refs):
    section_count = 1 + near_count + far_count
    first = half == 0
    refs = list(refs)

    def take(count):
        taken, refs[:] = refs[:count], refs[count:]
        return taken

    mask_ref, bucket_ref, seg_ref, table_ref, q_ref, do_ref, k_ref, v_ref = take(8)
    near_refs = take(near_count)
    far_refs = take(far_count)
    if not first:
        masks, biases, pay_in_ref = take(3)
        earlier = take(2 + near_count)
    out_ref, dq_ref = take(2)
    near_out_refs = take(near_count)
    own_ref, *far_out_refs, pay_ref = take(2 + far_count)
    if first:
        masks, biases = take(2)
    half_features = far_refs[0].shape[1]
    half_heads = half_features // DH

    if first:
        own_bucket = bucket_ref[0]
        seg_rows = seg_ref[...].astype(F32)
        in_row = row_iota((H, NB, LANES)) == own_bucket
        pay = jnp.zeros((1, LANES), F32)
        for s in range(section_count):
            if s == 0:
                seg_cols = seg_rows
                bucket = jnp.full((1, LANES), own_bucket, jnp.int32).astype(F32)
                shut = 0.0
            else:
                source = near_refs[s - 1] if s <= near_count else far_refs[s - 1 - near_count]
                info = source[2 * BLK : 2 * BLK + INFO, 0:LANES].astype(F32)
                seg_cols = info[0:1]
                bucket = info[1:2]
                shut = jnp.where(mask_ref[s] != 0, 0.0, MASKED)
            cols = jnp.broadcast_to(seg_cols, (BLK, BLK)).T
            masks[s * BLK : (s + 1) * BLK, :] = jnp.where(
                cols == seg_rows, jnp.full((BLK, BLK), shut, F32), MASKED
            )
            hot = (row_iota((NB, LANES)).astype(F32) == bucket).astype(BF16)
            picked = contract(table_ref[...], hot, 1, 0).reshape(H, NB, LANES)
            biases[s] = jnp.sum(jnp.where(in_row, picked, 0.0), axis=1)
            pay = jnp.where(lane_iota(pay.shape) == BUCKET_LANE + s, bucket, pay)
        pay_ref[...] = pay
    else:
        pay_ref[...] = pay_in_ref[...]
        for source, target in zip(earlier, [out_ref, dq_ref, *near_out_refs]):
            target[:, 0 : half * half_features] = source[...]

    low = lane_iota((BLK, PAIR_LANES)) < DH
    lanes = lane_iota((1, LANES))

    def one_pair(pair, carry):
        here = pl.ds(pl.multiple_of(pair * PAIR_LANES, PAIR_LANES), PAIR_LANES)
        there = pl.ds(
            pl.multiple_of(half * half_features + pair * PAIR_LANES, PAIR_LANES), PAIR_LANES
        )
        mine = here if first else there
        head = half * half_heads + 2 * pair
        q_stack = split_pair(q_ref[:, there] * jnp.asarray(0.125, BF16), low)
        grad_stack = split_pair(do_ref[:, there], low)
        key_rows = jnp.concatenate(
            [k_ref[:, there]]
            + [r[0:BLK, there] for r in near_refs]
            + [r[0:BLK, here] for r in far_refs],
            axis=0,
        )
        value_rows = jnp.concatenate(
            [v_ref[:, there]]
            + [r[BLK : 2 * BLK, there] for r in near_refs]
            + [r[BLK : 2 * BLK, here] for r in far_refs],
            axis=0,
        )
        raw = contract(key_rows, q_stack, 1, 1)
        dprob = contract(value_rows, grad_stack, 1, 1)
        scores = []
        shifts = []
        top = None
        for s in range(section_count):
            block = slice(s * BLK, (s + 1) * BLK)
            mask = masks[block, :]
            score = raw[block] + jnp.concatenate([mask, mask], axis=1)
            bias = jnp.concatenate(
                [biases[s, pl.ds(head, 1), :], biases[s, pl.ds(head + 1, 1), :]], axis=1
            )
            best = jnp.max(score, axis=0, keepdims=True) + bias
            top = best if top is None else jnp.maximum(top, best)
            scores.append(score)
            shifts.append(bias)
        weights = [jnp.exp(scores[s] - (top - shifts[s])) for s in range(section_count)]
        total = sum(jnp.sum(weight, axis=0, keepdims=True) for weight in weights)
        inverse = 1.0 / total
        probs = [weight * inverse for weight in weights]
        probs_low = jnp.concatenate([prob.astype(BF16) for prob in probs], axis=0)
        out_stack = contract(probs_low, value_rows, 0, 0)
        pulls = [probs[s] * dprob[s * BLK : (s + 1) * BLK] for s in range(section_count)]
        delta = sum(jnp.sum(pull, axis=0, keepdims=True) for pull in pulls)
        dscores = [pulls[s] - probs[s] * delta for s in range(section_count)]
        dscore_low = jnp.concatenate([dscore.astype(BF16) for dscore in dscores], axis=0)
        value_terms = contract(probs_low, grad_stack, 1, 0)
        key_terms = contract(dscore_low, q_stack, 1, 0)
        dq_stack = contract(dscore_low, key_rows, 0, 0)
        out_ref[:, mine] = jnp.where(low, out_stack[:BLK], out_stack[BLK:]).astype(BF16)
        dq_ref[:, mine] = (jnp.where(low, dq_stack[:BLK], dq_stack[BLK:]) * 0.125).astype(BF16)
        pay = pay_ref[...]
        for s in range(section_count):
            sums = jnp.sum(dscores[s], axis=0, keepdims=True)
            even = jnp.sum(sums[:, :BLK], axis=1, keepdims=True)
            odd = jnp.sum(sums[:, BLK:], axis=1, keepdims=True)
            pay = jnp.where(lanes == s * H + head, even, pay)
            pay = jnp.where(lanes == s * H + head + 1, odd, pay)
            key_term = key_terms[s * BLK : (s + 1) * BLK]
            value_term = value_terms[s * BLK : (s + 1) * BLK]
            if s == 0:
                own_ref[0:BLK, here] = key_term
                own_ref[BLK : 2 * BLK, here] = value_term
            elif s <= near_count:
                near_out_refs[s - 1][0:BLK, mine] = key_term.astype(BF16)
                near_out_refs[s - 1][BLK : 2 * BLK, mine] = value_term.astype(BF16)
            else:
                far_out_refs[s - 1 - near_count][0:BLK, here] = key_term.astype(BF16)
                far_out_refs[s - 1 - near_count][BLK : 2 * BLK, here] = value_term.astype(BF16)
        pay_ref[...] = pay
        return carry

    lax.fori_loop(0, half_features // PAIR_LANES, one_pair, 0, unroll=UNROLL)


def attention_half(half, scalars, table_rows, rows, near, far, previous):
    near_count, far_count = len(near), len(far)
    section_count = 1 + near_count + far_count
    row_count, feature_count = rows[0].shape
    half_features = feature_count // HALVES
    half_heads = half_features // DH
    smem = pl.BlockSpec(memory_space=pltpu.SMEM)
    vmem = pl.BlockSpec(memory_space=pltpu.VMEM)
    operands = [*scalars, table_rows, *rows, *near, *far]
    in_specs = [smem, smem] + [vmem] * (len(operands) - 2)
    covered = (half + 1) * half_features
    packed = jax.ShapeDtypeStruct((2 * row_count, half_features), BF16)
    out_shape = [
        *[jax.ShapeDtypeStruct((row_count, covered), BF16)] * 2,
        *[jax.ShapeDtypeStruct((2 * row_count, covered), BF16)] * near_count,
        jax.ShapeDtypeStruct((2 * row_count, half_features), F32),
        *[packed] * far_count,
        jax.ShapeDtypeStruct((1, LANES), F32),
    ]
    if previous is None:
        out_shape += [
            jax.ShapeDtypeStruct((section_count * BLK, BLK), F32),
            jax.ShapeDtypeStruct((section_count, H, LANES), F32),
        ]
    else:
        operands += [*previous[-2:], previous[-3], *previous[: 2 + near_count]]
        in_specs += [vmem] * (5 + near_count)
    return pl.pallas_call(
        functools.partial(attention_body, near_count, far_count, half),
        in_specs=in_specs,
        out_specs=[vmem] * len(out_shape),
        out_shape=out_shape,
        compiler_params=pltpu.CompilerParams(vmem_limit_bytes=VMEM_LIMIT),
        cost_estimate=pl.CostEstimate(
            flops=FLOPS, bytes_accessed=4 * 2**20, transcendentals=section_count * half_heads * BLK * BLK
        ),
        name="attention",
    )(*operands)


def finish_body(near_count, far_count, *refs):
    own_refs = refs[:HALVES]
    near_refs = refs[HALVES : HALVES + near_count]
    far_refs = refs[HALVES + near_count : -2]
    key_ref, value_ref = refs[-2:]
    half_features = far_refs[0].shape[1]
    for half in range(HALVES):
        window = slice(half * half_features, (half + 1) * half_features)
        for out_ref, block in ((key_ref, slice(0, BLK)), (value_ref, slice(BLK, 2 * BLK))):
            total = own_refs[half][block, :]
            for ref in near_refs:
                total = total + ref[block, window].astype(F32)
            for ref in far_refs[half * far_count : (half + 1) * far_count]:
                total = total + ref[block, :].astype(F32)
            out_ref[:, window] = total.astype(BF16)


def finish(own, near, far):
    row_count = own[0].shape[0] // 2
    vmem = pl.BlockSpec(memory_space=pltpu.VMEM)
    out = jax.ShapeDtypeStruct((row_count, HALVES * own[0].shape[1]), BF16)
    return pl.pallas_call(
        functools.partial(finish_body, len(near), len(far) // HALVES),
        in_specs=[vmem] * (HALVES + len(near) + len(far)),
        out_specs=[vmem, vmem],
        out_shape=[out, out],
        compiler_params=pltpu.CompilerParams(vmem_limit_bytes=VMEM_LIMIT),
        cost_estimate=pl.CostEstimate(flops=2**19, bytes_accessed=2**21, transcendentals=0),
        name="finish",
    )(*own, *near, *far)


def table_body(section_count, *refs):
    table_ref = refs[-1]
    gathered = jnp.concatenate([ref[...] for ref in refs[:-1]], axis=0)
    count = gathered.shape[0]
    lanes = lane_iota((count, PAIR_LANES))
    column = jnp.where(lanes < NB, lanes, lanes - NB).astype(F32)
    bucket = gathered[:, BUCKET_LANE : BUCKET_LANE + 1]
    row_hot = (lane_iota((count, NB)).astype(F32) == bucket).astype(F32)
    rows = jnp.concatenate([row_hot] * section_count, axis=0)
    hots = [
        column == gathered[:, BUCKET_LANE + s : BUCKET_LANE + s + 1] for s in range(section_count)
    ]
    for pair in range(H // 2):
        parts = []
        for s in range(section_count):
            lane = s * H + 2 * pair
            value = jnp.where(lanes < NB, gathered[:, lane : lane + 1], gathered[:, lane + 1 : lane + 2])
            parts.append(jnp.where(hots[s], value, 0.0))
        tile = lax.dot_general(
            rows,
            jnp.concatenate(parts, axis=0),
            (((0,), (0,)), ((), ())),
            preferred_element_type=F32,
            precision=lax.Precision.HIGHEST,
        )
        table_ref[2 * pair] = tile[:, :NB]
        table_ref[2 * pair + 1] = tile[:, NB:]


def table_of(blocks, section_count):
    vmem = pl.BlockSpec(memory_space=pltpu.VMEM)
    return pl.pallas_call(
        functools.partial(table_body, section_count),
        in_specs=[vmem] * len(blocks),
        out_specs=vmem,
        out_shape=jax.ShapeDtypeStruct((H, NB, NB), F32),
        compiler_params=pltpu.CompilerParams(vmem_limit_bytes=VMEM_LIMIT),
        name="table",
    )(*blocks)


def pack_body(bucket_ref, seg_ref, key_ref, value_ref, whole_ref, first_ref, second_ref):
    half_features = first_ref.shape[1]
    top = row_iota((INFO, LANES)) == 0
    bucket = jnp.full((INFO, LANES), bucket_ref[0], jnp.int32)
    info = jnp.where(top, seg_ref[...], bucket).astype(F32).astype(BF16)
    for block, source in ((slice(0, BLK), key_ref), (slice(BLK, 2 * BLK), value_ref)):
        whole_ref[block, :] = source[...]
        first_ref[block, :] = source[:, :half_features]
        second_ref[block, :] = source[:, half_features:]
    for target in (whole_ref, first_ref):
        for start in range(0, target.shape[1], LANES):
            target[2 * BLK : 2 * BLK + INFO, start : start + LANES] = info


def pack(bucket, seg, keys, values):
    row_count, feature_count = keys.shape
    half_features = feature_count // HALVES
    vmem = pl.BlockSpec(memory_space=pltpu.VMEM)
    return pl.pallas_call(
        pack_body,
        in_specs=[pl.BlockSpec(memory_space=pltpu.SMEM), vmem, vmem, vmem],
        out_specs=[vmem] * 3,
        out_shape=[
            jax.ShapeDtypeStruct((2 * row_count + INFO, feature_count), BF16),
            jax.ShapeDtypeStruct((2 * row_count + INFO, half_features), BF16),
            jax.ShapeDtypeStruct((2 * row_count, half_features), BF16),
        ],
        compiler_params=pltpu.CompilerParams(vmem_limit_bytes=VMEM_LIMIT),
        name="pack",
    )(bucket, seg, keys, values)


def after(value, *earlier):
    return lax.optimization_barrier((value, *earlier))[0]


def double(block, axis, mask):
    return jnp.concatenate([block, from_partner(block, axis, mask)], axis=0)


def local(queries, keys, values, d_out, segment_ids, block_bucket, block_mask, bias_table):
    level_count = lax.axis_size("seq").bit_length() - 1
    rows = [queries[0], d_out[0], keys[0], values[0]]
    scalars = (block_mask.reshape(-1), block_bucket.reshape(-1), segment_ids)
    table_rows = bias_table.reshape(H * NB, NB)
    far_levels = list(range(1, level_count))
    last = far_levels[-2:]

    def send(value, level):
        return from_partner(value, "seq", 1 << level)

    whole, first, second = pack(scalars[1], segment_ids, rows[2], rows[3])
    far = [{}, {}]
    for level in reversed(far_levels):
        far[0][level] = send(first, level)
    near = send(whole, 0)
    for level in reversed(far_levels):
        far[1][level] = send(after(second, near if level in last else far[0][level]), level)
    near_list = [near]
    near_count = len(near_list)

    one = attention_half(
        0, scalars, table_rows, rows, near_list, [far[0][level] for level in far_levels], None
    )
    terms = one[3 + near_count : 3 + level_count]
    back_one = {level: send(terms[level - 1], level) for level in reversed(far_levels)}
    early = [back_one[level] for level in far_levels if level not in last]
    late = [back_one[level] for level in last]
    two = attention_half(
        1, scalars, table_rows, rows, near_list, [far[1][level] for level in far_levels], one
    )
    terms = two[3 + near_count : 3 + level_count]
    back_two = {level: send(terms[level - 1], level) for level in reversed(last)}
    block = double(after(two[3 + level_count], *early), "seq", 1)
    for level in far_levels:
        if level not in last:
            back_two[level] = send(after(terms[level - 1], *late), level)
    near_back = send(after(two[2], *late), 0)
    block = after(block, *late)
    mask = 1
    while mask < lax.axis_size("dp"):
        block = double(block, "dp", mask)
        mask *= 2
    for level in far_levels:
        if level not in last:
            block = double(block, "seq", 1 << level)
    block = after(block, near_back, *[back_two[level] for level in far_levels if level not in last])
    blocks = [block]
    for mask in (1 << last[0], 1 << last[1], (1 << last[0]) | (1 << last[1])):
        blocks.append(from_partner(block, "seq", mask))
    table_total = table_of(blocks, level_count + 1)
    d_keys, d_values = finish(
        [one[2 + near_count], two[2 + near_count]],
        [near_back],
        [back[level] for back in (back_one, back_two) for level in far_levels],
    )
    return (two[0][None], two[1][None], d_keys[None], d_values[None], table_total)


def solution(mesh):
    rows = P("dp", "seq", None)
    in_specs = (
        rows,
        rows,
        rows,
        rows,
        P("dp", "seq"),
        P("dp", "seq"),
        P("dp", "seq", None, None),
        P(),
    )
    return jax.shard_map(
        local, mesh=mesh, in_specs=in_specs, out_specs=(rows,) * 4 + (P(),), check_vma=False
    )
```

time: 94.9 us -> 65.3 us (0.69)
  waiting for transfers between devices: 31.9 us -> 17.3 us
  Pallas kernels: 27 us -> 12.6 us
  local copies, waits for them, and re-layouts: 7.39 us -> 4.15 us
  starting transfers between devices: 26.6 us -> 29.7 us
    ppermute x21 -> x20, waiting for transfers between devices: 31.9 us -> 17.3 us  [from_partner(): return lax.ppermute(value, axis, pairs)]
    pallas_call x5, Pallas kernels: 27 us -> 12.6 us  [the longest x2 9.56 us: attention_half(): pl.pallas_call(functools.partial(attention_body, near_count, far_count, h...]
    ppermute x21 -> x20, starting transfers between devices: 26.6 us -> 29.7 us  [from_partner(): return lax.ppermute(value, axis, pairs)]
    concatenate x3 -> x0, local copies, waits for them, and re-layouts: 1.9 us -> none  [the longest x2 1.82 us: table_of(): jnp.concatenate([gathered, from_partner(gathered, axis, mask)], axis=0)]
    slice x1 -> x0, local copies, waits for them, and re-layouts: 1.13 us -> none  [local(): pieces = [own_keys[:, window], own_values[:, window]]]
    unnamed x46 -> x16, local copies, waits for them, and re-layouts: 4.36 us -> 4.15 us
  transfers between devices with their start and end apart: 21 -> 20, of which waited for: 7 -> 7; matrix products, arithmetic and copies ran while one was open for 2% -> 0% of each run, Pallas kernels for 16% -> 16%
where the time goes in v2:
time: 65.3 us; the launch traced here: 65.1 us
  starting transfers between devices  29.7 us (45%)
  waiting for transfers between devices  17.3 us (26%)
  Pallas kernels  12.6 us (19%)
  local copies, waits for them, and re-layouts  4.15 us (6%)
  between operations  1.36 us (2%)
    ppermute x20, starting transfers between devices, from_partner(): return lax.ppermute(value, axis, pairs)  29.7 us
    ppermute x20, waiting for transfers between devices, from_partner(): return lax.ppermute(value, axis, pairs)  17.3 us
    pallas_call x2, Pallas kernels, attention_half(): pl.pallas_call(functools.partial(attention_body, near_count, far_count, h...  9.56 us
    unnamed x16, local copies, waits for them, and re-layouts  4.15 us
    pallas_call x1, Pallas kernels, table_of(): pl.pallas_call(functools.partial(table_body, section_count), in_specs=[vm...  1.91 us
  transfers between devices with their start and end apart: 20, of which 7 were waited for; matrix products, arithmetic and copies ran while one was open for 0% of the time, Pallas kernels for 16%

profile of v2, /device:TPU:0, one launch (start us, length us, event | category | flops | bytes accessed | tf_op | source)
XLA Modules:
  0.0 65.1 jit_solution(11220858103044929686)
XLA Ops:
  1.3 0.6 copy-done.2
  1.9 0.9 %copy-done = bf16[1,128,1024]{2,1,0:T(8,128)(2,1)S(1)} copy-done((bf16[1,128,1024]{2,1,0:T(8,128)(2,1)S(1)}, bf16[1,128,1024]{2,1,0:T(8,128)(2,1)}, u32[]{:S(2)}) %copy-start) | copy-done | bytes 262168
  2.9 0.9 %copy-done.1 = bf16[1,128,1024]{2,1,0:T(8,128)(2,1)S(1)} copy-done((bf16[1,128,1024]{2,1,0:T(8,128)(2,1)S(1)}, bf16[1,128,1024]{2,1,0:T(8,128)(2,1)}, u32[]{:S(2)}) %copy-start.1) | copy-done | bytes 262168
  3.9 0.5 collective-permute-start
  4.4 2.6 %collective-permute-start.1 = (bf16[264,512]{1,0:T(8,128)(2,1)S(1)}, bf16[264,512]{1,0:T(8,128)(2,1)S(1)}, u32[]{:S(2)}, u32[]{:S(2)}) collective-permute-start(bf16[264,512]{1,0:T(8,128)(2,1)S(1)} %get-tuple-element.37), channel_id=1, source_target_pairs={{0,4},{2,6},{4,0},{6,2},{8,12},{10,14},{12,8},{14,10},{16,20},{18,... | collective-permute-start | bytes 811016 | tf_op jit(solution)/shard_map/ppermute | solution.py:34
  7.0 2.6 %collective-permute-start.6 = (bf16[264,512]{1,0:T(8,128)(2,1)S(1)}, bf16[264,512]{1,0:T(8,128)(2,1)S(1)}, u32[]{:S(2)}, u32[]{:S(2)}) collective-permute-start(bf16[264,512]{1,0:T(8,128)(2,1)S(1)} %get-tuple-element.37), channel_id=1, source_target_pairs={{0,16},{2,18},{4,20},{6,22},{8,24},{10,26},{12,28},{14,30},{16,0},... | collective-permute-start | bytes 811016 | tf_op jit(solution)/shard_map/ppermute | solution.py:34
  9.6 1.6 %collective-permute-start.5 = (bf16[264,512]{1,0:T(8,128)(2,1)S(1)}, bf16[264,512]{1,0:T(8,128)(2,1)S(1)}, u32[]{:S(2)}, u32[]{:S(2)}) collective-permute-start(bf16[264,512]{1,0:T(8,128)(2,1)S(1)} %get-tuple-element.37), channel_id=1, source_target_pairs={{0,8},{2,10},{4,12},{6,14},{8,0},{10,2},{12,4},{14,6},{16,24},{18,... | collective-permute-start | bytes 811016 | tf_op jit(solution)/shard_map/ppermute | solution.py:34
  11.2 2.9 %collective-permute-done.1.refs_9_ = bf16[264,512]{1,0:T(8,128)(2,1)S(1)} collective-permute-done((bf16[264,512]{1,0:T(8,128)(2,1)S(1)}, bf16[264,512]{1,0:T(8,128)(2,1)S(1)}, u32[]{:S(2)}, u32[]{:S(2)}) %collective-permute-start.1) | collective-permute-done | bytes 270368 | tf_op jit(solution)/shard_map/ppermute | solution.py:34
  14.1 1.8 %collective-permute-start.2 = (bf16[256,512]{1,0:T(8,128)(2,1)S(1)}, bf16[256,512]{1,0:T(8,128)(2,1)S(1)}, u32[]{:S(2)}, u32[]{:S(2)}) collective-permute-start(bf16[256,512]{1,0:T(8,128)(2,1)S(1)} %get-tuple-element.39), channel_id=1, source_target_pairs={{0,4},{2,6},{4,0},{6,2},{8,12},{10,14},{12,8},{14,10},{16,20},{18,... | collective-permute-start | bytes 786440 | tf_op jit(solution)/shard_map/ppermute | solution.py:34
  15.9 2.6 %collective-permute-start.4 = (bf16[256,512]{1,0:T(8,128)(2,1)S(1)}, bf16[256,512]{1,0:T(8,128)(2,1)S(1)}, u32[]{:S(2)}, u32[]{:S(2)}) collective-permute-start(bf16[256,512]{1,0:T(8,128)(2,1)S(1)} %get-tuple-element.39), channel_id=1, source_target_pairs={{0,16},{2,18},{4,20},{6,22},{8,24},{10,26},{12,28},{14,30},{16,0},... | collective-permute-start | bytes 786440 | tf_op jit(solution)/shard_map/ppermute | solution.py:34
  18.5 1.6 %collective-permute-start.3 = (bf16[256,512]{1,0:T(8,128)(2,1)S(1)}, bf16[256,512]{1,0:T(8,128)(2,1)S(1)}, u32[]{:S(2)}, u32[]{:S(2)}) collective-permute-start(bf16[256,512]{1,0:T(8,128)(2,1)S(1)} %get-tuple-element.39), channel_id=1, source_target_pairs={{0,8},{2,10},{4,12},{6,14},{8,0},{10,2},{12,4},{14,6},{16,24},{18,... | collective-permute-start | bytes 786440 | tf_op jit(solution)/shard_map/ppermute | solution.py:34
  20.0 3.6 %collective-permute-done.6.refs_11_ = bf16[264,512]{1,0:T(8,128)(2,1)S(1)} collective-permute-done((bf16[264,512]{1,0:T(8,128)(2,1)S(1)}, bf16[264,512]{1,0:T(8,128)(2,1)S(1)}, u32[]{:S(2)}, u32[]{:S(2)}) %collective-permute-start.6) | collective-permute-done | bytes 270368 | tf_op jit(solution)/shard_map/ppermute | solution.py:34
  23.6 0.6 copy-done.7
  24.3 0.9 %copy-done.5 = bf16[1,128,1024]{2,1,0:T(8,128)(2,1)S(1)} copy-done((bf16[1,128,1024]{2,1,0:T(8,128)(2,1)S(1)}, bf16[1,128,1024]{2,1,0:T(8,128)(2,1)}, u32[]{:S(2)}) %copy-start.5) | copy-done | bytes 262168
  25.2 4.5 %attention.2 = (bf16[128,512]{1,0:T(8,128)(2,1)S(1)}, bf16[128,512]{1,0:T(8,128)(2,1)S(1)}, bf16[256,512]{1,0:T(8,128)(2,1)S(1)}, f32[256,512]{1,0:T(8,128)S(1)}...) custom-call(s32[5]{0:T(128)S(1)} %bitcast.26, ...), custom_call_target="tpu_custom_call" | custom-call | flops 20000000000 | bytes 4194304 | tf_op jit(solution)/shard_map/attention/pallas_call | solution.py:209
  29.7 1.2 %collective-permute-start.7 = (bf16[256,512]{1,0:T(8,128)(2,1)S(1)}, bf16[256,512]{1,0:T(8,128)(2,1)S(1)}, u32[]{:S(2)}, u32[]{:S(2)}) collective-permute-start(bf16[256,512]{1,0:T(8,128)(2,1)S(1)} %get-tuple-element.51), channel_id=1, source_target_pairs={{0,8},{2,10},{4,12},{6,14},{8,0},{10,2},{12,4},{14,6},{16,24},{18,... | collective-permute-start | bytes 786440 | tf_op jit(solution)/shard_map/ppermute | solution.py:34
  31.0 2.5 %collective-permute-start.8 = (bf16[256,512]{1,0:T(8,128)(2,1)S(1)}, bf16[256,512]{1,0:T(8,128)(2,1)S(1)}, u32[]{:S(2)}, u32[]{:S(2)}) collective-permute-start(bf16[256,512]{1,0:T(8,128)(2,1)S(1)} %get-tuple-element.52), channel_id=1, source_target_pairs={{0,16},{2,18},{4,20},{6,22},{8,24},{10,26},{12,28},{14,30},{16,0},... | collective-permute-start | bytes 786440 | tf_op jit(solution)/shard_map/ppermute | solution.py:34
  33.4 0.5 collective-permute-start.10
  33.9 5.6 %collective-permute-done.3.refs_10_ = bf16[256,512]{1,0:T(8,128)(2,1)S(1)} collective-permute-done((bf16[256,512]{1,0:T(8,128)(2,1)S(1)}, bf16[256,512]{1,0:T(8,128)(2,1)S(1)}, u32[]{:S(2)}, u32[]{:S(2)}) %collective-permute-start.3) | collective-permute-done | bytes 262176 | tf_op jit(solution)/shard_map/ppermute | solution.py:34
  39.6 5.1 %attention.3 = (bf16[128,1024]{1,0:T(8,128)(2,1)}, bf16[128,1024]{1,0:T(8,128)(2,1)}, bf16[256,1024]{1,0:T(8,128)(2,1)S(1)}, f32[256,512]{1,0:T(8,128)S(1)}, bf1...) custom-call(s32[5]{0:T(128)S(1)} %bitcast.27, ...), custom_call_target="tpu_custom_call" | custom-call | flops 20000000000 | bytes 4194304 | tf_op jit(solution)/shard_map/attention/pallas_call | solution.py:209
  45.6 1.4 %collective-permute-start.12 = (bf16[256,512]{1,0:T(8,128)(2,1)S(1)}, bf16[256,512]{1,0:T(8,128)(2,1)S(1)}, u32[]{:S(2)}, u32[]{:S(2)}) collective-permute-start(bf16[256,512]{1,0:T(8,128)(2,1)S(1)} %get-tuple-element.57), channel_id=1, source_target_pairs={{0,8},{2,10},{4,12},{6,14},{8,0},{10,2},{12,4},{14,6},{16,24},{18,... | collective-permute-start | bytes 786440 | tf_op jit(solution)/shard_map/ppermute | solution.py:34
  46.9 2.4 %collective-permute-start.13 = (bf16[256,512]{1,0:T(8,128)(2,1)S(1)}, bf16[256,512]{1,0:T(8,128)(2,1)S(1)}, u32[]{:S(2)}, u32[]{:S(2)}) collective-permute-start(bf16[256,512]{1,0:T(8,128)(2,1)S(1)} %get-tuple-element.58), channel_id=1, source_target_pairs={{0,16},{2,18},{4,20},{6,22},{8,24},{10,26},{12,28},{14,30},{16,0},... | collective-permute-start | bytes 786440 | tf_op jit(solution)/shard_map/ppermute | solution.py:34
  49.9 1.6 %collective-permute-start.15 = (f32[2,128]{1,0:T(2,128)S(1)}, f32[2,128]{1,0:T(2,128)S(1)}, u32[]{:S(2)}, u32[]{:S(2)}) collective-permute-start(f32[2,128]{1,0:T(2,128)S(1)} %pad_maximum_fusion.2), channel_id=1, source_target_pairs={{0,1},{1,0},{2,3},{3,2},{4,5},{5,4},{6,7},{7,6},{8,9},{9,8},{10,11... | collective-permute-start | bytes 3080 | tf_op jit(solution)/shard_map/ppermute | solution.py:34
  51.4 2.1 %collective-permute-done.15 = f32[2,128]{1,0:T(2,128)S(1)} collective-permute-done((f32[2,128]{1,0:T(2,128)S(1)}, f32[2,128]{1,0:T(2,128)S(1)}, u32[]{:S(2)}, u32[]{:S(2)}) %collective-permute-start.15) | collective-permute-done | bytes 1056 | tf_op jit(solution)/shard_map/ppermute | solution.py:34
  53.5 1.5 %collective-permute-start.16 = (f32[4,128]{1,0:T(4,128)S(1)}, f32[4,128]{1,0:T(4,128)S(1)}, u32[]{:S(2)}, u32[]{:S(2)}) collective-permute-start(f32[4,128]{1,0:T(4,128)S(1)} %pad_maximum_fusion.1), channel_id=1, source_target_pairs={{0,4},{2,6},{4,0},{6,2},{8,12},{10,14},{12,8},{14,10},{16,20},{18,... | collective-permute-start | bytes 6152 | tf_op jit(solution)/shard_map/ppermute | solution.py:34
  55.0 2.1 %collective-permute-done.16 = f32[4,128]{1,0:T(4,128)S(1)} collective-permute-done((f32[4,128]{1,0:T(4,128)S(1)}, f32[4,128]{1,0:T(4,128)S(1)}, u32[]{:S(2)}, u32[]{:S(2)}) %collective-permute-start.16) | collective-permute-done | bytes 2080 | tf_op jit(solution)/shard_map/ppermute | solution.py:34
  57.2 0.7 %collective-permute-start.19 = (f32[8,128]{1,0:T(8,128)S(1)}, f32[8,128]{1,0:T(8,128)S(1)}, u32[]{:S(2)}, u32[]{:S(2)}) collective-permute-start(f32[8,128]{1,0:T(8,128)S(1)} %pad_maximum_fusion.refs_0_), channel_id=1, source_target_pairs={{0,24},{2,26},{4,28},{6,30},{8,16},{10,18},{12,20},{14,22},{16,8},... | collective-permute-start | bytes 12296 | tf_op jit(solution)/shard_map/ppermute | solution.py:34
  57.8 1.5 %collective-permute-start.18 = (f32[8,128]{1,0:T(8,128)S(1)}, f32[8,128]{1,0:T(8,128)S(1)}, u32[]{:S(2)}, u32[]{:S(2)}) collective-permute-start(f32[8,128]{1,0:T(8,128)S(1)} %pad_maximum_fusion.refs_0_), channel_id=1, source_target_pairs={{0,16},{2,18},{4,20},{6,22},{8,24},{10,26},{12,28},{14,30},{16,0},... | collective-permute-start | bytes 12296 | tf_op jit(solution)/shard_map/ppermute | solution.py:34
  59.3 2.3 %collective-permute-start.17 = (f32[8,128]{1,0:T(8,128)S(1)}, f32[8,128]{1,0:T(8,128)S(1)}, u32[]{:S(2)}, u32[]{:S(2)}) collective-permute-start(f32[8,128]{1,0:T(8,128)S(1)} %pad_maximum_fusion.refs_0_), channel_id=1, source_target_pairs={{0,8},{2,10},{4,12},{6,14},{8,0},{10,2},{12,4},{14,6},{16,24},{18,... | collective-permute-start | bytes 12296 | tf_op jit(solution)/shard_map/ppermute | solution.py:34
  61.6 1.0 %finish.1 = (bf16[128,1024]{1,0:T(8,128)(2,1)}, bf16[128,1024]{1,0:T(8,128)(2,1)}) custom-call(f32[256,512]{1,0:T(8,128)S(1)} %get-tuple-element.48.refs_0_, f32[256,512]{1,0:T(8,128)S(1)} %get-tuple-element.49.refs_1_, bf16[256,1024]{1,0:T(8,128)(2,1)S(1)} %collective-permute-done.9.refs_2_, bf16[256,512]{1,0:T(8,128)(2,1)S(1)} %collective-permute-done.10.refs_3_, ...), custom_call_target="tpu_custom_call" | custom-call | flops 524288 | bytes 2097152 | tf_op jit(solution)/shard_map/finish/pallas_call | solution.py:243
  62.7 0.5 collective-permute-done.17.refs_1_
  63.2 1.9 %table.1 = f32[16,64,64]{2,1,0:T(8,128)} custom-call(f32[8,128]{1,0:T(8,128)S(1)} %pad_maximum_fusion.refs_0_, f32[8,128]{1,0:T(8,128)S(1)} %collective-permute-done.17.refs_1_, f32[8,128]{1,0:T(8,128)S(1)} %collective-permute-done.18.refs_2_, f32[8,128]{1,0:T(8,128)S(1)} %collective-permute-done.19.refs_3_), custom_call_target="tpu_custom_call" | custom-call | tf_op jit(solution)/shard_map/table/pallas_call | solution.py:285
  (32 shorter events, 1.6 us)
Async XLA Ops:
  1.3 0.7 %copy-start.2 = (s32[1,128]{1,0:T(1,128)S(1)}, s32[1,128]{1,0:T(1,128)}, u32[]{:S(2)}) copy-start(s32[1,128]{1,0:T(1,128)} %refs_2_.3) | copy-start | bytes 1540
  1.9 0.9 %copy-start = (bf16[1,128,1024]{2,1,0:T(8,128)(2,1)S(1)}, bf16[1,128,1024]{2,1,0:T(8,128)(2,1)}, u32[]{:S(2)}) copy-start(bf16[1,128,1024]{2,1,0:T(8,128)(2,1)} %param.9) | copy-start | bytes 786436
  2.9 0.9 %copy-start.1 = (bf16[1,128,1024]{2,1,0:T(8,128)(2,1)S(1)}, bf16[1,128,1024]{2,1,0:T(8,128)(2,1)}, u32[]{:S(2)}) copy-start(bf16[1,128,1024]{2,1,0:T(8,128)(2,1)} %param.10) | copy-start | bytes 786436
  3.8 19.8 %copy-start.3 = (bf16[16,64,64]{2,1,0:T(8,128)(2,1)S(1)}, bf16[16,64,64]{2,1,0:T(8,128)(2,1)}, u32[]{:S(2)}) copy-start(bf16[16,64,64]{2,1,0:T(8,128)(2,1)} %param.15) | copy-start | bytes 393220
  3.8 19.8 %copy-start.4 = (bf16[1,128,1024]{2,1,0:T(8,128)(2,1)S(1)}, bf16[1,128,1024]{2,1,0:T(8,128)(2,1)}, u32[]{:S(2)}) copy-start(bf16[1,128,1024]{2,1,0:T(8,128)(2,1)} %param.8) | copy-start | bytes 786436
  3.9 11.9 %collective-permute-start = (bf16[264,1024]{1,0:T(8,128)(2,1)S(1)}, bf16[264,1024]{1,0:T(8,128)(2,1)S(1)}, u32[]{:S(2)}, u32[]{:S(2)}) collective-permute-start(bf16[264,1024]{1,0:T(8,128)(2,1)S(1)} %get-tuple-element.35), channel_id=1, source_target_pairs={{0,2},{2,0},{4,6},{6,4},{8,10},{10,8},{12,14},{14,12},{16,18},{18,... | collective-permute-start | bytes 1622024 | tf_op jit(solution)/shard_map/ppermute | solution.py:34
  4.4 9.7 %collective-permute-start.1 = (bf16[264,512]{1,0:T(8,128)(2,1)S(1)}, bf16[264,512]{1,0:T(8,128)(2,1)S(1)}, u32[]{:S(2)}, u32[]{:S(2)}) collective-permute-start(bf16[264,512]{1,0:T(8,128)(2,1)S(1)} %get-tuple-element.37), channel_id=1, source_target_pairs={{0,4},{2,6},{4,0},{6,2},{8,12},{10,14},{12,8},{14,10},{16,20},{18,... | collective-permute-start | bytes 811016 | tf_op jit(solution)/shard_map/ppermute | solution.py:34
  7.0 16.6 %collective-permute-start.6 = (bf16[264,512]{1,0:T(8,128)(2,1)S(1)}, bf16[264,512]{1,0:T(8,128)(2,1)S(1)}, u32[]{:S(2)}, u32[]{:S(2)}) collective-permute-start(bf16[264,512]{1,0:T(8,128)(2,1)S(1)} %get-tuple-element.37), channel_id=1, source_target_pairs={{0,16},{2,18},{4,20},{6,22},{8,24},{10,26},{12,28},{14,30},{16,0},... | collective-permute-start | bytes 811016 | tf_op jit(solution)/shard_map/ppermute | solution.py:34
  9.6 14.0 %collective-permute-start.5 = (bf16[264,512]{1,0:T(8,128)(2,1)S(1)}, bf16[264,512]{1,0:T(8,128)(2,1)S(1)}, u32[]{:S(2)}, u32[]{:S(2)}) collective-permute-start(bf16[264,512]{1,0:T(8,128)(2,1)S(1)} %get-tuple-element.37), channel_id=1, source_target_pairs={{0,8},{2,10},{4,12},{6,14},{8,0},{10,2},{12,4},{14,6},{16,24},{18,... | collective-permute-start | bytes 811016 | tf_op jit(solution)/shard_map/ppermute | solution.py:34
  14.1 19.3 %collective-permute-start.2 = (bf16[256,512]{1,0:T(8,128)(2,1)S(1)}, bf16[256,512]{1,0:T(8,128)(2,1)S(1)}, u32[]{:S(2)}, u32[]{:S(2)}) collective-permute-start(bf16[256,512]{1,0:T(8,128)(2,1)S(1)} %get-tuple-element.39), channel_id=1, source_target_pairs={{0,4},{2,6},{4,0},{6,2},{8,12},{10,14},{12,8},{14,10},{16,20},{18,... | collective-permute-start | bytes 786440 | tf_op jit(solution)/shard_map/ppermute | solution.py:34
  15.9 18.1 %collective-permute-start.4 = (bf16[256,512]{1,0:T(8,128)(2,1)S(1)}, bf16[256,512]{1,0:T(8,128)(2,1)S(1)}, u32[]{:S(2)}, u32[]{:S(2)}) collective-permute-start(bf16[256,512]{1,0:T(8,128)(2,1)S(1)} %get-tuple-element.39), channel_id=1, source_target_pairs={{0,16},{2,18},{4,20},{6,22},{8,24},{10,26},{12,28},{14,30},{16,0},... | collective-permute-start | bytes 786440 | tf_op jit(solution)/shard_map/ppermute | solution.py:34
  18.5 21.1 %collective-permute-start.3 = (bf16[256,512]{1,0:T(8,128)(2,1)S(1)}, bf16[256,512]{1,0:T(8,128)(2,1)S(1)}, u32[]{:S(2)}, u32[]{:S(2)}) collective-permute-start(bf16[256,512]{1,0:T(8,128)(2,1)S(1)} %get-tuple-element.39), channel_id=1, source_target_pairs={{0,8},{2,10},{4,12},{6,14},{8,0},{10,2},{12,4},{14,6},{16,24},{18,... | collective-permute-start | bytes 786440 | tf_op jit(solution)/shard_map/ppermute | solution.py:34
  23.6 0.7 %copy-start.7 = (s32[1,1,5,1]{2,3,1,0:T(1,128)S(1)}, s32[1,1,5,1]{2,3,1,0:T(1,128)}, u32[]{:S(2)}) copy-start(s32[1,1,5,1]{2,3,1,0:T(1,128)} %param.14) | copy-start | bytes 64
  24.3 0.9 %copy-start.5 = (bf16[1,128,1024]{2,1,0:T(8,128)(2,1)S(1)}, bf16[1,128,1024]{2,1,0:T(8,128)(2,1)}, u32[]{:S(2)}) copy-start(bf16[1,128,1024]{2,1,0:T(8,128)(2,1)} %param.11) | copy-start | bytes 786436
  25.2 14.3 %copy-start.6 = (bf16[1,128,1024]{2,1,0:T(8,128)(2,1)S(1)}, bf16[1,128,1024]{2,1,0:T(8,128)(2,1)}, u32[]{:S(2)}) copy-start(bf16[1,128,1024]{2,1,0:T(8,128)(2,1)} %param.11) | copy-start | bytes 786436
  29.7 15.3 %collective-permute-start.7 = (bf16[256,512]{1,0:T(8,128)(2,1)S(1)}, bf16[256,512]{1,0:T(8,128)(2,1)S(1)}, u32[]{:S(2)}, u32[]{:S(2)}) collective-permute-start(bf16[256,512]{1,0:T(8,128)(2,1)S(1)} %get-tuple-element.51), channel_id=1, source_target_pairs={{0,8},{2,10},{4,12},{6,14},{8,0},{10,2},{12,4},{14,6},{16,24},{18,... | collective-permute-start | bytes 786440 | tf_op jit(solution)/shard_map/ppermute | solution.py:34
  31.0 14.1 %collective-permute-start.8 = (bf16[256,512]{1,0:T(8,128)(2,1)S(1)}, bf16[256,512]{1,0:T(8,128)(2,1)S(1)}, u32[]{:S(2)}, u32[]{:S(2)}) collective-permute-start(bf16[256,512]{1,0:T(8,128)(2,1)S(1)} %get-tuple-element.52), channel_id=1, source_target_pairs={{0,16},{2,18},{4,20},{6,22},{8,24},{10,26},{12,28},{14,30},{16,0},... | collective-permute-start | bytes 786440 | tf_op jit(solution)/shard_map/ppermute | solution.py:34
  33.4 11.6 %collective-permute-start.10 = (bf16[256,512]{1,0:T(8,128)(2,1)S(1)}, bf16[256,512]{1,0:T(8,128)(2,1)S(1)}, u32[]{:S(2)}, u32[]{:S(2)}) collective-permute-start(bf16[256,512]{1,0:T(8,128)(2,1)S(1)} %get-tuple-element.54), channel_id=1, source_target_pairs={{0,4},{2,6},{4,0},{6,2},{8,12},{10,14},{12,8},{14,10},{16,20},{18,... | collective-permute-start | bytes 786440 | tf_op jit(solution)/shard_map/ppermute | solution.py:34
  45.0 12.1 %collective-permute-start.9 = (bf16[256,1024]{1,0:T(8,128)(2,1)S(1)}, bf16[256,1024]{1,0:T(8,128)(2,1)S(1)}, u32[]{:S(2)}, u32[]{:S(2)}) collective-permute-start(bf16[256,1024]{1,0:T(8,128)(2,1)S(1)} %get-tuple-element.53), channel_id=1, source_target_pairs={{0,2},{2,0},{4,6},{6,4},{8,10},{10,8},{12,14},{14,12},{16,18},{18,... | collective-permute-start | bytes 1572872 | tf_op jit(solution)/shard_map/ppermute | solution.py:34
  45.1 4.8 %collective-permute-start.14 = (f32[1,128]{1,0:T(1,128)S(1)}, f32[1,128]{1,0:T(1,128)S(1)}, u32[]{:S(2)}, u32[]{:S(2)}) collective-permute-start(f32[1,128]{1,0:T(1,128)S(1)} %get-tuple-element.62), channel_id=1, source_target_pairs={{0,2},{2,0},{4,6},{6,4},{8,10},{10,8},{12,14},{14,12},{16,18},{18,... | collective-permute-start | bytes 1544 | tf_op jit(solution)/shard_map/ppermute | solution.py:34
  45.6 16.1 %collective-permute-start.12 = (bf16[256,512]{1,0:T(8,128)(2,1)S(1)}, bf16[256,512]{1,0:T(8,128)(2,1)S(1)}, u32[]{:S(2)}, u32[]{:S(2)}) collective-permute-start(bf16[256,512]{1,0:T(8,128)(2,1)S(1)} %get-tuple-element.57), channel_id=1, source_target_pairs={{0,8},{2,10},{4,12},{6,14},{8,0},{10,2},{12,4},{14,6},{16,24},{18,... | collective-permute-start | bytes 786440 | tf_op jit(solution)/shard_map/ppermute | solution.py:34
  46.9 14.7 %collective-permute-start.13 = (bf16[256,512]{1,0:T(8,128)(2,1)S(1)}, bf16[256,512]{1,0:T(8,128)(2,1)S(1)}, u32[]{:S(2)}, u32[]{:S(2)}) collective-permute-start(bf16[256,512]{1,0:T(8,128)(2,1)S(1)} %get-tuple-element.58), channel_id=1, source_target_pairs={{0,16},{2,18},{4,20},{6,22},{8,24},{10,26},{12,28},{14,30},{16,0},... | collective-permute-start | bytes 786440 | tf_op jit(solution)/shard_map/ppermute | solution.py:34
  49.4 7.8 %collective-permute-start.11 = (bf16[256,512]{1,0:T(8,128)(2,1)S(1)}, bf16[256,512]{1,0:T(8,128)(2,1)S(1)}, u32[]{:S(2)}, u32[]{:S(2)}) collective-permute-start(bf16[256,512]{1,0:T(8,128)(2,1)S(1)} %get-tuple-element.56), channel_id=1, source_target_pairs={{0,4},{2,6},{4,0},{6,2},{8,12},{10,14},{12,8},{14,10},{16,20},{18,... | collective-permute-start | bytes 786440 | tf_op jit(solution)/shard_map/ppermute | solution.py:34
  49.9 3.6 %collective-permute-start.15 = (f32[2,128]{1,0:T(2,128)S(1)}, f32[2,128]{1,0:T(2,128)S(1)}, u32[]{:S(2)}, u32[]{:S(2)}) collective-permute-start(f32[2,128]{1,0:T(2,128)S(1)} %pad_maximum_fusion.2), channel_id=1, source_target_pairs={{0,1},{1,0},{2,3},{3,2},{4,5},{5,4},{6,7},{7,6},{8,9},{9,8},{10,11... | collective-permute-start | bytes 3080 | tf_op jit(solution)/shard_map/ppermute | solution.py:34
  53.5 3.6 %collective-permute-start.16 = (f32[4,128]{1,0:T(4,128)S(1)}, f32[4,128]{1,0:T(4,128)S(1)}, u32[]{:S(2)}, u32[]{:S(2)}) collective-permute-start(f32[4,128]{1,0:T(4,128)S(1)} %pad_maximum_fusion.1), channel_id=1, source_target_pairs={{0,4},{2,6},{4,0},{6,2},{8,12},{10,14},{12,8},{14,10},{16,20},{18,... | collective-permute-start | bytes 6152 | tf_op jit(solution)/shard_map/ppermute | solution.py:34
  57.2 5.5 %collective-permute-start.19 = (f32[8,128]{1,0:T(8,128)S(1)}, f32[8,128]{1,0:T(8,128)S(1)}, u32[]{:S(2)}, u32[]{:S(2)}) collective-permute-start(f32[8,128]{1,0:T(8,128)S(1)} %pad_maximum_fusion.refs_0_), channel_id=1, source_target_pairs={{0,24},{2,26},{4,28},{6,30},{8,16},{10,18},{12,20},{14,22},{16,8},... | collective-permute-start | bytes 12296 | tf_op jit(solution)/shard_map/ppermute | solution.py:34
  57.8 4.8 %collective-permute-start.18 = (f32[8,128]{1,0:T(8,128)S(1)}, f32[8,128]{1,0:T(8,128)S(1)}, u32[]{:S(2)}, u32[]{:S(2)}) collective-permute-start(f32[8,128]{1,0:T(8,128)S(1)} %pad_maximum_fusion.refs_0_), channel_id=1, source_target_pairs={{0,16},{2,18},{4,20},{6,22},{8,24},{10,26},{12,28},{14,30},{16,0},... | collective-permute-start | bytes 12296 | tf_op jit(solution)/shard_map/ppermute | solution.py:34
  59.3 3.9 %collective-permute-start.17 = (f32[8,128]{1,0:T(8,128)S(1)}, f32[8,128]{1,0:T(8,128)S(1)}, u32[]{:S(2)}, u32[]{:S(2)}) collective-permute-start(f32[8,128]{1,0:T(8,128)S(1)} %pad_maximum_fusion.refs_0_), channel_id=1, source_target_pairs={{0,8},{2,10},{4,12},{6,14},{8,0},{10,2},{12,4},{14,6},{16,24},{18,... | collective-permute-start | bytes 12296 | tf_op jit(solution)/shard_map/ppermute | solution.py:34

commit v3 on v2

v3 whole, which is shorter than its diff:
```python
import functools

import jax
import jax.numpy as jnp
from jax import lax
from jax.experimental import pallas as pl
from jax.experimental.pallas import tpu as pltpu
from jax.sharding import PartitionSpec as P

H = 16
DH = 64
NB = 64
BLK = 128
HALVES = 2
INFO = 8
LANES = 128
PAIR_LANES = 2 * DH
BUCKET_LANE = 112
MASKED = -1e30
UNROLL = 4
VMEM_LIMIT = 16 * 2**20
FLOPS = 2 * 10**10

F32 = jnp.float32
BF16 = jnp.bfloat16


def contract(a, b, dim_a, dim_b):
    return lax.dot_general(a, b, (((dim_a,), (dim_b,)), ((), ())), preferred_element_type=F32)


def from_partner(value, axis, mask):
    pairs = [(source, source ^ mask) for source in range(lax.axis_size(axis))]
    return lax.ppermute(value, axis, pairs)


def lane_iota(shape):
    return lax.broadcasted_iota(jnp.int32, shape, len(shape) - 1)


def row_iota(shape):
    return lax.broadcasted_iota(jnp.int32, shape, len(shape) - 2)


def split_pair(pair, low):
    zero = jnp.zeros_like(pair)
    return jnp.concatenate([jnp.where(low, pair, zero), jnp.where(low, zero, pair)], axis=0)


def attention_body(near_count, far_count, half, *refs):
    section_count = 1 + near_count + far_count
    first = half == 0
    refs = list(refs)

    def take(count):
        taken, refs[:] = refs[:count], refs[count:]
        return taken

    seg_ref, param_ref, table_ref, q_ref, do_ref, own_pack_ref = take(6)
    near_refs = take(near_count)
    far_refs = take(far_count)
    if not first:
        masks, biases, pay_in_ref = take(3)
        earlier = take(2)
    out_ref, dq_ref = take(2)
    own_ref, *term_refs, pay_ref = take(1 + section_count)
    if first:
        masks, biases = take(2)
    half_features = far_refs[0].shape[1]
    half_heads = half_features // DH

    if first:
        own_bucket = param_ref[INFO : INFO + 1, :]
        seg_rows = seg_ref[...].astype(F32)
        in_row = row_iota((H, NB, LANES)).astype(F32) == own_bucket
        pay = jnp.zeros((1, LANES), F32)
        for s in range(section_count):
            if s == 0:
                seg_cols = seg_rows
                bucket = own_bucket
            else:
                source = near_refs[s - 1] if s <= near_count else far_refs[s - 1 - near_count]
                info = source[2 * BLK : 2 * BLK + INFO, 0:LANES].astype(F32)
                seg_cols = info[0:1]
                bucket = info[1:2]
            cols = jnp.broadcast_to(seg_cols, (BLK, BLK)).T
            masks[s * BLK : (s + 1) * BLK, :] = jnp.where(
                cols == seg_rows, jnp.broadcast_to(param_ref[s : s + 1, :], (BLK, BLK)), MASKED
            )
            hot = (row_iota((NB, LANES)).astype(F32) == bucket).astype(BF16)
            picked = contract(table_ref[...], hot, 1, 0).reshape(H, NB, LANES)
            biases[s] = jnp.sum(jnp.where(in_row, picked, 0.0), axis=1)
            pay = jnp.where(lane_iota(pay.shape) == BUCKET_LANE + s, bucket, pay)
        pay_ref[0] = pay
    else:
        pay_ref[0] = pay_in_ref[0]
        for source, target in zip(earlier, [out_ref, dq_ref]):
            target[:, 0 : half * half_features] = source[...]

    low = lane_iota((BLK, PAIR_LANES)) < DH
    lanes = lane_iota((1, LANES))

    def one_pair(pair, carry):
        here = pl.ds(pl.multiple_of(pair * PAIR_LANES, PAIR_LANES), PAIR_LANES)
        there = pl.ds(
            pl.multiple_of(half * half_features + pair * PAIR_LANES, PAIR_LANES), PAIR_LANES
        )
        mine = here if first else there
        head = half * half_heads + 2 * pair
        q_stack = split_pair(q_ref[:, there] * jnp.asarray(0.125, BF16), low)
        grad_stack = split_pair(do_ref[:, there], low)
        key_rows = jnp.concatenate(
            [own_pack_ref[0:BLK, there]]
            + [r[0:BLK, there] for r in near_refs]
            + [r[0:BLK, here] for r in far_refs],
            axis=0,
        )
        value_rows = jnp.concatenate(
            [own_pack_ref[BLK : 2 * BLK, there]]
            + [r[BLK : 2 * BLK, there] for r in near_refs]
            + [r[BLK : 2 * BLK, here] for r in far_refs],
            axis=0,
        )
        raw = contract(key_rows, q_stack, 1, 1)
        dprob = contract(value_rows, grad_stack, 1, 1)
        scores = []
        shifts = []
        top = None
        for s in range(section_count):
            block = slice(s * BLK, (s + 1) * BLK)
            mask = masks[block, :]
            score = raw[block] + jnp.concatenate([mask, mask], axis=1)
            bias = jnp.concatenate(
                [biases[s, pl.ds(head, 1), :], biases[s, pl.ds(head + 1, 1), :]], axis=1
            )
            best = jnp.max(score, axis=0, keepdims=True) + bias
            top = best if top is None else jnp.maximum(top, best)
            scores.append(score)
            shifts.append(bias)
        weights = [jnp.exp(scores[s] - (top - shifts[s])) for s in range(section_count)]
        total = sum(jnp.sum(weight, axis=0, keepdims=True) for weight in weights)
        inverse = 1.0 / total
        probs = [weight * inverse for weight in weights]
        probs_low = jnp.concatenate([prob.astype(BF16) for prob in probs], axis=0)
        out_stack = contract(probs_low, value_rows, 0, 0)
        pulls = [probs[s] * dprob[s * BLK : (s + 1) * BLK] for s in range(section_count)]
        delta = sum(jnp.sum(pull, axis=0, keepdims=True) for pull in pulls)
        dscores = [pulls[s] - probs[s] * delta for s in range(section_count)]
        dscore_low = jnp.concatenate([dscore.astype(BF16) for dscore in dscores], axis=0)
        value_terms = contract(probs_low, grad_stack, 1, 0)
        key_terms = contract(dscore_low, q_stack, 1, 0)
        dq_stack = contract(dscore_low, key_rows, 0, 0)
        out_ref[:, mine] = jnp.where(low, out_stack[:BLK], out_stack[BLK:]).astype(BF16)
        dq_ref[:, mine] = (jnp.where(low, dq_stack[:BLK], dq_stack[BLK:]) * 0.125).astype(BF16)
        pay = pay_ref[0]
        for s in range(section_count):
            sums = jnp.sum(dscores[s], axis=0, keepdims=True)
            even = jnp.sum(sums[:, :BLK], axis=1, keepdims=True)
            odd = jnp.sum(sums[:, BLK:], axis=1, keepdims=True)
            pay = jnp.where(lanes == s * H + head, even, pay)
            pay = jnp.where(lanes == s * H + head + 1, odd, pay)
            key_term = key_terms[s * BLK : (s + 1) * BLK]
            value_term = value_terms[s * BLK : (s + 1) * BLK]
            if s == 0:
                own_ref[0:BLK, here] = key_term
                own_ref[BLK : 2 * BLK, here] = value_term
            else:
                term_refs[s - 1][0:BLK, here] = key_term.astype(BF16)
                term_refs[s - 1][BLK : 2 * BLK, here] = value_term.astype(BF16)
        pay_ref[...] = jnp.broadcast_to(pay[:, None, :], pay_ref.shape)
        return carry

    lax.fori_loop(0, half_features // PAIR_LANES, one_pair, 0, unroll=UNROLL)


def attention_half(half, copies, scalars, table_rows, rows, near, far, previous):
    near_count, far_count = len(near), len(far)
    section_count = 1 + near_count + far_count
    row_count, feature_count = rows[0].shape
    half_features = feature_count // HALVES
    half_heads = half_features // DH
    vmem = pl.BlockSpec(memory_space=pltpu.VMEM)
    operands = [*scalars, table_rows, *rows, *near, *far]
    in_specs = [vmem] * len(operands)
    covered = (half + 1) * half_features
    packed = jax.ShapeDtypeStruct((2 * row_count, half_features), BF16)
    out_shape = [
        *[jax.ShapeDtypeStruct((row_count, covered), BF16)] * 2,
        jax.ShapeDtypeStruct((2 * row_count, half_features), F32),
        *[packed] * (section_count - 1),
        jax.ShapeDtypeStruct((1 if previous is None else copies, 1, LANES), F32),
    ]
    if previous is None:
        out_shape += [
            jax.ShapeDtypeStruct((section_count * BLK, BLK), F32),
            jax.ShapeDtypeStruct((section_count, H, LANES), F32),
        ]
    else:
        operands += [*previous[-2:], previous[-3], *previous[:2]]
        in_specs += [vmem] * 5
    return pl.pallas_call(
        functools.partial(attention_body, near_count, far_count, half),
        in_specs=in_specs,
        out_specs=[vmem] * len(out_shape),
        out_shape=out_shape,
        compiler_params=pltpu.CompilerParams(vmem_limit_bytes=VMEM_LIMIT),
        cost_estimate=pl.CostEstimate(
            flops=FLOPS, bytes_accessed=4 * 2**20, transcendentals=section_count * half_heads * BLK * BLK
        ),
        name="attention",
    )(*operands)


def gather_body(*refs):
    total = refs[0][...]
    for ref in refs[1:-1]:
        total = total + ref[...].astype(F32)
    refs[-1][...] = total


def gather_terms(own, terms):
    vmem = pl.BlockSpec(memory_space=pltpu.VMEM)
    return pl.pallas_call(
        gather_body,
        in_specs=[vmem] * (1 + len(terms)),
        out_specs=vmem,
        out_shape=jax.ShapeDtypeStruct(own.shape, F32),
        compiler_params=pltpu.CompilerParams(vmem_limit_bytes=VMEM_LIMIT),
        cost_estimate=pl.CostEstimate(flops=2**19, bytes_accessed=2**21, transcendentals=0),
        name="gather",
    )(own, *terms)


def finish_body(*refs):
    one_ref, two_ref, *term_refs = refs[:-2]
    half_features = one_ref.shape[1]
    for out_ref, block in zip(refs[-2:], (slice(0, BLK), slice(BLK, 2 * BLK))):
        out_ref[:, :half_features] = one_ref[block, :].astype(BF16)
        total = two_ref[block, :]
        for ref in term_refs:
            total = total + ref[block, :].astype(F32)
        out_ref[:, half_features:] = total.astype(BF16)


def finish(one, two, terms):
    vmem = pl.BlockSpec(memory_space=pltpu.VMEM)
    out = jax.ShapeDtypeStruct((one.shape[0] // 2, HALVES * one.shape[1]), BF16)
    return pl.pallas_call(
        finish_body,
        in_specs=[vmem] * (2 + len(terms)),
        out_specs=[vmem, vmem],
        out_shape=[out, out],
        compiler_params=pltpu.CompilerParams(vmem_limit_bytes=VMEM_LIMIT),
        cost_estimate=pl.CostEstimate(flops=2**19, bytes_accessed=2**21, transcendentals=0),
        name="finish",
    )(one, two, *terms)


def table_body(section_count, *refs):
    table_ref = refs[1]
    gathered_ref, scratch = refs[0], refs[2]
    count = gathered_ref.shape[0]

    def copy_row(row, carry):
        scratch[pl.ds(row, 1), :] = gathered_ref[row]
        return carry

    lax.fori_loop(0, count, copy_row, 0, unroll=8)
    gathered = scratch[...]
    lanes = lane_iota((count, PAIR_LANES))
    column = jnp.where(lanes < NB, lanes, lanes - NB).astype(F32)
    bucket = gathered[:, BUCKET_LANE : BUCKET_LANE + 1]
    row_hot = (lane_iota((count, NB)).astype(F32) == bucket).astype(F32)
    rows = jnp.concatenate([row_hot] * section_count, axis=0)
    hots = [
        column == gathered[:, BUCKET_LANE + s : BUCKET_LANE + s + 1] for s in range(section_count)
    ]
    for pair in range(H // 2):
        parts = []
        for s in range(section_count):
            lane = s * H + 2 * pair
            value = jnp.where(lanes < NB, gathered[:, lane : lane + 1], gathered[:, lane + 1 : lane + 2])
            parts.append(jnp.where(hots[s], value, 0.0))
        tile = lax.dot_general(
            rows,
            jnp.concatenate(parts, axis=0),
            (((0,), (0,)), ((), ())),
            preferred_element_type=F32,
            precision=lax.Precision.HIGHEST,
        )
        table_ref[2 * pair] = tile[:, :NB]
        table_ref[2 * pair + 1] = tile[:, NB:]


def table_of(gathered, section_count):
    vmem = pl.BlockSpec(memory_space=pltpu.VMEM)
    return pl.pallas_call(
        functools.partial(table_body, section_count),
        in_specs=[vmem],
        out_specs=vmem,
        out_shape=jax.ShapeDtypeStruct((H, NB, NB), F32),
        scratch_shapes=[pltpu.VMEM((gathered.shape[0], LANES), F32)],
        compiler_params=pltpu.CompilerParams(vmem_limit_bytes=VMEM_LIMIT),
        name="table",
    )(gathered)


def in_hbm(array):
    return pltpu.with_memory_space_constraint(array, pltpu.HBM)


def pack_body(*refs):
    mask_hbm, bucket_hbm, seg_hbm, key_hbm, value_hbm = refs[:5]
    whole_ref, first_ref, second_ref, seg_ref, param_ref = refs[5:10]
    mask_ref, bucket_ref, sems = refs[10:]
    half_features = first_ref.shape[1]
    small = [(mask_hbm, mask_ref), (bucket_hbm, bucket_ref), (seg_hbm, seg_ref)]
    copies = [
        pltpu.make_async_copy(source, target, sems.at[i]) for i, (source, target) in enumerate(small)
    ]
    for target, start, width in (
        (first_ref, 0, half_features),
        (second_ref, half_features, half_features),
        (whole_ref, 0, HALVES * half_features),
    ):
        for row, source in ((0, key_hbm), (BLK, value_hbm)):
            copies.append(
                pltpu.make_async_copy(
                    source.at[:, pl.ds(start, width)],
                    target.at[pl.ds(row, BLK), :],
                    sems.at[len(copies)],
                )
            )
    for copy in copies:
        copy.start()
    for copy in copies[: len(small)]:
        copy.wait()
    top = row_iota((INFO, LANES)) == 0
    bucket = jnp.broadcast_to(bucket_ref[...], (INFO, LANES))
    info = jnp.where(top, seg_ref[...], bucket).astype(F32).astype(BF16)
    for target in (whole_ref, first_ref):
        for start in range(0, target.shape[1], LANES):
            target[2 * BLK : 2 * BLK + INFO, start : start + LANES] = info
    lines = row_iota((2 * INFO, LANES))
    params = jnp.where(lines == INFO, bucket_ref[...].astype(F32), 0.0)
    for s in range(1, mask_ref.shape[1]):
        shut = jnp.where(mask_ref[:, s : s + 1] != 0, 0.0, MASKED)
        params = jnp.where(lines == s, shut, params)
    param_ref[...] = params
    for copy in copies[len(small) :]:
        copy.wait()


def pack(mask, bucket, seg, keys, values):
    row_count, feature_count = keys.shape
    half_features = feature_count // HALVES
    vmem = pl.BlockSpec(memory_space=pltpu.VMEM)
    hbm = pl.BlockSpec(memory_space=pltpu.HBM)
    return pl.pallas_call(
        pack_body,
        in_specs=[hbm, pl.BlockSpec(memory_space=pl.ANY), hbm, hbm, hbm],
        out_specs=[vmem] * 5,
        out_shape=[
            jax.ShapeDtypeStruct((2 * row_count + INFO, feature_count), BF16),
            jax.ShapeDtypeStruct((2 * row_count + INFO, half_features), BF16),
            jax.ShapeDtypeStruct((2 * row_count, half_features), BF16),
            jax.ShapeDtypeStruct(seg.shape, jnp.int32),
            jax.ShapeDtypeStruct((2 * INFO, LANES), F32),
        ],
        scratch_shapes=[
            pltpu.VMEM(mask.shape, jnp.int32),
            pltpu.VMEM(bucket.shape, jnp.int32),
            pltpu.SemaphoreType.DMA((3 + 3 * HALVES,)),
        ],
        compiler_params=pltpu.CompilerParams(vmem_limit_bytes=VMEM_LIMIT),
        name="pack",
    )(*[bucket if a is bucket else in_hbm(a) for a in (mask, bucket, seg, keys, values)])


def load_body(*refs):
    count = len(refs) // 2
    sems = refs[-1]
    copies = [
        pltpu.make_async_copy(source, target, sems.at[i])
        for i, (source, target) in enumerate(zip(refs[:count], refs[count : 2 * count]))
    ]
    for copy in copies:
        copy.start()
    for copy in copies:
        copy.wait()


def load(*arrays):
    return pl.pallas_call(
        load_body,
        in_specs=[pl.BlockSpec(memory_space=pltpu.HBM)] * len(arrays),
        out_specs=[pl.BlockSpec(memory_space=pltpu.VMEM)] * len(arrays),
        out_shape=[jax.ShapeDtypeStruct(a.shape, a.dtype) for a in arrays],
        scratch_shapes=[pltpu.SemaphoreType.DMA((len(arrays),))],
        compiler_params=pltpu.CompilerParams(vmem_limit_bytes=VMEM_LIMIT),
        name="load",
    )(*[in_hbm(a) for a in arrays])


def after(value, *earlier):
    return lax.optimization_barrier((value, *earlier))[0]


def double(block, axis, mask):
    return jnp.concatenate([block, from_partner(block, axis, mask)], axis=0)


def local(queries, keys, values, d_out, segment_ids, block_bucket, block_mask, bias_table):
    level_count = lax.axis_size("seq").bit_length() - 1
    far_levels = list(range(1, level_count))
    last = far_levels[-2:]

    def send(value, level):
        return from_partner(value, "seq", 1 << level)

    whole, first, second, *scalars = pack(
        block_mask.reshape(1, -1), block_bucket, segment_ids, keys[0], values[0]
    )
    query_rows, grad_rows, table_rows = load(queries[0], d_out[0], bias_table.reshape(H * NB, NB))
    rows = [query_rows, grad_rows, whole]
    far = [{}, {}]
    near = send(whole, 0)
    for level in reversed(far_levels):
        far[0][level] = send(first, level)
    for level in far_levels:
        gate = (near, query_rows)
        far[1][level] = send(after(second, *gate), level)
    near_list = [near]
    near_count = len(near_list)

    device_count = lax.axis_size("dp") * lax.axis_size("seq")
    one = attention_half(
        0, device_count, scalars, table_rows, rows, near_list, [far[0][level] for level in far_levels], None
    )
    middle = [level for level in range(level_count) if level not in last]
    terms = one[3 : 3 + level_count]
    back_one = {level: send(terms[level], level) for level in [*last, *middle]}
    late = [back_one[level] for level in last]
    two = attention_half(
        1, device_count, scalars, table_rows, rows, near_list, [far[1][level] for level in far_levels], one
    )
    terms = two[3 : 3 + level_count]
    back_two = {level: send(terms[level], level) for level in last}
    block = after(two[3 + level_count], *[back_one[level] for level in middle])
    gathered = lax.all_to_all(block, ("dp", "seq"), 0, 0, tiled=True)
    for level in middle:
        back_two[level] = send(after(terms[level], *late), level)
    sum_one = gather_terms(one[2], list(back_one.values()))
    sum_two = gather_terms(two[2], [back_two[level] for level in last])
    d_keys, d_values = finish(sum_one, sum_two, [back_two[level] for level in middle])
    table_total = table_of(after(gathered, d_keys), level_count + 1)
    return (two[0][None], two[1][None], d_keys[None], d_values[None], table_total)


def solution(mesh):
    rows = P("dp", "seq", None)
    in_specs = (
        rows,
        rows,
        rows,
        rows,
        P("dp", "seq"),
        P("dp", "seq"),
        P("dp", "seq", None, None),
        P(),
    )
    return jax.shard_map(
        local, mesh=mesh, in_specs=in_specs, out_specs=(rows,) * 4 + (P(),), check_vma=False
    )
```

time: 65.3 us -> 61.4 us (0.940)
  starting transfers between devices: 29.7 us -> 23.1 us
  waiting for transfers between devices: 17.3 us -> 22.6 us
  local copies, waits for them, and re-layouts: 4.15 us -> 0 us
  Pallas kernels: 12.6 us -> 14.2 us
    ppermute x20 -> x15, starting transfers between devices: 29.7 us -> 17.8 us  [from_partner(): return lax.ppermute(value, axis, pairs)]
    all_to_all x0 -> x1, starting transfers between devices: none -> 5.31 us  [local(): gathered = lax.all_to_all(block, ('dp', 'seq'), 0, 0, tiled=True)]
    ppermute x20 -> x15, waiting for transfers between devices: 17.3 us -> 21.9 us  [from_partner(): return lax.ppermute(value, axis, pairs)]
    unnamed x16 -> x0, local copies, waits for them, and re-layouts: 4.15 us -> none
    pallas_call x2 -> x5, Pallas kernels: 1.11 us -> 3.6 us  [the longest x1 1.39 us: pack(): pl.pallas_call(pack_body, in_specs=[hbm, pl.BlockSpec(memory_space=pl.ANY...]
    pallas_call x2, Pallas kernels: 9.56 us -> 8.71 us  [attention_half(): pl.pallas_call(functools.partial(attention_body, near_count, far_count, h...]
  transfers between devices with their start and end apart: 20 -> 16, of which waited for: 7 -> 7; matrix products, arithmetic and copies ran while one was open for 0% -> 0% of each run, Pallas kernels for 16% -> 18%
where the time goes in v3:
time: 61.4 us; the launch traced here: 61.2 us
  starting transfers between devices  23.1 us (38%)
  waiting for transfers between devices  22.6 us (37%)
  Pallas kernels  14.2 us (23%)
  between operations  1.37 us (2%)
    ppermute x15, waiting for transfers between devices, from_partner(): return lax.ppermute(value, axis, pairs)  21.9 us
    ppermute x15, starting transfers between devices, from_partner(): return lax.ppermute(value, axis, pairs)  17.8 us
    pallas_call x2, Pallas kernels, attention_half(): pl.pallas_call(functools.partial(attention_body, near_count, far_count, h...  8.71 us
    all_to_all x1, starting transfers between devices, local(): gathered = lax.all_to_all(block, ('dp', 'seq'), 0, 0, tiled=True)  5.31 us
    pallas_call x1, Pallas kernels, table_of(): pl.pallas_call(functools.partial(table_body, section_count), in_specs=[vm...  1.92 us
    pallas_call x1, Pallas kernels, pack(): pl.pallas_call(pack_body, in_specs=[hbm, pl.BlockSpec(memory_space=pl.ANY...  1.39 us
  transfers between devices with their start and end apart: 16, of which 7 were waited for; matrix products, arithmetic and copies ran while one was open for 0% of the time, Pallas kernels for 18%

profile of v3, /device:TPU:0, one launch (start us, length us, event | category | flops | bytes accessed | tf_op | source)
XLA Modules:
  0.0 61.2 jit_solution(16895926543131760366)
XLA Ops:
  1.3 1.4 %pack.1 = (bf16[264,1024]{1,0:T(8,128)(2,1)S(1)}, bf16[264,512]{1,0:T(8,128)(2,1)S(1)}, bf16[256,512]{1,0:T(8,128)(2,1)S(1)}, s32[1,128]{1,0:T(1,128)S(1)}, f32[16,128]{1,0:T(8,128)S(1)}) custom-call(s32[1,5]{1,0:T(1,128)} %bitcast.15, s32[1,1]{1,0:T(1,128)S(6)} %copy.13.refs_1_, s32[1,128]{1,0:T(1,128)} %refs_2_.1, bf16[128,1024]{1,0:T(8,128)(2,1)} %bitcast.13, ...), custom_call_target="tpu_custom_call" | custom-call | tf_op jit(solution)/shard_map/pack/pallas_call | solution.py:359
  2.7 0.5 collective-permute-start
  3.2 3.7 %collective-permute-start.6 = (bf16[264,512]{1,0:T(8,128)(2,1)S(1)}, bf16[264,512]{1,0:T(8,128)(2,1)S(1)}, u32[]{:S(2)}, u32[]{:S(2)}) collective-permute-start(bf16[264,512]{1,0:T(8,128)(2,1)S(1)} %get-tuple-element.46), channel_id=1, source_target_pairs={{0,16},{2,18},{4,20},{6,22},{8,24},{10,26},{12,28},{14,30},{16,0},... | collective-permute-start | bytes 811016 | tf_op jit(solution)/shard_map/ppermute | solution.py:34
  6.9 1.6 %collective-permute-start.5 = (bf16[264,512]{1,0:T(8,128)(2,1)S(1)}, bf16[264,512]{1,0:T(8,128)(2,1)S(1)}, u32[]{:S(2)}, u32[]{:S(2)}) collective-permute-start(bf16[264,512]{1,0:T(8,128)(2,1)S(1)} %get-tuple-element.46), channel_id=1, source_target_pairs={{0,8},{2,10},{4,12},{6,14},{8,0},{10,2},{12,4},{14,6},{16,24},{18,... | collective-permute-start | bytes 811016 | tf_op jit(solution)/shard_map/ppermute | solution.py:34
  8.4 1.5 %collective-permute-start.4 = (bf16[264,512]{1,0:T(8,128)(2,1)S(1)}, bf16[264,512]{1,0:T(8,128)(2,1)S(1)}, u32[]{:S(2)}, u32[]{:S(2)}) collective-permute-start(bf16[264,512]{1,0:T(8,128)(2,1)S(1)} %get-tuple-element.46), channel_id=1, source_target_pairs={{0,4},{2,6},{4,0},{6,2},{8,12},{10,14},{12,8},{14,10},{16,20},{18,... | collective-permute-start | bytes 811016 | tf_op jit(solution)/shard_map/ppermute | solution.py:34
  10.0 1.1 %load.1 = (bf16[128,1024]{1,0:T(8,128)(2,1)S(1)}, bf16[128,1024]{1,0:T(8,128)(2,1)S(1)}, bf16[1024,64]{1,0:T(8,128)(2,1)S(1)}) custom-call(bf16[128,1024]{1,0:T(8,128)(2,1)} %bitcast.10, bf16[128,1024]{1,0:T(8,128)(2,1)} %bitcast.11, bf16[1024,64]{1,0:T(8,128)(2,1)} %bitcast.12), custom_call_target="tpu_custom_call" | custom-call | tf_op jit(solution)/shard_map/load/pallas_call | solution.py:394
  11.1 0.0 collective-permute-done.refs_6_
  11.1 0.4 collective-permute-start.3
  11.5 0.4 collective-permute-start.2
  12.0 8.1 %collective-permute-done.6.refs_9_ = bf16[264,512]{1,0:T(8,128)(2,1)S(1)} collective-permute-done((bf16[264,512]{1,0:T(8,128)(2,1)S(1)}, bf16[264,512]{1,0:T(8,128)(2,1)S(1)}, u32[]{:S(2)}, u32[]{:S(2)}) %collective-permute-start.6) | collective-permute-done | bytes 270368 | tf_op jit(solution)/shard_map/ppermute | solution.py:34
  20.1 1.8 %collective-permute-start.1 = (bf16[256,512]{1,0:T(8,128)(2,1)S(1)}, bf16[256,512]{1,0:T(8,128)(2,1)S(1)}, u32[]{:S(2)}, u32[]{:S(2)}) collective-permute-start(bf16[256,512]{1,0:T(8,128)(2,1)S(1)} %get-tuple-element.45), channel_id=1, source_target_pairs={{0,4},{2,6},{4,0},{6,2},{8,12},{10,14},{12,8},{14,10},{16,20},{18,... | collective-permute-start | bytes 786440 | tf_op jit(solution)/shard_map/ppermute | solution.py:34
  21.9 0.1 collective-permute-done.5.refs_8_
  22.0 0.0 collective-permute-done.4.refs_7_
  22.0 4.0 %attention.2 = (bf16[128,512]{1,0:T(8,128)(2,1)S(1)}, bf16[128,512]{1,0:T(8,128)(2,1)S(1)}, f32[256,512]{1,0:T(8,128)S(1)}, bf16[256,512]{1,0:T(8,128)(2,1)S(1)}...) custom-call(s32[1,128]{1,0:T(1,128)S(1)} %get-tuple-element.38.refs_, ...), custom_call_target="tpu_custom_call" | custom-call | flops 20000000000 | bytes 4194304 | tf_op jit(solution)/shard_map/attention/pallas_call | solution.py:201
  26.0 0.4 collective-permute-start.7
  26.4 3.6 %collective-permute-start.8 = (bf16[256,512]{1,0:T(8,128)(2,1)S(1)}, bf16[256,512]{1,0:T(8,128)(2,1)S(1)}, u32[]{:S(2)}, u32[]{:S(2)}) collective-permute-start(bf16[256,512]{1,0:T(8,128)(2,1)S(1)} %get-tuple-element.56), channel_id=1, source_target_pairs={{0,16},{2,18},{4,20},{6,22},{8,24},{10,26},{12,28},{14,30},{16,0},... | collective-permute-start | bytes 786440 | tf_op jit(solution)/shard_map/ppermute | solution.py:34
  30.0 1.4 %collective-permute-done.3.refs_9_ = bf16[256,512]{1,0:T(8,128)(2,1)S(1)} collective-permute-done((bf16[256,512]{1,0:T(8,128)(2,1)S(1)}, bf16[256,512]{1,0:T(8,128)(2,1)S(1)}, u32[]{:S(2)}, u32[]{:S(2)}) %collective-permute-start.3) | collective-permute-done | bytes 262176 | tf_op jit(solution)/shard_map/ppermute | solution.py:34
  31.4 5.6 %collective-permute-done.2.refs_8_ = bf16[256,512]{1,0:T(8,128)(2,1)S(1)} collective-permute-done((bf16[256,512]{1,0:T(8,128)(2,1)S(1)}, bf16[256,512]{1,0:T(8,128)(2,1)S(1)}, u32[]{:S(2)}, u32[]{:S(2)}) %collective-permute-start.2) | collective-permute-done | bytes 262176 | tf_op jit(solution)/shard_map/ppermute | solution.py:34
  37.0 1.9 %collective-permute-start.10 = (bf16[256,512]{1,0:T(8,128)(2,1)S(1)}, bf16[256,512]{1,0:T(8,128)(2,1)S(1)}, u32[]{:S(2)}, u32[]{:S(2)}) collective-permute-start(bf16[256,512]{1,0:T(8,128)(2,1)S(1)} %get-tuple-element.58), channel_id=1, source_target_pairs={{0,4},{2,6},{4,0},{6,2},{8,12},{10,14},{12,8},{14,10},{16,20},{18,... | collective-permute-start | bytes 786440 | tf_op jit(solution)/shard_map/ppermute | solution.py:34
  38.9 0.0 collective-permute-done.1.refs_7_
  38.9 4.7 %attention.3 = (bf16[128,1024]{1,0:T(8,128)(2,1)}, bf16[128,1024]{1,0:T(8,128)(2,1)}, f32[256,512]{1,0:T(8,128)S(1)}, bf16[256,512]{1,0:T(8,128)(2,1)}, bf16[256...) custom-call(s32[1,128]{1,0:T(1,128)S(1)} %get-tuple-element.38.refs_0_, ...), custom_call_target="tpu_custom_call" | custom-call | flops 20000000000 | bytes 4194304 | tf_op jit(solution)/shard_map/attention/pallas_call | solution.py:201
  43.6 0.4 collective-permute-start.12
  44.0 0.0 collective-permute-done.8.refs_2_
  44.0 1.6 %collective-permute-start.14 = (bf16[256,512]{1,0:T(8,128)(2,1)S(1)}, bf16[256,512]{1,0:T(8,128)(2,1)S(1)}, u32[]{:S(2)}, u32[]{:S(2)}) collective-permute-start(bf16[256,512]{1,0:T(8,128)(2,1)S(1)} %get-tuple-element.65), channel_id=1, source_target_pairs={{0,4},{2,6},{4,0},{6,2},{8,12},{10,14},{12,8},{14,10},{16,20},{18,... | collective-permute-start | bytes 786440 | tf_op jit(solution)/shard_map/ppermute | solution.py:34
  45.6 5.3 %all-to-all-start = ((f32[32,1,128]{2,1,0:T(1,128)}), f32[32,1,128]{2,1,0:T(1,128)S(1)}, u32[]{:S(2)}, u32[]{:S(2)}) async-start(f32[32,1,128]{2,1,0:T(1,128)} %get-tuple-element.69), calls=%async_computation | async-start | bytes 32768 | tf_op jit(solution)/shard_map/all_to_all | solution.py:450
  50.9 0.1 gather.2.refs_0_
  51.0 0.9 %collective-permute-done.11.refs_1_ = bf16[256,512]{1,0:T(8,128)(2,1)S(1)} collective-permute-done((bf16[256,512]{1,0:T(8,128)(2,1)}, bf16[256,512]{1,0:T(8,128)(2,1)S(1)}, u32[]{:S(2)}, u32[]{:S(2)}) %collective-permute-start.11) | collective-permute-done | bytes 262176 | tf_op jit(solution)/shard_map/ppermute | solution.py:34
  51.9 5.8 %collective-permute-done.12.refs_2_ = bf16[256,512]{1,0:T(8,128)(2,1)S(1)} collective-permute-done((bf16[256,512]{1,0:T(8,128)(2,1)}, bf16[256,512]{1,0:T(8,128)(2,1)S(1)}, u32[]{:S(2)}, u32[]{:S(2)}) %collective-permute-start.12) | collective-permute-done | bytes 262176 | tf_op jit(solution)/shard_map/ppermute | solution.py:34
  57.7 0.1 gather.3.refs_1_
  57.8 0.9 %finish.1 = (bf16[128,1024]{1,0:T(8,128)(2,1)}, bf16[128,1024]{1,0:T(8,128)(2,1)}) custom-call(f32[256,512]{1,0:T(8,128)S(1)} %gather.2.refs_0_, f32[256,512]{1,0:T(8,128)S(1)} %gather.3.refs_1_, bf16[256,512]{1,0:T(8,128)(2,1)S(1)} %collective-permute-done.13.refs_2_, bf16[256,512]{1,0:T(8,128)(2,1)S(1)} %collective-permute-done.14.refs_3_), custom_call_target="tpu_custom_call" | custom-call | flops 524288 | bytes 2097152 | tf_op jit(solution)/shard_map/finish/pallas_call | solution.py:248
  58.7 0.6 %all-to-all-done.refs_0_ = f32[32,1,128]{2,1,0:T(1,128)S(1)} async-done(((f32[32,1,128]{2,1,0:T(1,128)}), f32[32,1,128]{2,1,0:T(1,128)S(1)}, u32[]{:S(2)}, u32[]{:S(2)}) %all-to-all-start) | async-done | bytes 16416 | tf_op jit(solution)/shard_map/all_to_all | solution.py:450
  59.3 1.9 %table.1 = f32[16,64,64]{2,1,0:T(8,128)} custom-call(f32[32,1,128]{2,1,0:T(1,128)S(1)} %all-to-all-done.refs_0_), custom_call_target="tpu_custom_call" | custom-call | tf_op jit(solution)/shard_map/table/pallas_call | solution.py:297
  (8 shorter events, 0.0 us)
Async XLA Ops:
  2.7 8.4 %collective-permute-start = (bf16[264,1024]{1,0:T(8,128)(2,1)S(1)}, bf16[264,1024]{1,0:T(8,128)(2,1)S(1)}, u32[]{:S(2)}, u32[]{:S(2)}) collective-permute-start(bf16[264,1024]{1,0:T(8,128)(2,1)S(1)} %get-tuple-element.43.refs_5_), channel_id=1, source_target_pairs={{0,2},{2,0},{4,6},{6,4},{8,10},{10,8},{12,14},{14,12},{16,18},{18,... | collective-permute-start | bytes 1622024 | tf_op jit(solution)/shard_map/ppermute | solution.py:34
  3.2 16.9 %collective-permute-start.6 = (bf16[264,512]{1,0:T(8,128)(2,1)S(1)}, bf16[264,512]{1,0:T(8,128)(2,1)S(1)}, u32[]{:S(2)}, u32[]{:S(2)}) collective-permute-start(bf16[264,512]{1,0:T(8,128)(2,1)S(1)} %get-tuple-element.46), channel_id=1, source_target_pairs={{0,16},{2,18},{4,20},{6,22},{8,24},{10,26},{12,28},{14,30},{16,0},... | collective-permute-start | bytes 811016 | tf_op jit(solution)/shard_map/ppermute | solution.py:34
  6.9 15.1 %collective-permute-start.5 = (bf16[264,512]{1,0:T(8,128)(2,1)S(1)}, bf16[264,512]{1,0:T(8,128)(2,1)S(1)}, u32[]{:S(2)}, u32[]{:S(2)}) collective-permute-start(bf16[264,512]{1,0:T(8,128)(2,1)S(1)} %get-tuple-element.46), channel_id=1, source_target_pairs={{0,8},{2,10},{4,12},{6,14},{8,0},{10,2},{12,4},{14,6},{16,24},{18,... | collective-permute-start | bytes 811016 | tf_op jit(solution)/shard_map/ppermute | solution.py:34
  8.4 13.5 %collective-permute-start.4 = (bf16[264,512]{1,0:T(8,128)(2,1)S(1)}, bf16[264,512]{1,0:T(8,128)(2,1)S(1)}, u32[]{:S(2)}, u32[]{:S(2)}) collective-permute-start(bf16[264,512]{1,0:T(8,128)(2,1)S(1)} %get-tuple-element.46), channel_id=1, source_target_pairs={{0,4},{2,6},{4,0},{6,2},{8,12},{10,14},{12,8},{14,10},{16,20},{18,... | collective-permute-start | bytes 811016 | tf_op jit(solution)/shard_map/ppermute | solution.py:34
  11.1 20.3 %collective-permute-start.3 = (bf16[256,512]{1,0:T(8,128)(2,1)S(1)}, bf16[256,512]{1,0:T(8,128)(2,1)S(1)}, u32[]{:S(2)}, u32[]{:S(2)}) collective-permute-start(bf16[256,512]{1,0:T(8,128)(2,1)S(1)} %get-tuple-element.45), channel_id=1, source_target_pairs={{0,16},{2,18},{4,20},{6,22},{8,24},{10,26},{12,28},{14,30},{16,0},... | collective-permute-start | bytes 786440 | tf_op jit(solution)/shard_map/ppermute | solution.py:34
  11.5 25.5 %collective-permute-start.2 = (bf16[256,512]{1,0:T(8,128)(2,1)S(1)}, bf16[256,512]{1,0:T(8,128)(2,1)S(1)}, u32[]{:S(2)}, u32[]{:S(2)}) collective-permute-start(bf16[256,512]{1,0:T(8,128)(2,1)S(1)} %get-tuple-element.45), channel_id=1, source_target_pairs={{0,8},{2,10},{4,12},{6,14},{8,0},{10,2},{12,4},{14,6},{16,24},{18,... | collective-permute-start | bytes 786440 | tf_op jit(solution)/shard_map/ppermute | solution.py:34
  20.1 18.8 %collective-permute-start.1 = (bf16[256,512]{1,0:T(8,128)(2,1)S(1)}, bf16[256,512]{1,0:T(8,128)(2,1)S(1)}, u32[]{:S(2)}, u32[]{:S(2)}) collective-permute-start(bf16[256,512]{1,0:T(8,128)(2,1)S(1)} %get-tuple-element.45), channel_id=1, source_target_pairs={{0,4},{2,6},{4,0},{6,2},{8,12},{10,14},{12,8},{14,10},{16,20},{18,... | collective-permute-start | bytes 786440 | tf_op jit(solution)/shard_map/ppermute | solution.py:34
  26.0 17.6 %collective-permute-start.7 = (bf16[256,512]{1,0:T(8,128)(2,1)S(1)}, bf16[256,512]{1,0:T(8,128)(2,1)S(1)}, u32[]{:S(2)}, u32[]{:S(2)}) collective-permute-start(bf16[256,512]{1,0:T(8,128)(2,1)S(1)} %get-tuple-element.55), channel_id=1, source_target_pairs={{0,8},{2,10},{4,12},{6,14},{8,0},{10,2},{12,4},{14,6},{16,24},{18,... | collective-permute-start | bytes 786440 | tf_op jit(solution)/shard_map/ppermute | solution.py:34
  26.4 17.6 %collective-permute-start.8 = (bf16[256,512]{1,0:T(8,128)(2,1)S(1)}, bf16[256,512]{1,0:T(8,128)(2,1)S(1)}, u32[]{:S(2)}, u32[]{:S(2)}) collective-permute-start(bf16[256,512]{1,0:T(8,128)(2,1)S(1)} %get-tuple-element.56), channel_id=1, source_target_pairs={{0,16},{2,18},{4,20},{6,22},{8,24},{10,26},{12,28},{14,30},{16,0},... | collective-permute-start | bytes 786440 | tf_op jit(solution)/shard_map/ppermute | solution.py:34
  31.4 12.6 %collective-permute-start.9 = (bf16[256,512]{1,0:T(8,128)(2,1)S(1)}, bf16[256,512]{1,0:T(8,128)(2,1)S(1)}, u32[]{:S(2)}, u32[]{:S(2)}) collective-permute-start(bf16[256,512]{1,0:T(8,128)(2,1)S(1)} %get-tuple-element.57), channel_id=1, source_target_pairs={{0,2},{2,0},{4,6},{6,4},{8,10},{10,8},{12,14},{14,12},{16,18},{18,... | collective-permute-start | bytes 786440 | tf_op jit(solution)/shard_map/ppermute | solution.py:34
  37.0 8.6 %collective-permute-start.10 = (bf16[256,512]{1,0:T(8,128)(2,1)S(1)}, bf16[256,512]{1,0:T(8,128)(2,1)S(1)}, u32[]{:S(2)}, u32[]{:S(2)}) collective-permute-start(bf16[256,512]{1,0:T(8,128)(2,1)S(1)} %get-tuple-element.58), channel_id=1, source_target_pairs={{0,4},{2,6},{4,0},{6,2},{8,12},{10,14},{12,8},{14,10},{16,20},{18,... | collective-permute-start | bytes 786440 | tf_op jit(solution)/shard_map/ppermute | solution.py:34
  43.6 8.3 %collective-permute-start.11 = (bf16[256,512]{1,0:T(8,128)(2,1)}, bf16[256,512]{1,0:T(8,128)(2,1)S(1)}, u32[]{:S(2)}, u32[]{:S(2)}) collective-permute-start(bf16[256,512]{1,0:T(8,128)(2,1)} %get-tuple-element.60), channel_id=1, source_target_pairs={{0,8},{2,10},{4,12},{6,14},{8,0},{10,2},{12,4},{14,6},{16,24},{18,... | collective-permute-start | bytes 786440 | tf_op jit(solution)/shard_map/ppermute | solution.py:34
  43.6 14.1 %collective-permute-start.12 = (bf16[256,512]{1,0:T(8,128)(2,1)}, bf16[256,512]{1,0:T(8,128)(2,1)S(1)}, u32[]{:S(2)}, u32[]{:S(2)}) collective-permute-start(bf16[256,512]{1,0:T(8,128)(2,1)} %get-tuple-element.61), channel_id=1, source_target_pairs={{0,16},{2,18},{4,20},{6,22},{8,24},{10,26},{12,28},{14,30},{16,0},... | collective-permute-start | bytes 786440 | tf_op jit(solution)/shard_map/ppermute | solution.py:34
  44.0 13.8 %collective-permute-start.13 = (bf16[256,512]{1,0:T(8,128)(2,1)}, bf16[256,512]{1,0:T(8,128)(2,1)S(1)}, u32[]{:S(2)}, u32[]{:S(2)}) collective-permute-start(bf16[256,512]{1,0:T(8,128)(2,1)} %get-tuple-element.63), channel_id=1, source_target_pairs={{0,2},{2,0},{4,6},{6,4},{8,10},{10,8},{12,14},{14,12},{16,18},{18,... | collective-permute-start | bytes 786440 | tf_op jit(solution)/shard_map/ppermute | solution.py:34
  44.0 13.8 %collective-permute-start.14 = (bf16[256,512]{1,0:T(8,128)(2,1)S(1)}, bf16[256,512]{1,0:T(8,128)(2,1)S(1)}, u32[]{:S(2)}, u32[]{:S(2)}) collective-permute-start(bf16[256,512]{1,0:T(8,128)(2,1)S(1)} %get-tuple-element.65), channel_id=1, source_target_pairs={{0,4},{2,6},{4,0},{6,2},{8,12},{10,14},{12,8},{14,10},{16,20},{18,... | collective-permute-start | bytes 786440 | tf_op jit(solution)/shard_map/ppermute | solution.py:34
  45.6 13.7 %all-to-all-start = ((f32[32,1,128]{2,1,0:T(1,128)}), f32[32,1,128]{2,1,0:T(1,128)S(1)}, u32[]{:S(2)}, u32[]{:S(2)}) async-start(f32[32,1,128]{2,1,0:T(1,128)} %get-tuple-element.69), calls=%async_computation | async-start | bytes 32768 | tf_op jit(solution)/shard_map/all_to_all | solution.py:450

commit v4 on v3

--- a/solution.py
+++ b/solution.py
@@ -17,6 +17,7 @@
 PAIR_LANES = 2 * DH
 BUCKET_LANE = 112
 MASKED = -1e30
+TABLE_ROWS = 32
 UNROLL = 4
 VMEM_LIMIT = 16 * 2**20
 FLOPS = 2 * 10**10
@@ -256,9 +257,35 @@
     )(one, two, *terms)
 
 
-def table_body(section_count, *refs):
-    table_ref = refs[1]
-    gathered_ref, scratch = refs[0], refs[2]
+def table_part(section_count, gathered):
+    count = gathered.shape[0]
+    lanes = lane_iota((count, LANES))
+    column = jnp.where(lanes < NB, lanes, lanes - NB).astype(F32)
+    section = jnp.right_shift(lanes, 4)
+    high = gathered.astype(BF16)
+    low = (gathered - high.astype(F32)).astype(BF16)
+    row_hot = (lane_iota((count, NB)).astype(F32) == gathered[:, BUCKET_LANE : BUCKET_LANE + 1]).astype(BF16)
+    spread = jnp.bitwise_and(row_iota((LANES, H * NB)), H - 1) == jnp.right_shift(
+        lane_iota((LANES, H * NB)), 6
+    )
+    spread = jnp.where(spread, 1.0, 0.0).astype(BF16)
+    pieces = []
+    for s in range(section_count):
+        for part in (high, low):
+            pieces.append(jnp.where(section == s, part, jnp.zeros_like(part)))
+    wide = contract(jnp.concatenate(pieces, axis=0), spread, 1, 0)
+    masked = []
+    for s in range(section_count):
+        hot = column == gathered[:, BUCKET_LANE + s : BUCKET_LANE + s + 1]
+        hot = jnp.concatenate([hot.astype(F32)] * (H * NB // LANES), axis=1)
+        for part in range(2):
+            start = (2 * s + part) * count
+            masked.append((wide[start : start + count] * hot).astype(BF16))
+    rows = jnp.concatenate([row_hot] * (2 * section_count), axis=0)
+    return contract(rows, jnp.concatenate(masked, axis=0), 0, 0)
+
+
+def table_body(section_count, gathered_ref, table_ref, scratch, total):
     count = gathered_ref.shape[0]
 
     def copy_row(row, carry):
@@ -266,30 +293,20 @@
         return carry
 
     lax.fori_loop(0, count, copy_row, 0, unroll=8)
-    gathered = scratch[...]
-    lanes = lane_iota((count, PAIR_LANES))
-    column = jnp.where(lanes < NB, lanes, lanes - NB).astype(F32)
-    bucket = gathered[:, BUCKET_LANE : BUCKET_LANE + 1]
-    row_hot = (lane_iota((count, NB)).astype(F32) == bucket).astype(F32)
-    rows = jnp.concatenate([row_hot] * section_count, axis=0)
-    hots = [
-        column == gathered[:, BUCKET_LANE + s : BUCKET_LANE + s + 1] for s in range(section_count)
-    ]
-    for pair in range(H // 2):
-        parts = []
-        for s in range(section_count):
-            lane = s * H + 2 * pair
-            value = jnp.where(lanes < NB, gathered[:, lane : lane + 1], gathered[:, lane + 1 : lane + 2])
-            parts.append(jnp.where(hots[s], value, 0.0))
-        tile = lax.dot_general(
-            rows,
-            jnp.concatenate(parts, axis=0),
-            (((0,), (0,)), ((), ())),
-            preferred_element_type=F32,
-            precision=lax.Precision.HIGHEST,
-        )
-        table_ref[2 * pair] = tile[:, :NB]
-        table_ref[2 * pair + 1] = tile[:, NB:]
+    if count <= TABLE_ROWS:
+        table = table_part(section_count, scratch[...])
+    else:
+        total[...] = jnp.zeros_like(total)
+
+        def add_part(step, carry):
+            start = pl.multiple_of(step * TABLE_ROWS, TABLE_ROWS)
+            total[...] += table_part(section_count, scratch[pl.ds(start, TABLE_ROWS), :])
+            return carry
+
+        lax.fori_loop(0, count // TABLE_ROWS, add_part, 0)
+        table = total[...]
+    for head in range(H):
+        table_ref[head] = table[:, head * NB : (head + 1) * NB]
 
 
 def table_of(gathered, section_count):
@@ -299,7 +316,10 @@
         in_specs=[vmem],
         out_specs=vmem,
         out_shape=jax.ShapeDtypeStruct((H, NB, NB), F32),
-        scratch_shapes=[pltpu.VMEM((gathered.shape[0], LANES), F32)],
+        scratch_shapes=[
+            pltpu.VMEM((gathered.shape[0], LANES), F32),
+            pltpu.VMEM((NB, H * NB), F32),
+        ],
         compiler_params=pltpu.CompilerParams(vmem_limit_bytes=VMEM_LIMIT),
         name="table",
     )(gathered)
@@ -439,17 +459,18 @@
     )
     middle = [level for level in range(level_count) if level not in last]
     terms = one[3 : 3 + level_count]
-    back_one = {level: send(terms[level], level) for level in [*last, *middle]}
+    back_one = {level: send(terms[level], level) for level in [*last, *middle[1:]]}
     late = [back_one[level] for level in last]
     two = attention_half(
         1, device_count, scalars, table_rows, rows, near_list, [far[1][level] for level in far_levels], one
     )
     terms = two[3 : 3 + level_count]
     back_two = {level: send(terms[level], level) for level in last}
-    block = after(two[3 + level_count], *[back_one[level] for level in middle])
+    block = two[3 + level_count]
     gathered = lax.all_to_all(block, ("dp", "seq"), 0, 0, tiled=True)
     for level in middle:
-        back_two[level] = send(after(terms[level], *late), level)
+        back_two[level] = send(after(terms[level], *late, *[back_one[m] for m in middle[1:]]), level)
+    back_one[0] = send(after(one[3], *late), 0)
     sum_one = gather_terms(one[2], list(back_one.values()))
     sum_two = gather_terms(two[2], [back_two[level] for level in last])
     d_keys, d_values = finish(sum_one, sum_two, [back_two[level] for level in middle])

time: 61.4 us -> 59 us (0.961)
  waiting for transfers between devices: 22.6 us -> 20.8 us
    ppermute x15, waiting for transfers between devices: 21.9 us -> 19.3 us  [from_partner(): return lax.ppermute(value, axis, pairs)]
    all_to_all x1, waiting for transfers between devices: 0.65 us -> 1.52 us  [local(): gathered = lax.all_to_all(block, ('dp', 'seq'), 0, 0, tiled=True)]
  transfers between devices with their start and end apart: 16 -> 16, of which waited for: 7 -> 8; matrix products, arithmetic and copies ran while one was open for 0% -> 0% of each run, Pallas kernels for 18% -> 19%
where the time goes in v4:
time: 59 us; the launch traced here: 58.8 us
  starting transfers between devices  23 us (39%)
  waiting for transfers between devices  20.8 us (35%)
  Pallas kernels  13.7 us (23%)
  between operations  1.38 us (2%)
    ppermute x15, waiting for transfers between devices, from_partner(): return lax.ppermute(value, axis, pairs)  19.3 us
    ppermute x15, starting transfers between devices, from_partner(): return lax.ppermute(value, axis, pairs)  18.1 us
    pallas_call x2, Pallas kernels, attention_half(): pl.pallas_call(functools.partial(attention_body, near_count, far_count, h...  8.76 us
    all_to_all x1, starting transfers between devices, local(): gathered = lax.all_to_all(block, ('dp', 'seq'), 0, 0, tiled=True)  4.8 us
    all_to_all x1, waiting for transfers between devices, local(): gathered = lax.all_to_all(block, ('dp', 'seq'), 0, 0, tiled=True)  1.52 us
    pallas_call x1, Pallas kernels, pack(): pl.pallas_call(pack_body, in_specs=[hbm, pl.BlockSpec(memory_space=pl.ANY...  1.39 us
    pallas_call x1, Pallas kernels, table_of(): pl.pallas_call(functools.partial(table_body, section_count), in_specs=[vm...  1.36 us
  transfers between devices with their start and end apart: 16, of which 8 were waited for; matrix products, arithmetic and copies ran while one was open for 0% of the time, Pallas kernels for 19%

profile of v4, /device:TPU:0, one launch (start us, length us, event | category | flops | bytes accessed | tf_op | source)
XLA Modules:
  0.0 58.8 jit_solution(4931430274880513538)
XLA Ops:
  1.3 1.4 %pack.1 = (bf16[264,1024]{1,0:T(8,128)(2,1)S(1)}, bf16[264,512]{1,0:T(8,128)(2,1)S(1)}, bf16[256,512]{1,0:T(8,128)(2,1)S(1)}, s32[1,128]{1,0:T(1,128)S(1)}, f32[16,128]{1,0:T(8,128)S(1)}) custom-call(s32[1,5]{1,0:T(1,128)} %bitcast.15, s32[1,1]{1,0:T(1,128)S(6)} %copy.13.refs_1_, s32[1,128]{1,0:T(1,128)} %refs_2_.1, bf16[128,1024]{1,0:T(8,128)(2,1)} %bitcast.13, ...), custom_call_target="tpu_custom_call" | custom-call | tf_op jit(solution)/shard_map/pack/pallas_call | solution.py:379
  2.7 0.5 collective-permute-start
  3.2 3.7 %collective-permute-start.6 = (bf16[264,512]{1,0:T(8,128)(2,1)S(1)}, bf16[264,512]{1,0:T(8,128)(2,1)S(1)}, u32[]{:S(2)}, u32[]{:S(2)}) collective-permute-start(bf16[264,512]{1,0:T(8,128)(2,1)S(1)} %get-tuple-element.46), channel_id=1, source_target_pairs={{0,16},{2,18},{4,20},{6,22},{8,24},{10,26},{12,28},{14,30},{16,0},... | collective-permute-start | bytes 811016 | tf_op jit(solution)/shard_map/ppermute | solution.py:35
  6.9 1.6 %collective-permute-start.5 = (bf16[264,512]{1,0:T(8,128)(2,1)S(1)}, bf16[264,512]{1,0:T(8,128)(2,1)S(1)}, u32[]{:S(2)}, u32[]{:S(2)}) collective-permute-start(bf16[264,512]{1,0:T(8,128)(2,1)S(1)} %get-tuple-element.46), channel_id=1, source_target_pairs={{0,8},{2,10},{4,12},{6,14},{8,0},{10,2},{12,4},{14,6},{16,24},{18,... | collective-permute-start | bytes 811016 | tf_op jit(solution)/shard_map/ppermute | solution.py:35
  8.4 1.5 %collective-permute-start.4 = (bf16[264,512]{1,0:T(8,128)(2,1)S(1)}, bf16[264,512]{1,0:T(8,128)(2,1)S(1)}, u32[]{:S(2)}, u32[]{:S(2)}) collective-permute-start(bf16[264,512]{1,0:T(8,128)(2,1)S(1)} %get-tuple-element.46), channel_id=1, source_target_pairs={{0,4},{2,6},{4,0},{6,2},{8,12},{10,14},{12,8},{14,10},{16,20},{18,... | collective-permute-start | bytes 811016 | tf_op jit(solution)/shard_map/ppermute | solution.py:35
  10.0 1.1 %load.1 = (bf16[128,1024]{1,0:T(8,128)(2,1)S(1)}, bf16[128,1024]{1,0:T(8,128)(2,1)S(1)}, bf16[1024,64]{1,0:T(8,128)(2,1)S(1)}) custom-call(bf16[128,1024]{1,0:T(8,128)(2,1)} %bitcast.10, bf16[128,1024]{1,0:T(8,128)(2,1)} %bitcast.11, bf16[1024,64]{1,0:T(8,128)(2,1)} %bitcast.12), custom_call_target="tpu_custom_call" | custom-call | tf_op jit(solution)/shard_map/load/pallas_call | solution.py:414
  11.1 0.4 collective-permute-start.3
  11.5 0.4 collective-permute-start.2
  12.0 8.1 %collective-permute-done.6.refs_9_ = bf16[264,512]{1,0:T(8,128)(2,1)S(1)} collective-permute-done((bf16[264,512]{1,0:T(8,128)(2,1)S(1)}, bf16[264,512]{1,0:T(8,128)(2,1)S(1)}, u32[]{:S(2)}, u32[]{:S(2)}) %collective-permute-start.6) | collective-permute-done | bytes 270368 | tf_op jit(solution)/shard_map/ppermute | solution.py:35
  20.1 1.8 %collective-permute-start.1 = (bf16[256,512]{1,0:T(8,128)(2,1)S(1)}, bf16[256,512]{1,0:T(8,128)(2,1)S(1)}, u32[]{:S(2)}, u32[]{:S(2)}) collective-permute-start(bf16[256,512]{1,0:T(8,128)(2,1)S(1)} %get-tuple-element.45), channel_id=1, source_target_pairs={{0,4},{2,6},{4,0},{6,2},{8,12},{10,14},{12,8},{14,10},{16,20},{18,... | collective-permute-start | bytes 786440 | tf_op jit(solution)/shard_map/ppermute | solution.py:35
  21.9 0.1 collective-permute-done.5.refs_8_
  22.0 4.0 %attention.2 = (bf16[128,512]{1,0:T(8,128)(2,1)S(1)}, bf16[128,512]{1,0:T(8,128)(2,1)S(1)}, f32[256,512]{1,0:T(8,128)S(1)}, bf16[256,512]{1,0:T(8,128)(2,1)S(1)}...) custom-call(s32[1,128]{1,0:T(1,128)S(1)} %get-tuple-element.38.refs_, ...), custom_call_target="tpu_custom_call" | custom-call | flops 20000000000 | bytes 4194304 | tf_op jit(solution)/shard_map/attention/pallas_call | solution.py:202
  26.0 0.4 collective-permute-start.7
  26.4 3.6 %collective-permute-start.8 = (bf16[256,512]{1,0:T(8,128)(2,1)S(1)}, bf16[256,512]{1,0:T(8,128)(2,1)S(1)}, u32[]{:S(2)}, u32[]{:S(2)}) collective-permute-start(bf16[256,512]{1,0:T(8,128)(2,1)S(1)} %get-tuple-element.56), channel_id=1, source_target_pairs={{0,16},{2,18},{4,20},{6,22},{8,24},{10,26},{12,28},{14,30},{16,0},... | collective-permute-start | bytes 786440 | tf_op jit(solution)/shard_map/ppermute | solution.py:35
  30.0 1.4 %collective-permute-done.3.refs_9_ = bf16[256,512]{1,0:T(8,128)(2,1)S(1)} collective-permute-done((bf16[256,512]{1,0:T(8,128)(2,1)S(1)}, bf16[256,512]{1,0:T(8,128)(2,1)S(1)}, u32[]{:S(2)}, u32[]{:S(2)}) %collective-permute-start.3) | collective-permute-done | bytes 262176 | tf_op jit(solution)/shard_map/ppermute | solution.py:35
  31.4 1.8 %collective-permute-start.9 = (bf16[256,512]{1,0:T(8,128)(2,1)S(1)}, bf16[256,512]{1,0:T(8,128)(2,1)S(1)}, u32[]{:S(2)}, u32[]{:S(2)}) collective-permute-start(bf16[256,512]{1,0:T(8,128)(2,1)S(1)} %get-tuple-element.57), channel_id=1, source_target_pairs={{0,4},{2,6},{4,0},{6,2},{8,12},{10,14},{12,8},{14,10},{16,20},{18,... | collective-permute-start | bytes 786440 | tf_op jit(solution)/shard_map/ppermute | solution.py:35
  33.1 3.8 %collective-permute-done.2.refs_8_ = bf16[256,512]{1,0:T(8,128)(2,1)S(1)} collective-permute-done((bf16[256,512]{1,0:T(8,128)(2,1)S(1)}, bf16[256,512]{1,0:T(8,128)(2,1)S(1)}, u32[]{:S(2)}, u32[]{:S(2)}) %collective-permute-start.2) | collective-permute-done | bytes 262176 | tf_op jit(solution)/shard_map/ppermute | solution.py:35
  37.0 0.0 collective-permute-done.1.refs_7_
  37.0 4.8 %attention.3 = (bf16[128,1024]{1,0:T(8,128)(2,1)}, bf16[128,1024]{1,0:T(8,128)(2,1)}, f32[256,512]{1,0:T(8,128)S(1)}, bf16[256,512]{1,0:T(8,128)(2,1)}, bf16[256...) custom-call(s32[1,128]{1,0:T(1,128)S(1)} %get-tuple-element.38.refs_0_, ...), custom_call_target="tpu_custom_call" | custom-call | flops 20000000000 | bytes 4194304 | tf_op jit(solution)/shard_map/attention/pallas_call | solution.py:202
  41.7 0.0 collective-permute-start.11
  41.7 0.0 collective-permute-start.12
  41.8 0.9 %collective-permute-done.7.refs_1_ = bf16[256,512]{1,0:T(8,128)(2,1)S(1)} collective-permute-done((bf16[256,512]{1,0:T(8,128)(2,1)S(1)}, bf16[256,512]{1,0:T(8,128)(2,1)S(1)}, u32[]{:S(2)}, u32[]{:S(2)}) %collective-permute-start.7) | collective-permute-done | bytes 262176 | tf_op jit(solution)/shard_map/ppermute | solution.py:35
  42.7 0.5 collective-permute-start.13
  43.2 1.9 %collective-permute-start.14 = (bf16[256,512]{1,0:T(8,128)(2,1)}, bf16[256,512]{1,0:T(8,128)(2,1)S(1)}, u32[]{:S(2)}, u32[]{:S(2)}) collective-permute-start(bf16[256,512]{1,0:T(8,128)(2,1)} %get-tuple-element.66), channel_id=1, source_target_pairs={{0,4},{2,6},{4,0},{6,2},{8,12},{10,14},{12,8},{14,10},{16,20},{18,... | collective-permute-start | bytes 786440 | tf_op jit(solution)/shard_map/ppermute | solution.py:35
  45.1 4.8 %all-to-all-start = ((f32[32,1,128]{2,1,0:T(1,128)}), f32[32,1,128]{2,1,0:T(1,128)S(1)}, u32[]{:S(2)}, u32[]{:S(2)}) async-start(f32[32,1,128]{2,1,0:T(1,128)} %get-tuple-element.69), calls=%async_computation | async-start | bytes 32768 | tf_op jit(solution)/shard_map/all_to_all | solution.py:470
  49.9 0.1 gather.2.refs_0_
  50.1 3.6 %collective-permute-done.11.refs_1_ = bf16[256,512]{1,0:T(8,128)(2,1)S(1)} collective-permute-done((bf16[256,512]{1,0:T(8,128)(2,1)}, bf16[256,512]{1,0:T(8,128)(2,1)S(1)}, u32[]{:S(2)}, u32[]{:S(2)}) %collective-permute-start.11) | collective-permute-done | bytes 262176 | tf_op jit(solution)/shard_map/ppermute | solution.py:35
  53.6 1.4 %collective-permute-done.12.refs_2_ = bf16[256,512]{1,0:T(8,128)(2,1)S(1)} collective-permute-done((bf16[256,512]{1,0:T(8,128)(2,1)}, bf16[256,512]{1,0:T(8,128)(2,1)S(1)}, u32[]{:S(2)}, u32[]{:S(2)}) %collective-permute-start.12) | collective-permute-done | bytes 262176 | tf_op jit(solution)/shard_map/ppermute | solution.py:35
  55.0 0.1 gather.3.refs_1_
  55.1 0.9 %finish.1 = (bf16[128,1024]{1,0:T(8,128)(2,1)}, bf16[128,1024]{1,0:T(8,128)(2,1)}) custom-call(f32[256,512]{1,0:T(8,128)S(1)} %gather.2.refs_0_, f32[256,512]{1,0:T(8,128)S(1)} %gather.3.refs_1_, bf16[256,512]{1,0:T(8,128)(2,1)S(1)} %collective-permute-done.13.refs_2_, bf16[256,512]{1,0:T(8,128)(2,1)S(1)} %collective-permute-done.14.refs_3_), custom_call_target="tpu_custom_call" | custom-call | flops 524288 | bytes 2097152 | tf_op jit(solution)/shard_map/finish/pallas_call | solution.py:249
  56.0 1.5 %all-to-all-done.gathered_ref = f32[32,1,128]{2,1,0:T(1,128)S(1)} async-done(((f32[32,1,128]{2,1,0:T(1,128)}), f32[32,1,128]{2,1,0:T(1,128)S(1)}, u32[]{:S(2)}, u32[]{:S(2)}) %all-to-all-start) | async-done | bytes 16416 | tf_op jit(solution)/shard_map/all_to_all | solution.py:470
  57.5 1.4 %table.1 = f32[16,64,64]{2,1,0:T(8,128)} custom-call(f32[32,1,128]{2,1,0:T(1,128)S(1)} %all-to-all-done.gathered_ref), custom_call_target="tpu_custom_call" | custom-call | tf_op jit(solution)/shard_map/table/pallas_call | solution.py:314
  (8 shorter events, 0.0 us)
Async XLA Ops:
  2.7 8.4 %collective-permute-start = (bf16[264,1024]{1,0:T(8,128)(2,1)S(1)}, bf16[264,1024]{1,0:T(8,128)(2,1)S(1)}, u32[]{:S(2)}, u32[]{:S(2)}) collective-permute-start(bf16[264,1024]{1,0:T(8,128)(2,1)S(1)} %get-tuple-element.43.refs_5_), channel_id=1, source_target_pairs={{0,2},{2,0},{4,6},{6,4},{8,10},{10,8},{12,14},{14,12},{16,18},{18,... | collective-permute-start | bytes 1622024 | tf_op jit(solution)/shard_map/ppermute | solution.py:35
  3.2 16.9 %collective-permute-start.6 = (bf16[264,512]{1,0:T(8,128)(2,1)S(1)}, bf16[264,512]{1,0:T(8,128)(2,1)S(1)}, u32[]{:S(2)}, u32[]{:S(2)}) collective-permute-start(bf16[264,512]{1,0:T(8,128)(2,1)S(1)} %get-tuple-element.46), channel_id=1, source_target_pairs={{0,16},{2,18},{4,20},{6,22},{8,24},{10,26},{12,28},{14,30},{16,0},... | collective-permute-start | bytes 811016 | tf_op jit(solution)/shard_map/ppermute | solution.py:35
  6.9 15.1 %collective-permute-start.5 = (bf16[264,512]{1,0:T(8,128)(2,1)S(1)}, bf16[264,512]{1,0:T(8,128)(2,1)S(1)}, u32[]{:S(2)}, u32[]{:S(2)}) collective-permute-start(bf16[264,512]{1,0:T(8,128)(2,1)S(1)} %get-tuple-element.46), channel_id=1, source_target_pairs={{0,8},{2,10},{4,12},{6,14},{8,0},{10,2},{12,4},{14,6},{16,24},{18,... | collective-permute-start | bytes 811016 | tf_op jit(solution)/shard_map/ppermute | solution.py:35
  8.4 13.5 %collective-permute-start.4 = (bf16[264,512]{1,0:T(8,128)(2,1)S(1)}, bf16[264,512]{1,0:T(8,128)(2,1)S(1)}, u32[]{:S(2)}, u32[]{:S(2)}) collective-permute-start(bf16[264,512]{1,0:T(8,128)(2,1)S(1)} %get-tuple-element.46), channel_id=1, source_target_pairs={{0,4},{2,6},{4,0},{6,2},{8,12},{10,14},{12,8},{14,10},{16,20},{18,... | collective-permute-start | bytes 811016 | tf_op jit(solution)/shard_map/ppermute | solution.py:35
  11.1 20.3 %collective-permute-start.3 = (bf16[256,512]{1,0:T(8,128)(2,1)S(1)}, bf16[256,512]{1,0:T(8,128)(2,1)S(1)}, u32[]{:S(2)}, u32[]{:S(2)}) collective-permute-start(bf16[256,512]{1,0:T(8,128)(2,1)S(1)} %get-tuple-element.45), channel_id=1, source_target_pairs={{0,16},{2,18},{4,20},{6,22},{8,24},{10,26},{12,28},{14,30},{16,0},... | collective-permute-start | bytes 786440 | tf_op jit(solution)/shard_map/ppermute | solution.py:35
  11.5 25.5 %collective-permute-start.2 = (bf16[256,512]{1,0:T(8,128)(2,1)S(1)}, bf16[256,512]{1,0:T(8,128)(2,1)S(1)}, u32[]{:S(2)}, u32[]{:S(2)}) collective-permute-start(bf16[256,512]{1,0:T(8,128)(2,1)S(1)} %get-tuple-element.45), channel_id=1, source_target_pairs={{0,8},{2,10},{4,12},{6,14},{8,0},{10,2},{12,4},{14,6},{16,24},{18,... | collective-permute-start | bytes 786440 | tf_op jit(solution)/shard_map/ppermute | solution.py:35
  20.1 16.9 %collective-permute-start.1 = (bf16[256,512]{1,0:T(8,128)(2,1)S(1)}, bf16[256,512]{1,0:T(8,128)(2,1)S(1)}, u32[]{:S(2)}, u32[]{:S(2)}) collective-permute-start(bf16[256,512]{1,0:T(8,128)(2,1)S(1)} %get-tuple-element.45), channel_id=1, source_target_pairs={{0,4},{2,6},{4,0},{6,2},{8,12},{10,14},{12,8},{14,10},{16,20},{18,... | collective-permute-start | bytes 786440 | tf_op jit(solution)/shard_map/ppermute | solution.py:35
  26.0 16.7 %collective-permute-start.7 = (bf16[256,512]{1,0:T(8,128)(2,1)S(1)}, bf16[256,512]{1,0:T(8,128)(2,1)S(1)}, u32[]{:S(2)}, u32[]{:S(2)}) collective-permute-start(bf16[256,512]{1,0:T(8,128)(2,1)S(1)} %get-tuple-element.55), channel_id=1, source_target_pairs={{0,8},{2,10},{4,12},{6,14},{8,0},{10,2},{12,4},{14,6},{16,24},{18,... | collective-permute-start | bytes 786440 | tf_op jit(solution)/shard_map/ppermute | solution.py:35
  26.4 16.2 %collective-permute-start.8 = (bf16[256,512]{1,0:T(8,128)(2,1)S(1)}, bf16[256,512]{1,0:T(8,128)(2,1)S(1)}, u32[]{:S(2)}, u32[]{:S(2)}) collective-permute-start(bf16[256,512]{1,0:T(8,128)(2,1)S(1)} %get-tuple-element.56), channel_id=1, source_target_pairs={{0,16},{2,18},{4,20},{6,22},{8,24},{10,26},{12,28},{14,30},{16,0},... | collective-permute-start | bytes 786440 | tf_op jit(solution)/shard_map/ppermute | solution.py:35
  31.4 11.3 %collective-permute-start.9 = (bf16[256,512]{1,0:T(8,128)(2,1)S(1)}, bf16[256,512]{1,0:T(8,128)(2,1)S(1)}, u32[]{:S(2)}, u32[]{:S(2)}) collective-permute-start(bf16[256,512]{1,0:T(8,128)(2,1)S(1)} %get-tuple-element.57), channel_id=1, source_target_pairs={{0,4},{2,6},{4,0},{6,2},{8,12},{10,14},{12,8},{14,10},{16,20},{18,... | collective-permute-start | bytes 786440 | tf_op jit(solution)/shard_map/ppermute | solution.py:35
  41.7 11.9 %collective-permute-start.11 = (bf16[256,512]{1,0:T(8,128)(2,1)}, bf16[256,512]{1,0:T(8,128)(2,1)S(1)}, u32[]{:S(2)}, u32[]{:S(2)}) collective-permute-start(bf16[256,512]{1,0:T(8,128)(2,1)} %get-tuple-element.61), channel_id=1, source_target_pairs={{0,8},{2,10},{4,12},{6,14},{8,0},{10,2},{12,4},{14,6},{16,24},{18,... | collective-permute-start | bytes 786440 | tf_op jit(solution)/shard_map/ppermute | solution.py:35
  41.7 13.3 %collective-permute-start.12 = (bf16[256,512]{1,0:T(8,128)(2,1)}, bf16[256,512]{1,0:T(8,128)(2,1)S(1)}, u32[]{:S(2)}, u32[]{:S(2)}) collective-permute-start(bf16[256,512]{1,0:T(8,128)(2,1)} %get-tuple-element.62), channel_id=1, source_target_pairs={{0,16},{2,18},{4,20},{6,22},{8,24},{10,26},{12,28},{14,30},{16,0},... | collective-permute-start | bytes 786440 | tf_op jit(solution)/shard_map/ppermute | solution.py:35
  42.7 7.3 %collective-permute-start.10 = (bf16[256,512]{1,0:T(8,128)(2,1)S(1)}, bf16[256,512]{1,0:T(8,128)(2,1)S(1)}, u32[]{:S(2)}, u32[]{:S(2)}) collective-permute-start(bf16[256,512]{1,0:T(8,128)(2,1)S(1)} %get-tuple-element.59), channel_id=1, source_target_pairs={{0,2},{2,0},{4,6},{6,4},{8,10},{10,8},{12,14},{14,12},{16,18},{18,... | collective-permute-start | bytes 786440 | tf_op jit(solution)/shard_map/ppermute | solution.py:35
  42.7 12.4 %collective-permute-start.13 = (bf16[256,512]{1,0:T(8,128)(2,1)}, bf16[256,512]{1,0:T(8,128)(2,1)S(1)}, u32[]{:S(2)}, u32[]{:S(2)}) collective-permute-start(bf16[256,512]{1,0:T(8,128)(2,1)} %get-tuple-element.64), channel_id=1, source_target_pairs={{0,2},{2,0},{4,6},{6,4},{8,10},{10,8},{12,14},{14,12},{16,18},{18,... | collective-permute-start | bytes 786440 | tf_op jit(solution)/shard_map/ppermute | solution.py:35
  43.2 11.9 %collective-permute-start.14 = (bf16[256,512]{1,0:T(8,128)(2,1)}, bf16[256,512]{1,0:T(8,128)(2,1)S(1)}, u32[]{:S(2)}, u32[]{:S(2)}) collective-permute-start(bf16[256,512]{1,0:T(8,128)(2,1)} %get-tuple-element.66), channel_id=1, source_target_pairs={{0,4},{2,6},{4,0},{6,2},{8,12},{10,14},{12,8},{14,10},{16,20},{18,... | collective-permute-start | bytes 786440 | tf_op jit(solution)/shard_map/ppermute | solution.py:35
  45.1 12.4 %all-to-all-start = ((f32[32,1,128]{2,1,0:T(1,128)}), f32[32,1,128]{2,1,0:T(1,128)S(1)}, u32[]{:S(2)}, u32[]{:S(2)}) async-start(f32[32,1,128]{2,1,0:T(1,128)} %get-tuple-element.69), calls=%async_computation | async-start | bytes 32768 | tf_op jit(solution)/shard_map/all_to_all | solution.py:470

commit v5 on v4

--- a/solution.py
+++ b/solution.py
@@ -331,26 +331,20 @@
 
 def pack_body(*refs):
     mask_hbm, bucket_hbm, seg_hbm, key_hbm, value_hbm = refs[:5]
-    whole_ref, first_ref, second_ref, seg_ref, param_ref = refs[5:10]
-    mask_ref, bucket_ref, sems = refs[10:]
+    first_ref, seg_ref, param_ref, mask_ref, bucket_ref, sems = refs[5:]
     half_features = first_ref.shape[1]
     small = [(mask_hbm, mask_ref), (bucket_hbm, bucket_ref), (seg_hbm, seg_ref)]
     copies = [
         pltpu.make_async_copy(source, target, sems.at[i]) for i, (source, target) in enumerate(small)
     ]
-    for target, start, width in (
-        (first_ref, 0, half_features),
-        (second_ref, half_features, half_features),
-        (whole_ref, 0, HALVES * half_features),
-    ):
-        for row, source in ((0, key_hbm), (BLK, value_hbm)):
-            copies.append(
-                pltpu.make_async_copy(
-                    source.at[:, pl.ds(start, width)],
-                    target.at[pl.ds(row, BLK), :],
-                    sems.at[len(copies)],
-                )
+    for row, source in ((0, key_hbm), (BLK, value_hbm)):
+        copies.append(
+            pltpu.make_async_copy(
+                source.at[:, pl.ds(0, half_features)],
+                first_ref.at[pl.ds(row, BLK), :],
+                sems.at[len(copies)],
             )
+        )
     for copy in copies:
         copy.start()
     for copy in copies[: len(small)]:
@@ -358,9 +352,8 @@
     top = row_iota((INFO, LANES)) == 0
     bucket = jnp.broadcast_to(bucket_ref[...], (INFO, LANES))
     info = jnp.where(top, seg_ref[...], bucket).astype(F32).astype(BF16)
-    for target in (whole_ref, first_ref):
-        for start in range(0, target.shape[1], LANES):
-            target[2 * BLK : 2 * BLK + INFO, start : start + LANES] = info
+    for start in range(0, half_features, LANES):
+        first_ref[2 * BLK : 2 * BLK + INFO, start : start + LANES] = info
     lines = row_iota((2 * INFO, LANES))
     params = jnp.where(lines == INFO, bucket_ref[...].astype(F32), 0.0)
     for s in range(1, mask_ref.shape[1]):
@@ -373,53 +366,67 @@
 
 def pack(mask, bucket, seg, keys, values):
     row_count, feature_count = keys.shape
-    half_features = feature_count // HALVES
     vmem = pl.BlockSpec(memory_space=pltpu.VMEM)
     hbm = pl.BlockSpec(memory_space=pltpu.HBM)
     return pl.pallas_call(
         pack_body,
         in_specs=[hbm, pl.BlockSpec(memory_space=pl.ANY), hbm, hbm, hbm],
-        out_specs=[vmem] * 5,
+        out_specs=[vmem] * 3,
         out_shape=[
-            jax.ShapeDtypeStruct((2 * row_count + INFO, feature_count), BF16),
-            jax.ShapeDtypeStruct((2 * row_count + INFO, half_features), BF16),
-            jax.ShapeDtypeStruct((2 * row_count, half_features), BF16),
+            jax.ShapeDtypeStruct((2 * row_count + INFO, feature_count // HALVES), BF16),
             jax.ShapeDtypeStruct(seg.shape, jnp.int32),
             jax.ShapeDtypeStruct((2 * INFO, LANES), F32),
         ],
         scratch_shapes=[
             pltpu.VMEM(mask.shape, jnp.int32),
             pltpu.VMEM(bucket.shape, jnp.int32),
-            pltpu.SemaphoreType.DMA((3 + 3 * HALVES,)),
+            pltpu.SemaphoreType.DMA((5,)),
         ],
         compiler_params=pltpu.CompilerParams(vmem_limit_bytes=VMEM_LIMIT),
         name="pack",
     )(*[bucket if a is bucket else in_hbm(a) for a in (mask, bucket, seg, keys, values)])
 
 
-def load_body(*refs):
-    count = len(refs) // 2
-    sems = refs[-1]
-    copies = [
-        pltpu.make_async_copy(source, target, sems.at[i])
-        for i, (source, target) in enumerate(zip(refs[:count], refs[count : 2 * count]))
-    ]
-    for copy in copies:
-        copy.start()
+def load_body(first_ref, *refs):
+    sources, targets, sems = refs[:5], refs[5:10], refs[10]
+    whole_ref, second_ref = targets[:2]
+    half_features = first_ref.shape[1]
+    copies = []
+
+    def add(source, target):
+        copies.append(pltpu.make_async_copy(source, target, sems.at[len(copies)]))
+        copies[-1].start()
+
+    for row, source in ((0, sources[0]), (BLK, sources[1])):
+        add(source, whole_ref.at[pl.ds(row, BLK), :])
+        add(source.at[:, pl.ds(half_features, half_features)], second_ref.at[pl.ds(row, BLK), :])
+    for source, target in zip(sources[2:], targets[2:]):
+        add(source, target)
+    info = first_ref[2 * BLK : 2 * BLK + INFO, :]
+    for half in range(HALVES):
+        window = slice(half * half_features, (half + 1) * half_features)
+        whole_ref[2 * BLK : 2 * BLK + INFO, window] = info
     for copy in copies:
         copy.wait()
 
 
-def load(*arrays):
+def load(first, keys, values, *arrays):
+    row_count, feature_count = keys.shape
+    vmem = pl.BlockSpec(memory_space=pltpu.VMEM)
+    out_shape = [
+        jax.ShapeDtypeStruct((2 * row_count + INFO, feature_count), BF16),
+        jax.ShapeDtypeStruct((2 * row_count, feature_count // HALVES), BF16),
+        *[jax.ShapeDtypeStruct(a.shape, a.dtype) for a in arrays],
+    ]
     return pl.pallas_call(
         load_body,
-        in_specs=[pl.BlockSpec(memory_space=pltpu.HBM)] * len(arrays),
-        out_specs=[pl.BlockSpec(memory_space=pltpu.VMEM)] * len(arrays),
-        out_shape=[jax.ShapeDtypeStruct(a.shape, a.dtype) for a in arrays],
-        scratch_shapes=[pltpu.SemaphoreType.DMA((len(arrays),))],
+        in_specs=[vmem] + [pl.BlockSpec(memory_space=pltpu.HBM)] * 5,
+        out_specs=[vmem] * 5,
+        out_shape=out_shape,
+        scratch_shapes=[pltpu.SemaphoreType.DMA((4 + len(arrays),))],
         compiler_params=pltpu.CompilerParams(vmem_limit_bytes=VMEM_LIMIT),
         name="load",
-    )(*[in_hbm(a) for a in arrays])
+    )(first, *[in_hbm(a) for a in (keys, values, *arrays)])
 
 
 def after(value, *earlier):
@@ -432,25 +439,26 @@
 
 def local(queries, keys, values, d_out, segment_ids, block_bucket, block_mask, bias_table):
     level_count = lax.axis_size("seq").bit_length() - 1
-    far_levels = list(range(1, level_count))
+    far_levels = list(range(level_count))
     last = far_levels[-2:]
 
     def send(value, level):
         return from_partner(value, "seq", 1 << level)
 
-    whole, first, second, *scalars = pack(
+    first, *scalars = pack(
         block_mask.reshape(1, -1), block_bucket, segment_ids, keys[0], values[0]
     )
-    query_rows, grad_rows, table_rows = load(queries[0], d_out[0], bias_table.reshape(H * NB, NB))
+    whole, second, query_rows, grad_rows, table_rows = load(
+        first, keys[0], values[0], queries[0], d_out[0], bias_table.reshape(H * NB, NB)
+    )
     rows = [query_rows, grad_rows, whole]
     far = [{}, {}]
-    near = send(whole, 0)
     for level in reversed(far_levels):
         far[0][level] = send(first, level)
     for level in far_levels:
-        gate = (near, query_rows)
+        gate = (far[0][0], query_rows) if level else (far[0][last[-1]], query_rows)
         far[1][level] = send(after(second, *gate), level)
-    near_list = [near]
+    near_list = []
     near_count = len(near_list)
 
     device_count = lax.axis_size("dp") * lax.axis_size("seq")

time: 59 us -> 58.2 us (0.986)
  waiting for transfers between devices: 20.8 us -> 20.1 us
    ppermute x15 -> x16, waiting for transfers between devices: 19.3 us -> 19 us  [from_partner(): return lax.ppermute(value, axis, pairs)]
    ppermute x15 -> x16, starting transfers between devices: 18.1 us -> 18.1 us  [from_partner(): return lax.ppermute(value, axis, pairs)]
  transfers between devices with their start and end apart: 16 -> 17, of which waited for: 8 -> 8; matrix products, arithmetic and copies ran while one was open for 0% -> 0% of each run, Pallas kernels for 19% -> 19%
where the time goes in v5:
time: 58.2 us; the launch traced here: 58 us
  starting transfers between devices  23 us (40%)
  waiting for transfers between devices  20.1 us (35%)
  Pallas kernels  13.6 us (23%)
  between operations  1.38 us (2%)
    ppermute x16, waiting for transfers between devices, from_partner(): return lax.ppermute(value, axis, pairs)  19 us
    ppermute x16, starting transfers between devices, from_partner(): return lax.ppermute(value, axis, pairs)  18.1 us
    pallas_call x2, Pallas kernels, attention_half(): pl.pallas_call(functools.partial(attention_body, near_count, far_count, h...  8.72 us
    all_to_all x1, starting transfers between devices, local(): gathered = lax.all_to_all(block, ('dp', 'seq'), 0, 0, tiled=True)  4.87 us
    pallas_call x1, Pallas kernels, load(): pl.pallas_call(load_body, in_specs=[vmem] + [pl.BlockSpec(memory_space=pl...  1.43 us
    pallas_call x1, Pallas kernels, table_of(): pl.pallas_call(functools.partial(table_body, section_count), in_specs=[vm...  1.36 us
  transfers between devices with their start and end apart: 17, of which 8 were waited for; matrix products, arithmetic and copies ran while one was open for 0% of the time, Pallas kernels for 19%

profile of v5, /device:TPU:0, one launch (start us, length us, event | category | flops | bytes accessed | tf_op | source)
XLA Modules:
  0.0 58.0 jit_solution(10826284189795110835)
XLA Ops:
  1.3 1.0 %pack.1 = (bf16[264,512]{1,0:T(8,128)(2,1)S(1)}, s32[1,128]{1,0:T(1,128)S(1)}, f32[16,128]{1,0:T(8,128)S(1)}) custom-call(s32[1,5]{1,0:T(1,128)} %bitcast.17, s32[1,1]{1,0:T(1,128)S(6)} %copy.13.refs_1_, s32[1,128]{1,0:T(1,128)} %refs_2_.1, bf16[128,1024]{1,0:T(8,128)(2,1)} %bitcast.10, bf16[128,1024]{1,0:T(8,128)(2,1)} %bitcast.12), custom_call_target="tpu_custom_call" | custom-call | tf_op jit(solution)/shard_map/pack/pallas_call | solution.py:371
  2.3 0.5 collective-permute-start.2
  2.8 3.7 %collective-permute-start = (bf16[264,512]{1,0:T(8,128)(2,1)S(1)}, bf16[264,512]{1,0:T(8,128)(2,1)S(1)}, u32[]{:S(2)}, u32[]{:S(2)}) collective-permute-start(bf16[264,512]{1,0:T(8,128)(2,1)S(1)} %get-tuple-element.41.first_ref), channel_id=1, source_target_pairs={{0,16},{2,18},{4,20},{6,22},{8,24},{10,26},{12,28},{14,30},{16,0},... | collective-permute-start | bytes 811016 | tf_op jit(solution)/shard_map/ppermute | solution.py:35
  6.5 1.6 %collective-permute-start.7 = (bf16[264,512]{1,0:T(8,128)(2,1)S(1)}, bf16[264,512]{1,0:T(8,128)(2,1)S(1)}, u32[]{:S(2)}, u32[]{:S(2)}) collective-permute-start(bf16[264,512]{1,0:T(8,128)(2,1)S(1)} %get-tuple-element.41.first_ref), channel_id=1, source_target_pairs={{0,8},{2,10},{4,12},{6,14},{8,0},{10,2},{12,4},{14,6},{16,24},{18,... | collective-permute-start | bytes 811016 | tf_op jit(solution)/shard_map/ppermute | solution.py:35
  8.1 1.5 %collective-permute-start.6 = (bf16[264,512]{1,0:T(8,128)(2,1)S(1)}, bf16[264,512]{1,0:T(8,128)(2,1)S(1)}, u32[]{:S(2)}, u32[]{:S(2)}) collective-permute-start(bf16[264,512]{1,0:T(8,128)(2,1)S(1)} %get-tuple-element.41.first_ref), channel_id=1, source_target_pairs={{0,4},{2,6},{4,0},{6,2},{8,12},{10,14},{12,8},{14,10},{16,20},{18,... | collective-permute-start | bytes 811016 | tf_op jit(solution)/shard_map/ppermute | solution.py:35
  9.6 1.4 %load.1 = (bf16[264,1024]{1,0:T(8,128)(2,1)S(1)}, bf16[256,512]{1,0:T(8,128)(2,1)S(1)}, bf16[128,1024]{1,0:T(8,128)(2,1)S(1)}, bf16[128,1024]{1,0:T(8,128)(2,1)S(1)}, bf16[1024,64]{1,0:T(8,128)(2,1)S(1)}) custom-call(bf16[264,512]{1,0:T(8,128)(2,1)S(1)} %get-tuple-element.41.first_ref, bf16[128,1024]{1,0:T(8,128)(2,1)} %bitcast.11, ...), custom_call_target="tpu_custom_call" | custom-call | tf_op jit(solution)/shard_map/load/pallas_call | solution.py:421
  11.1 0.4 collective-permute-start.5
  11.5 0.4 collective-permute-start.4
  11.9 7.8 %collective-permute-done.refs_9_ = bf16[264,512]{1,0:T(8,128)(2,1)S(1)} collective-permute-done((bf16[264,512]{1,0:T(8,128)(2,1)S(1)}, bf16[264,512]{1,0:T(8,128)(2,1)S(1)}, u32[]{:S(2)}, u32[]{:S(2)}) %collective-permute-start) | collective-permute-done | bytes 270368 | tf_op jit(solution)/shard_map/ppermute | solution.py:35
  19.7 1.8 %collective-permute-start.3 = (bf16[256,512]{1,0:T(8,128)(2,1)S(1)}, bf16[256,512]{1,0:T(8,128)(2,1)S(1)}, u32[]{:S(2)}, u32[]{:S(2)}) collective-permute-start(bf16[256,512]{1,0:T(8,128)(2,1)S(1)} %get-tuple-element.48), channel_id=1, source_target_pairs={{0,4},{2,6},{4,0},{6,2},{8,12},{10,14},{12,8},{14,10},{16,20},{18,... | collective-permute-start | bytes 786440 | tf_op jit(solution)/shard_map/ppermute | solution.py:35
  21.5 0.1 collective-permute-done.7.refs_8_
  21.6 0.0 collective-permute-start.1
  21.6 4.0 %attention.2 = (bf16[128,512]{1,0:T(8,128)(2,1)S(1)}, bf16[128,512]{1,0:T(8,128)(2,1)S(1)}, f32[256,512]{1,0:T(8,128)S(1)}, bf16[256,512]{1,0:T(8,128)(2,1)S(1)}...) custom-call(s32[1,128]{1,0:T(1,128)S(1)} %get-tuple-element.39.refs_, ...), custom_call_target="tpu_custom_call" | custom-call | flops 20000000000 | bytes 4194304 | tf_op jit(solution)/shard_map/attention/pallas_call | solution.py:202
  25.6 0.4 collective-permute-start.8
  26.1 0.0 collective-permute-done.1.refs_6_
  26.1 3.6 %collective-permute-start.9 = (bf16[256,512]{1,0:T(8,128)(2,1)S(1)}, bf16[256,512]{1,0:T(8,128)(2,1)S(1)}, u32[]{:S(2)}, u32[]{:S(2)}) collective-permute-start(bf16[256,512]{1,0:T(8,128)(2,1)S(1)} %get-tuple-element.58), channel_id=1, source_target_pairs={{0,16},{2,18},{4,20},{6,22},{8,24},{10,26},{12,28},{14,30},{16,0},... | collective-permute-start | bytes 786440 | tf_op jit(solution)/shard_map/ppermute | solution.py:35
  29.6 1.1 %collective-permute-done.5.refs_9_ = bf16[256,512]{1,0:T(8,128)(2,1)S(1)} collective-permute-done((bf16[256,512]{1,0:T(8,128)(2,1)S(1)}, bf16[256,512]{1,0:T(8,128)(2,1)S(1)}, u32[]{:S(2)}, u32[]{:S(2)}) %collective-permute-start.5) | collective-permute-done | bytes 262176 | tf_op jit(solution)/shard_map/ppermute | solution.py:35
  30.8 2.0 %collective-permute-start.10 = (bf16[256,512]{1,0:T(8,128)(2,1)S(1)}, bf16[256,512]{1,0:T(8,128)(2,1)S(1)}, u32[]{:S(2)}, u32[]{:S(2)}) collective-permute-start(bf16[256,512]{1,0:T(8,128)(2,1)S(1)} %get-tuple-element.59), channel_id=1, source_target_pairs={{0,4},{2,6},{4,0},{6,2},{8,12},{10,14},{12,8},{14,10},{16,20},{18,... | collective-permute-start | bytes 786440 | tf_op jit(solution)/shard_map/ppermute | solution.py:35
  32.8 3.8 %collective-permute-done.4.refs_8_ = bf16[256,512]{1,0:T(8,128)(2,1)S(1)} collective-permute-done((bf16[256,512]{1,0:T(8,128)(2,1)S(1)}, bf16[256,512]{1,0:T(8,128)(2,1)S(1)}, u32[]{:S(2)}, u32[]{:S(2)}) %collective-permute-start.4) | collective-permute-done | bytes 262176 | tf_op jit(solution)/shard_map/ppermute | solution.py:35
  36.6 0.0 collective-permute-done.3.refs_7_
  36.6 4.7 %attention.3 = (bf16[128,1024]{1,0:T(8,128)(2,1)}, bf16[128,1024]{1,0:T(8,128)(2,1)}, f32[256,512]{1,0:T(8,128)S(1)}, bf16[256,512]{1,0:T(8,128)(2,1)}, bf16[256...) custom-call(s32[1,128]{1,0:T(1,128)S(1)} %get-tuple-element.39.refs_0_, ...), custom_call_target="tpu_custom_call" | custom-call | flops 20000000000 | bytes 4194304 | tf_op jit(solution)/shard_map/attention/pallas_call | solution.py:202
  41.4 0.9 %collective-permute-done.8.refs_1_ = bf16[256,512]{1,0:T(8,128)(2,1)S(1)} collective-permute-done((bf16[256,512]{1,0:T(8,128)(2,1)S(1)}, bf16[256,512]{1,0:T(8,128)(2,1)S(1)}, u32[]{:S(2)}, u32[]{:S(2)}) %collective-permute-start.8) | collective-permute-done | bytes 262176 | tf_op jit(solution)/shard_map/ppermute | solution.py:35
  42.3 0.5 collective-permute-start.14
  42.8 1.6 %collective-permute-start.15 = (bf16[256,512]{1,0:T(8,128)(2,1)}, bf16[256,512]{1,0:T(8,128)(2,1)S(1)}, u32[]{:S(2)}, u32[]{:S(2)}) collective-permute-start(bf16[256,512]{1,0:T(8,128)(2,1)} %get-tuple-element.68), channel_id=1, source_target_pairs={{0,4},{2,6},{4,0},{6,2},{8,12},{10,14},{12,8},{14,10},{16,20},{18,... | collective-permute-start | bytes 786440 | tf_op jit(solution)/shard_map/ppermute | solution.py:35
  44.4 4.9 %all-to-all-start = ((f32[32,1,128]{2,1,0:T(1,128)}), f32[32,1,128]{2,1,0:T(1,128)S(1)}, u32[]{:S(2)}, u32[]{:S(2)}) async-start(f32[32,1,128]{2,1,0:T(1,128)} %get-tuple-element.71), calls=%async_computation | async-start | bytes 32768 | tf_op jit(solution)/shard_map/all_to_all | solution.py:478
  49.3 0.1 gather.2.refs_0_
  49.5 3.8 %collective-permute-done.12.refs_1_ = bf16[256,512]{1,0:T(8,128)(2,1)S(1)} collective-permute-done((bf16[256,512]{1,0:T(8,128)(2,1)}, bf16[256,512]{1,0:T(8,128)(2,1)S(1)}, u32[]{:S(2)}, u32[]{:S(2)}) %collective-permute-start.12) | collective-permute-done | bytes 262176 | tf_op jit(solution)/shard_map/ppermute | solution.py:35
  53.3 1.4 %collective-permute-done.13.refs_2_ = bf16[256,512]{1,0:T(8,128)(2,1)S(1)} collective-permute-done((bf16[256,512]{1,0:T(8,128)(2,1)}, bf16[256,512]{1,0:T(8,128)(2,1)S(1)}, u32[]{:S(2)}, u32[]{:S(2)}) %collective-permute-start.13) | collective-permute-done | bytes 262176 | tf_op jit(solution)/shard_map/ppermute | solution.py:35
  54.7 0.1 gather.3.refs_1_
  54.8 0.9 %finish.1 = (bf16[128,1024]{1,0:T(8,128)(2,1)}, bf16[128,1024]{1,0:T(8,128)(2,1)}) custom-call(f32[256,512]{1,0:T(8,128)S(1)} %gather.2.refs_0_, f32[256,512]{1,0:T(8,128)S(1)} %gather.3.refs_1_, bf16[256,512]{1,0:T(8,128)(2,1)S(1)} %collective-permute-done.14.refs_2_, bf16[256,512]{1,0:T(8,128)(2,1)S(1)} %collective-permute-done.15.refs_3_), custom_call_target="tpu_custom_call" | custom-call | flops 524288 | bytes 2097152 | tf_op jit(solution)/shard_map/finish/pallas_call | solution.py:249
  55.6 1.0 %all-to-all-done.gathered_ref = f32[32,1,128]{2,1,0:T(1,128)S(1)} async-done(((f32[32,1,128]{2,1,0:T(1,128)}), f32[32,1,128]{2,1,0:T(1,128)S(1)}, u32[]{:S(2)}, u32[]{:S(2)}) %all-to-all-start) | async-done | bytes 16416 | tf_op jit(solution)/shard_map/all_to_all | solution.py:478
  56.7 1.4 %table.1 = f32[16,64,64]{2,1,0:T(8,128)} custom-call(f32[32,1,128]{2,1,0:T(1,128)S(1)} %all-to-all-done.gathered_ref), custom_call_target="tpu_custom_call" | custom-call | tf_op jit(solution)/shard_map/table/pallas_call | solution.py:314
  (10 shorter events, 0.0 us)
Async XLA Ops:
  2.3 8.7 %collective-permute-start.2 = (bf16[264,512]{1,0:T(8,128)(2,1)S(1)}, bf16[264,512]{1,0:T(8,128)(2,1)S(1)}, u32[]{:S(2)}, u32[]{:S(2)}) collective-permute-start(bf16[264,512]{1,0:T(8,128)(2,1)S(1)} %get-tuple-element.41.first_ref), channel_id=1, source_target_pairs={{0,2},{2,0},{4,6},{6,4},{8,10},{10,8},{12,14},{14,12},{16,18},{18,... | collective-permute-start | bytes 811016 | tf_op jit(solution)/shard_map/ppermute | solution.py:35
  2.8 16.9 %collective-permute-start = (bf16[264,512]{1,0:T(8,128)(2,1)S(1)}, bf16[264,512]{1,0:T(8,128)(2,1)S(1)}, u32[]{:S(2)}, u32[]{:S(2)}) collective-permute-start(bf16[264,512]{1,0:T(8,128)(2,1)S(1)} %get-tuple-element.41.first_ref), channel_id=1, source_target_pairs={{0,16},{2,18},{4,20},{6,22},{8,24},{10,26},{12,28},{14,30},{16,0},... | collective-permute-start | bytes 811016 | tf_op jit(solution)/shard_map/ppermute | solution.py:35
  6.5 15.1 %collective-permute-start.7 = (bf16[264,512]{1,0:T(8,128)(2,1)S(1)}, bf16[264,512]{1,0:T(8,128)(2,1)S(1)}, u32[]{:S(2)}, u32[]{:S(2)}) collective-permute-start(bf16[264,512]{1,0:T(8,128)(2,1)S(1)} %get-tuple-element.41.first_ref), channel_id=1, source_target_pairs={{0,8},{2,10},{4,12},{6,14},{8,0},{10,2},{12,4},{14,6},{16,24},{18,... | collective-permute-start | bytes 811016 | tf_op jit(solution)/shard_map/ppermute | solution.py:35
  8.1 13.5 %collective-permute-start.6 = (bf16[264,512]{1,0:T(8,128)(2,1)S(1)}, bf16[264,512]{1,0:T(8,128)(2,1)S(1)}, u32[]{:S(2)}, u32[]{:S(2)}) collective-permute-start(bf16[264,512]{1,0:T(8,128)(2,1)S(1)} %get-tuple-element.41.first_ref), channel_id=1, source_target_pairs={{0,4},{2,6},{4,0},{6,2},{8,12},{10,14},{12,8},{14,10},{16,20},{18,... | collective-permute-start | bytes 811016 | tf_op jit(solution)/shard_map/ppermute | solution.py:35
  11.1 19.7 %collective-permute-start.5 = (bf16[256,512]{1,0:T(8,128)(2,1)S(1)}, bf16[256,512]{1,0:T(8,128)(2,1)S(1)}, u32[]{:S(2)}, u32[]{:S(2)}) collective-permute-start(bf16[256,512]{1,0:T(8,128)(2,1)S(1)} %get-tuple-element.48), channel_id=1, source_target_pairs={{0,16},{2,18},{4,20},{6,22},{8,24},{10,26},{12,28},{14,30},{16,0},... | collective-permute-start | bytes 786440 | tf_op jit(solution)/shard_map/ppermute | solution.py:35
  11.5 25.2 %collective-permute-start.4 = (bf16[256,512]{1,0:T(8,128)(2,1)S(1)}, bf16[256,512]{1,0:T(8,128)(2,1)S(1)}, u32[]{:S(2)}, u32[]{:S(2)}) collective-permute-start(bf16[256,512]{1,0:T(8,128)(2,1)S(1)} %get-tuple-element.48), channel_id=1, source_target_pairs={{0,8},{2,10},{4,12},{6,14},{8,0},{10,2},{12,4},{14,6},{16,24},{18,... | collective-permute-start | bytes 786440 | tf_op jit(solution)/shard_map/ppermute | solution.py:35
  19.7 16.9 %collective-permute-start.3 = (bf16[256,512]{1,0:T(8,128)(2,1)S(1)}, bf16[256,512]{1,0:T(8,128)(2,1)S(1)}, u32[]{:S(2)}, u32[]{:S(2)}) collective-permute-start(bf16[256,512]{1,0:T(8,128)(2,1)S(1)} %get-tuple-element.48), channel_id=1, source_target_pairs={{0,4},{2,6},{4,0},{6,2},{8,12},{10,14},{12,8},{14,10},{16,20},{18,... | collective-permute-start | bytes 786440 | tf_op jit(solution)/shard_map/ppermute | solution.py:35
  21.6 4.4 %collective-permute-start.1 = (bf16[256,512]{1,0:T(8,128)(2,1)S(1)}, bf16[256,512]{1,0:T(8,128)(2,1)S(1)}, u32[]{:S(2)}, u32[]{:S(2)}) collective-permute-start(bf16[256,512]{1,0:T(8,128)(2,1)S(1)} %get-tuple-element.48), channel_id=1, source_target_pairs={{0,2},{2,0},{4,6},{6,4},{8,10},{10,8},{12,14},{14,12},{16,18},{18,... | collective-permute-start | bytes 786440 | tf_op jit(solution)/shard_map/ppermute | solution.py:35
  25.6 16.7 %collective-permute-start.8 = (bf16[256,512]{1,0:T(8,128)(2,1)S(1)}, bf16[256,512]{1,0:T(8,128)(2,1)S(1)}, u32[]{:S(2)}, u32[]{:S(2)}) collective-permute-start(bf16[256,512]{1,0:T(8,128)(2,1)S(1)} %get-tuple-element.57), channel_id=1, source_target_pairs={{0,8},{2,10},{4,12},{6,14},{8,0},{10,2},{12,4},{14,6},{16,24},{18,... | collective-permute-start | bytes 786440 | tf_op jit(solution)/shard_map/ppermute | solution.py:35
  26.1 16.2 %collective-permute-start.9 = (bf16[256,512]{1,0:T(8,128)(2,1)S(1)}, bf16[256,512]{1,0:T(8,128)(2,1)S(1)}, u32[]{:S(2)}, u32[]{:S(2)}) collective-permute-start(bf16[256,512]{1,0:T(8,128)(2,1)S(1)} %get-tuple-element.58), channel_id=1, source_target_pairs={{0,16},{2,18},{4,20},{6,22},{8,24},{10,26},{12,28},{14,30},{16,0},... | collective-permute-start | bytes 786440 | tf_op jit(solution)/shard_map/ppermute | solution.py:35
  30.8 11.5 %collective-permute-start.10 = (bf16[256,512]{1,0:T(8,128)(2,1)S(1)}, bf16[256,512]{1,0:T(8,128)(2,1)S(1)}, u32[]{:S(2)}, u32[]{:S(2)}) collective-permute-start(bf16[256,512]{1,0:T(8,128)(2,1)S(1)} %get-tuple-element.59), channel_id=1, source_target_pairs={{0,4},{2,6},{4,0},{6,2},{8,12},{10,14},{12,8},{14,10},{16,20},{18,... | collective-permute-start | bytes 786440 | tf_op jit(solution)/shard_map/ppermute | solution.py:35
  41.4 11.9 %collective-permute-start.12 = (bf16[256,512]{1,0:T(8,128)(2,1)}, bf16[256,512]{1,0:T(8,128)(2,1)S(1)}, u32[]{:S(2)}, u32[]{:S(2)}) collective-permute-start(bf16[256,512]{1,0:T(8,128)(2,1)} %get-tuple-element.63), channel_id=1, source_target_pairs={{0,8},{2,10},{4,12},{6,14},{8,0},{10,2},{12,4},{14,6},{16,24},{18,... | collective-permute-start | bytes 786440 | tf_op jit(solution)/shard_map/ppermute | solution.py:35
  41.4 13.3 %collective-permute-start.13 = (bf16[256,512]{1,0:T(8,128)(2,1)}, bf16[256,512]{1,0:T(8,128)(2,1)S(1)}, u32[]{:S(2)}, u32[]{:S(2)}) collective-permute-start(bf16[256,512]{1,0:T(8,128)(2,1)} %get-tuple-element.64), channel_id=1, source_target_pairs={{0,16},{2,18},{4,20},{6,22},{8,24},{10,26},{12,28},{14,30},{16,0},... | collective-permute-start | bytes 786440 | tf_op jit(solution)/shard_map/ppermute | solution.py:35
  42.3 7.0 %collective-permute-start.11 = (bf16[256,512]{1,0:T(8,128)(2,1)S(1)}, bf16[256,512]{1,0:T(8,128)(2,1)S(1)}, u32[]{:S(2)}, u32[]{:S(2)}) collective-permute-start(bf16[256,512]{1,0:T(8,128)(2,1)S(1)} %get-tuple-element.61), channel_id=1, source_target_pairs={{0,2},{2,0},{4,6},{6,4},{8,10},{10,8},{12,14},{14,12},{16,18},{18,... | collective-permute-start | bytes 786440 | tf_op jit(solution)/shard_map/ppermute | solution.py:35
  42.3 12.4 %collective-permute-start.14 = (bf16[256,512]{1,0:T(8,128)(2,1)}, bf16[256,512]{1,0:T(8,128)(2,1)S(1)}, u32[]{:S(2)}, u32[]{:S(2)}) collective-permute-start(bf16[256,512]{1,0:T(8,128)(2,1)} %get-tuple-element.66), channel_id=1, source_target_pairs={{0,2},{2,0},{4,6},{6,4},{8,10},{10,8},{12,14},{14,12},{16,18},{18,... | collective-permute-start | bytes 786440 | tf_op jit(solution)/shard_map/ppermute | solution.py:35
  42.8 12.0 %collective-permute-start.15 = (bf16[256,512]{1,0:T(8,128)(2,1)}, bf16[256,512]{1,0:T(8,128)(2,1)S(1)}, u32[]{:S(2)}, u32[]{:S(2)}) collective-permute-start(bf16[256,512]{1,0:T(8,128)(2,1)} %get-tuple-element.68), channel_id=1, source_target_pairs={{0,4},{2,6},{4,0},{6,2},{8,12},{10,14},{12,8},{14,10},{16,20},{18,... | collective-permute-start | bytes 786440 | tf_op jit(solution)/shard_map/ppermute | solution.py:35
  44.4 12.2 %all-to-all-start = ((f32[32,1,128]{2,1,0:T(1,128)}), f32[32,1,128]{2,1,0:T(1,128)S(1)}, u32[]{:S(2)}, u32[]{:S(2)}) async-start(f32[32,1,128]{2,1,0:T(1,128)} %get-tuple-element.71), calls=%async_computation | async-start | bytes 32768 | tf_op jit(solution)/shard_map/all_to_all | solution.py:478

commit v6 on v5

--- a/solution.py
+++ b/solution.py
@@ -67,8 +67,9 @@
     own_ref, *term_refs, pay_ref = take(1 + section_count)
     if first:
         masks, biases = take(2)
-    half_features = far_refs[0].shape[1]
+    half_features = own_ref.shape[1]
     half_heads = half_features // DH
+    info_row = half_features // PAIR_LANES * 2 * BLK
 
     if first:
         own_bucket = param_ref[INFO : INFO + 1, :]
@@ -80,8 +81,7 @@
                 seg_cols = seg_rows
                 bucket = own_bucket
             else:
-                source = near_refs[s - 1] if s <= near_count else far_refs[s - 1 - near_count]
-                info = source[2 * BLK : 2 * BLK + INFO, 0:LANES].astype(F32)
+                info = far_refs[s - 1][info_row : info_row + INFO, :].astype(F32)
                 seg_cols = info[0:1]
                 bucket = info[1:2]
             cols = jnp.broadcast_to(seg_cols, (BLK, BLK)).T
@@ -107,19 +107,19 @@
             pl.multiple_of(half * half_features + pair * PAIR_LANES, PAIR_LANES), PAIR_LANES
         )
         mine = here if first else there
+        key_block = pl.ds(pl.multiple_of(pair * 2 * BLK, BLK), BLK)
+        value_block = pl.ds(pl.multiple_of(pair * 2 * BLK + BLK, BLK), BLK)
         head = half * half_heads + 2 * pair
         q_stack = split_pair(q_ref[:, there] * jnp.asarray(0.125, BF16), low)
         grad_stack = split_pair(do_ref[:, there], low)
         key_rows = jnp.concatenate(
             [own_pack_ref[0:BLK, there]]
-            + [r[0:BLK, there] for r in near_refs]
-            + [r[0:BLK, here] for r in far_refs],
+            + [r[key_block, :] for r in far_refs],
             axis=0,
         )
         value_rows = jnp.concatenate(
             [own_pack_ref[BLK : 2 * BLK, there]]
-            + [r[BLK : 2 * BLK, there] for r in near_refs]
-            + [r[BLK : 2 * BLK, here] for r in far_refs],
+            + [r[value_block, :] for r in far_refs],
             axis=0,
         )
         raw = contract(key_rows, q_stack, 1, 1)
@@ -332,19 +332,20 @@
 def pack_body(*refs):
     mask_hbm, bucket_hbm, seg_hbm, key_hbm, value_hbm = refs[:5]
     first_ref, seg_ref, param_ref, mask_ref, bucket_ref, sems = refs[5:]
-    half_features = first_ref.shape[1]
+    pairs = (first_ref.shape[0] - INFO) // (2 * BLK)
     small = [(mask_hbm, mask_ref), (bucket_hbm, bucket_ref), (seg_hbm, seg_ref)]
     copies = [
         pltpu.make_async_copy(source, target, sems.at[i]) for i, (source, target) in enumerate(small)
     ]
-    for row, source in ((0, key_hbm), (BLK, value_hbm)):
-        copies.append(
-            pltpu.make_async_copy(
-                source.at[:, pl.ds(0, half_features)],
-                first_ref.at[pl.ds(row, BLK), :],
-                sems.at[len(copies)],
+    for pair in range(pairs):
+        for row, source in ((0, key_hbm), (BLK, value_hbm)):
+            copies.append(
+                pltpu.make_async_copy(
+                    source.at[:, pl.ds(pair * PAIR_LANES, PAIR_LANES)],
+                    first_ref.at[pl.ds(pair * 2 * BLK + row, BLK), :],
+                    sems.at[len(copies)],
+                )
             )
-        )
     for copy in copies:
         copy.start()
     for copy in copies[: len(small)]:
@@ -352,8 +353,7 @@
     top = row_iota((INFO, LANES)) == 0
     bucket = jnp.broadcast_to(bucket_ref[...], (INFO, LANES))
     info = jnp.where(top, seg_ref[...], bucket).astype(F32).astype(BF16)
-    for start in range(0, half_features, LANES):
-        first_ref[2 * BLK : 2 * BLK + INFO, start : start + LANES] = info
+    first_ref[pairs * 2 * BLK : pairs * 2 * BLK + INFO, :] = info
     lines = row_iota((2 * INFO, LANES))
     params = jnp.where(lines == INFO, bucket_ref[...].astype(F32), 0.0)
     for s in range(1, mask_ref.shape[1]):
@@ -365,7 +365,7 @@
 
 
 def pack(mask, bucket, seg, keys, values):
-    row_count, feature_count = keys.shape
+    pairs = keys.shape[1] // HALVES // PAIR_LANES
     vmem = pl.BlockSpec(memory_space=pltpu.VMEM)
     hbm = pl.BlockSpec(memory_space=pltpu.HBM)
     return pl.pallas_call(
@@ -373,14 +373,14 @@
         in_specs=[hbm, pl.BlockSpec(memory_space=pl.ANY), hbm, hbm, hbm],
         out_specs=[vmem] * 3,
         out_shape=[
-            jax.ShapeDtypeStruct((2 * row_count + INFO, feature_count // HALVES), BF16),
+            jax.ShapeDtypeStruct((pairs * 2 * BLK + INFO, PAIR_LANES), BF16),
             jax.ShapeDtypeStruct(seg.shape, jnp.int32),
             jax.ShapeDtypeStruct((2 * INFO, LANES), F32),
         ],
         scratch_shapes=[
             pltpu.VMEM(mask.shape, jnp.int32),
             pltpu.VMEM(bucket.shape, jnp.int32),
-            pltpu.SemaphoreType.DMA((5,)),
+            pltpu.SemaphoreType.DMA((3 + 2 * pairs,)),
         ],
         compiler_params=pltpu.CompilerParams(vmem_limit_bytes=VMEM_LIMIT),
         name="pack",
@@ -390,7 +390,7 @@
 def load_body(first_ref, *refs):
     sources, targets, sems = refs[:5], refs[5:10], refs[10]
     whole_ref, second_ref = targets[:2]
-    half_features = first_ref.shape[1]
+    pairs = second_ref.shape[0] // (2 * BLK)
     copies = []
 
     def add(source, target):
@@ -398,24 +398,23 @@
         copies[-1].start()
 
     for row, source in ((0, sources[0]), (BLK, sources[1])):
+        for pair in range(pairs):
+            window = pl.ds((pairs + pair) * PAIR_LANES, PAIR_LANES)
+            add(source.at[:, window], second_ref.at[pl.ds(pair * 2 * BLK + row, BLK), :])
         add(source, whole_ref.at[pl.ds(row, BLK), :])
-        add(source.at[:, pl.ds(half_features, half_features)], second_ref.at[pl.ds(row, BLK), :])
     for source, target in zip(sources[2:], targets[2:]):
         add(source, target)
-    info = first_ref[2 * BLK : 2 * BLK + INFO, :]
-    for half in range(HALVES):
-        window = slice(half * half_features, (half + 1) * half_features)
-        whole_ref[2 * BLK : 2 * BLK + INFO, window] = info
     for copy in copies:
         copy.wait()
 
 
 def load(first, keys, values, *arrays):
     row_count, feature_count = keys.shape
+    pairs = feature_count // HALVES // PAIR_LANES
     vmem = pl.BlockSpec(memory_space=pltpu.VMEM)
     out_shape = [
-        jax.ShapeDtypeStruct((2 * row_count + INFO, feature_count), BF16),
-        jax.ShapeDtypeStruct((2 * row_count, feature_count // HALVES), BF16),
+        jax.ShapeDtypeStruct((2 * row_count, feature_count), BF16),
+        jax.ShapeDtypeStruct((pairs * 2 * BLK, PAIR_LANES), BF16),
         *[jax.ShapeDtypeStruct(a.shape, a.dtype) for a in arrays],
     ]
     return pl.pallas_call(
@@ -423,7 +422,7 @@
         in_specs=[vmem] + [pl.BlockSpec(memory_space=pltpu.HBM)] * 5,
         out_specs=[vmem] * 5,
         out_shape=out_shape,
-        scratch_shapes=[pltpu.SemaphoreType.DMA((4 + len(arrays),))],
+        scratch_shapes=[pltpu.SemaphoreType.DMA((2 + 2 * pairs + len(arrays),))],
         compiler_params=pltpu.CompilerParams(vmem_limit_bytes=VMEM_LIMIT),
         name="load",
     )(first, *[in_hbm(a) for a in (keys, values, *arrays)])

time: 58.2 us -> 58 us (level)
  transfers between devices with their start and end apart: 17 -> 17, of which waited for: 8 -> 8; matrix products, arithmetic and copies ran while one was open for 0% -> 0% of each run, Pallas kernels for 19% -> 20%
where the time goes in v6:
time: 58 us; the launch traced here: 57.7 us
  starting transfers between devices  23 us (40%)
  waiting for transfers between devices  19.7 us (34%)
  Pallas kernels  13.7 us (24%)
  between operations  1.38 us (2%)
    ppermute x16, waiting for transfers between devices, from_partner(): return lax.ppermute(value, axis, pairs)  18.6 us
    ppermute x16, starting transfers between devices, from_partner(): return lax.ppermute(value, axis, pairs)  18.1 us
    pallas_call x2, Pallas kernels, attention_half(): pl.pallas_call(functools.partial(attention_body, near_count, far_count, h...  8.7 us
    all_to_all x1, starting transfers between devices, local(): gathered = lax.all_to_all(block, ('dp', 'seq'), 0, 0, tiled=True)  4.87 us
    pallas_call x1, Pallas kernels, load(): pl.pallas_call(load_body, in_specs=[vmem] + [pl.BlockSpec(memory_space=pl...  1.52 us
    pallas_call x1, Pallas kernels, table_of(): pl.pallas_call(functools.partial(table_body, section_count), in_specs=[vm...  1.35 us
  transfers between devices with their start and end apart: 17, of which 8 were waited for; matrix products, arithmetic and copies ran while one was open for 0% of the time, Pallas kernels for 20%

profile of v6, /device:TPU:0, one launch (start us, length us, event | category | flops | bytes accessed | tf_op | source)
XLA Modules:
  0.0 57.7 jit_solution(17275199728484639613)
XLA Ops:
  1.3 1.0 %pack.1 = (bf16[1032,128]{1,0:T(8,128)(2,1)S(1)}, s32[1,128]{1,0:T(1,128)S(1)}, f32[16,128]{1,0:T(8,128)S(1)}) custom-call(s32[1,5]{1,0:T(1,128)} %bitcast.17, s32[1,1]{1,0:T(1,128)S(6)} %copy.13.refs_1_, s32[1,128]{1,0:T(1,128)} %refs_2_.1, bf16[128,1024]{1,0:T(8,128)(2,1)} %bitcast.10, bf16[128,1024]{1,0:T(8,128)(2,1)} %bitcast.12), custom_call_target="tpu_custom_call" | custom-call | tf_op jit(solution)/shard_map/pack/pallas_call | solution.py:371
  2.3 0.5 collective-permute-start.2
  2.8 3.7 %collective-permute-start = (bf16[1032,128]{1,0:T(8,128)(2,1)S(1)}, bf16[1032,128]{1,0:T(8,128)(2,1)S(1)}, u32[]{:S(2)}, u32[]{:S(2)}) collective-permute-start(bf16[1032,128]{1,0:T(8,128)(2,1)S(1)} %get-tuple-element.41.first_ref), channel_id=1, source_target_pairs={{0,16},{2,18},{4,20},{6,22},{8,24},{10,26},{12,28},{14,30},{16,0},... | collective-permute-start | bytes 792584 | tf_op jit(solution)/shard_map/ppermute | solution.py:35
  6.5 1.6 %collective-permute-start.7 = (bf16[1032,128]{1,0:T(8,128)(2,1)S(1)}, bf16[1032,128]{1,0:T(8,128)(2,1)S(1)}, u32[]{:S(2)}, u32[]{:S(2)}) collective-permute-start(bf16[1032,128]{1,0:T(8,128)(2,1)S(1)} %get-tuple-element.41.first_ref), channel_id=1, source_target_pairs={{0,8},{2,10},{4,12},{6,14},{8,0},{10,2},{12,4},{14,6},{16,24},{18,... | collective-permute-start | bytes 792584 | tf_op jit(solution)/shard_map/ppermute | solution.py:35
  8.0 1.5 %collective-permute-start.6 = (bf16[1032,128]{1,0:T(8,128)(2,1)S(1)}, bf16[1032,128]{1,0:T(8,128)(2,1)S(1)}, u32[]{:S(2)}, u32[]{:S(2)}) collective-permute-start(bf16[1032,128]{1,0:T(8,128)(2,1)S(1)} %get-tuple-element.41.first_ref), channel_id=1, source_target_pairs={{0,4},{2,6},{4,0},{6,2},{8,12},{10,14},{12,8},{14,10},{16,20},{18,... | collective-permute-start | bytes 792584 | tf_op jit(solution)/shard_map/ppermute | solution.py:35
  9.6 1.5 %load.1 = (bf16[256,1024]{1,0:T(8,128)(2,1)S(1)}, bf16[1024,128]{1,0:T(8,128)(2,1)S(1)}, bf16[128,1024]{1,0:T(8,128)(2,1)S(1)}, bf16[128,1024]{1,0:T(8,128)(2,1)S(1)}, bf16[1024,64]{1,0:T(8,128)(2,1)S(1)}) custom-call(bf16[1032,128]{1,0:T(8,128)(2,1)S(1)} %get-tuple-element.41.first_ref, bf16[128,1024]{1,0:T(8,128)(2,1)} %bitcast.11, ...), custom_call_target="tpu_custom_call" | custom-call | tf_op jit(solution)/shard_map/load/pallas_call | solution.py:420
  11.1 0.4 collective-permute-start.5
  11.5 0.4 collective-permute-start.4
  12.0 7.5 %collective-permute-done.refs_9_ = bf16[1032,128]{1,0:T(8,128)(2,1)S(1)} collective-permute-done((bf16[1032,128]{1,0:T(8,128)(2,1)S(1)}, bf16[1032,128]{1,0:T(8,128)(2,1)S(1)}, u32[]{:S(2)}, u32[]{:S(2)}) %collective-permute-start) | collective-permute-done | bytes 264224 | tf_op jit(solution)/shard_map/ppermute | solution.py:35
  19.4 1.8 %collective-permute-start.3 = (bf16[1024,128]{1,0:T(8,128)(2,1)S(1)}, bf16[1024,128]{1,0:T(8,128)(2,1)S(1)}, u32[]{:S(2)}, u32[]{:S(2)}) collective-permute-start(bf16[1024,128]{1,0:T(8,128)(2,1)S(1)} %get-tuple-element.48), channel_id=1, source_target_pairs={{0,4},{2,6},{4,0},{6,2},{8,12},{10,14},{12,8},{14,10},{16,20},{18,... | collective-permute-start | bytes 786440 | tf_op jit(solution)/shard_map/ppermute | solution.py:35
  21.2 0.1 collective-permute-done.7.refs_8_
  21.3 0.0 collective-permute-start.1
  21.3 0.0 collective-permute-done.6.refs_7_
  21.3 4.0 %attention.2 = (bf16[128,512]{1,0:T(8,128)(2,1)S(1)}, bf16[128,512]{1,0:T(8,128)(2,1)S(1)}, f32[256,512]{1,0:T(8,128)S(1)}, bf16[256,512]{1,0:T(8,128)(2,1)S(1)}...) custom-call(s32[1,128]{1,0:T(1,128)S(1)} %get-tuple-element.39.refs_, ...), custom_call_target="tpu_custom_call" | custom-call | flops 20000000000 | bytes 4194304 | tf_op jit(solution)/shard_map/attention/pallas_call | solution.py:202
  25.3 0.4 collective-permute-start.8
  25.8 3.6 %collective-permute-start.9 = (bf16[256,512]{1,0:T(8,128)(2,1)S(1)}, bf16[256,512]{1,0:T(8,128)(2,1)S(1)}, u32[]{:S(2)}, u32[]{:S(2)}) collective-permute-start(bf16[256,512]{1,0:T(8,128)(2,1)S(1)} %get-tuple-element.58), channel_id=1, source_target_pairs={{0,16},{2,18},{4,20},{6,22},{8,24},{10,26},{12,28},{14,30},{16,0},... | collective-permute-start | bytes 786440 | tf_op jit(solution)/shard_map/ppermute | solution.py:35
  29.3 1.1 %collective-permute-done.5.refs_9_ = bf16[1024,128]{1,0:T(8,128)(2,1)S(1)} collective-permute-done((bf16[1024,128]{1,0:T(8,128)(2,1)S(1)}, bf16[1024,128]{1,0:T(8,128)(2,1)S(1)}, u32[]{:S(2)}, u32[]{:S(2)}) %collective-permute-start.5) | collective-permute-done | bytes 262176 | tf_op jit(solution)/shard_map/ppermute | solution.py:35
  30.5 2.0 %collective-permute-start.10 = (bf16[256,512]{1,0:T(8,128)(2,1)S(1)}, bf16[256,512]{1,0:T(8,128)(2,1)S(1)}, u32[]{:S(2)}, u32[]{:S(2)}) collective-permute-start(bf16[256,512]{1,0:T(8,128)(2,1)S(1)} %get-tuple-element.59), channel_id=1, source_target_pairs={{0,4},{2,6},{4,0},{6,2},{8,12},{10,14},{12,8},{14,10},{16,20},{18,... | collective-permute-start | bytes 786440 | tf_op jit(solution)/shard_map/ppermute | solution.py:35
  32.5 3.8 %collective-permute-done.4.refs_8_ = bf16[1024,128]{1,0:T(8,128)(2,1)S(1)} collective-permute-done((bf16[1024,128]{1,0:T(8,128)(2,1)S(1)}, bf16[1024,128]{1,0:T(8,128)(2,1)S(1)}, u32[]{:S(2)}, u32[]{:S(2)}) %collective-permute-start.4) | collective-permute-done | bytes 262176 | tf_op jit(solution)/shard_map/ppermute | solution.py:35
  36.3 4.7 %attention.3 = (bf16[128,1024]{1,0:T(8,128)(2,1)}, bf16[128,1024]{1,0:T(8,128)(2,1)}, f32[256,512]{1,0:T(8,128)S(1)}, bf16[256,512]{1,0:T(8,128)(2,1)}, bf16[256...) custom-call(s32[1,128]{1,0:T(1,128)S(1)} %get-tuple-element.39.refs_0_, ...), custom_call_target="tpu_custom_call" | custom-call | flops 20000000000 | bytes 4194304 | tf_op jit(solution)/shard_map/attention/pallas_call | solution.py:202
  41.0 0.0 collective-permute-start.12
  41.1 0.9 %collective-permute-done.8.refs_1_ = bf16[256,512]{1,0:T(8,128)(2,1)S(1)} collective-permute-done((bf16[256,512]{1,0:T(8,128)(2,1)S(1)}, bf16[256,512]{1,0:T(8,128)(2,1)S(1)}, u32[]{:S(2)}, u32[]{:S(2)}) %collective-permute-start.8) | collective-permute-done | bytes 262176 | tf_op jit(solution)/shard_map/ppermute | solution.py:35
  42.0 0.5 collective-permute-start.14
  42.5 1.6 %collective-permute-start.15 = (bf16[256,512]{1,0:T(8,128)(2,1)}, bf16[256,512]{1,0:T(8,128)(2,1)S(1)}, u32[]{:S(2)}, u32[]{:S(2)}) collective-permute-start(bf16[256,512]{1,0:T(8,128)(2,1)} %get-tuple-element.68), channel_id=1, source_target_pairs={{0,4},{2,6},{4,0},{6,2},{8,12},{10,14},{12,8},{14,10},{16,20},{18,... | collective-permute-start | bytes 786440 | tf_op jit(solution)/shard_map/ppermute | solution.py:35
  44.1 4.9 %all-to-all-start = ((f32[32,1,128]{2,1,0:T(1,128)}), f32[32,1,128]{2,1,0:T(1,128)S(1)}, u32[]{:S(2)}, u32[]{:S(2)}) async-start(f32[32,1,128]{2,1,0:T(1,128)} %get-tuple-element.71), calls=%async_computation | async-start | bytes 32768 | tf_op jit(solution)/shard_map/all_to_all | solution.py:477
  49.0 0.1 gather.2.refs_0_
  49.2 3.9 %collective-permute-done.12.refs_1_ = bf16[256,512]{1,0:T(8,128)(2,1)S(1)} collective-permute-done((bf16[256,512]{1,0:T(8,128)(2,1)}, bf16[256,512]{1,0:T(8,128)(2,1)S(1)}, u32[]{:S(2)}, u32[]{:S(2)}) %collective-permute-start.12) | collective-permute-done | bytes 262176 | tf_op jit(solution)/shard_map/ppermute | solution.py:35
  53.0 1.2 %collective-permute-done.13.refs_2_ = bf16[256,512]{1,0:T(8,128)(2,1)S(1)} collective-permute-done((bf16[256,512]{1,0:T(8,128)(2,1)}, bf16[256,512]{1,0:T(8,128)(2,1)S(1)}, u32[]{:S(2)}, u32[]{:S(2)}) %collective-permute-start.13) | collective-permute-done | bytes 262176 | tf_op jit(solution)/shard_map/ppermute | solution.py:35
  54.3 0.1 gather.3.refs_1_
  54.4 0.9 %finish.1 = (bf16[128,1024]{1,0:T(8,128)(2,1)}, bf16[128,1024]{1,0:T(8,128)(2,1)}) custom-call(f32[256,512]{1,0:T(8,128)S(1)} %gather.2.refs_0_, f32[256,512]{1,0:T(8,128)S(1)} %gather.3.refs_1_, bf16[256,512]{1,0:T(8,128)(2,1)S(1)} %collective-permute-done.14.refs_2_, bf16[256,512]{1,0:T(8,128)(2,1)S(1)} %collective-permute-done.15.refs_3_), custom_call_target="tpu_custom_call" | custom-call | flops 524288 | bytes 2097152 | tf_op jit(solution)/shard_map/finish/pallas_call | solution.py:249
  55.2 1.1 %all-to-all-done.gathered_ref = f32[32,1,128]{2,1,0:T(1,128)S(1)} async-done(((f32[32,1,128]{2,1,0:T(1,128)}), f32[32,1,128]{2,1,0:T(1,128)S(1)}, u32[]{:S(2)}, u32[]{:S(2)}) %all-to-all-start) | async-done | bytes 16416 | tf_op jit(solution)/shard_map/all_to_all | solution.py:477
  56.3 1.4 %table.1 = f32[16,64,64]{2,1,0:T(8,128)} custom-call(f32[32,1,128]{2,1,0:T(1,128)S(1)} %all-to-all-done.gathered_ref), custom_call_target="tpu_custom_call" | custom-call | tf_op jit(solution)/shard_map/table/pallas_call | solution.py:314
  (10 shorter events, 0.0 us)
Async XLA Ops:
  2.3 8.8 %collective-permute-start.2 = (bf16[1032,128]{1,0:T(8,128)(2,1)S(1)}, bf16[1032,128]{1,0:T(8,128)(2,1)S(1)}, u32[]{:S(2)}, u32[]{:S(2)}) collective-permute-start(bf16[1032,128]{1,0:T(8,128)(2,1)S(1)} %get-tuple-element.41.first_ref), channel_id=1, source_target_pairs={{0,2},{2,0},{4,6},{6,4},{8,10},{10,8},{12,14},{14,12},{16,18},{18,... | collective-permute-start | bytes 792584 | tf_op jit(solution)/shard_map/ppermute | solution.py:35
  2.8 16.6 %collective-permute-start = (bf16[1032,128]{1,0:T(8,128)(2,1)S(1)}, bf16[1032,128]{1,0:T(8,128)(2,1)S(1)}, u32[]{:S(2)}, u32[]{:S(2)}) collective-permute-start(bf16[1032,128]{1,0:T(8,128)(2,1)S(1)} %get-tuple-element.41.first_ref), channel_id=1, source_target_pairs={{0,16},{2,18},{4,20},{6,22},{8,24},{10,26},{12,28},{14,30},{16,0},... | collective-permute-start | bytes 792584 | tf_op jit(solution)/shard_map/ppermute | solution.py:35
  6.5 14.9 %collective-permute-start.7 = (bf16[1032,128]{1,0:T(8,128)(2,1)S(1)}, bf16[1032,128]{1,0:T(8,128)(2,1)S(1)}, u32[]{:S(2)}, u32[]{:S(2)}) collective-permute-start(bf16[1032,128]{1,0:T(8,128)(2,1)S(1)} %get-tuple-element.41.first_ref), channel_id=1, source_target_pairs={{0,8},{2,10},{4,12},{6,14},{8,0},{10,2},{12,4},{14,6},{16,24},{18,... | collective-permute-start | bytes 792584 | tf_op jit(solution)/shard_map/ppermute | solution.py:35
  8.0 13.3 %collective-permute-start.6 = (bf16[1032,128]{1,0:T(8,128)(2,1)S(1)}, bf16[1032,128]{1,0:T(8,128)(2,1)S(1)}, u32[]{:S(2)}, u32[]{:S(2)}) collective-permute-start(bf16[1032,128]{1,0:T(8,128)(2,1)S(1)} %get-tuple-element.41.first_ref), channel_id=1, source_target_pairs={{0,4},{2,6},{4,0},{6,2},{8,12},{10,14},{12,8},{14,10},{16,20},{18,... | collective-permute-start | bytes 792584 | tf_op jit(solution)/shard_map/ppermute | solution.py:35
  11.1 19.3 %collective-permute-start.5 = (bf16[1024,128]{1,0:T(8,128)(2,1)S(1)}, bf16[1024,128]{1,0:T(8,128)(2,1)S(1)}, u32[]{:S(2)}, u32[]{:S(2)}) collective-permute-start(bf16[1024,128]{1,0:T(8,128)(2,1)S(1)} %get-tuple-element.48), channel_id=1, source_target_pairs={{0,16},{2,18},{4,20},{6,22},{8,24},{10,26},{12,28},{14,30},{16,0},... | collective-permute-start | bytes 786440 | tf_op jit(solution)/shard_map/ppermute | solution.py:35
  11.5 24.8 %collective-permute-start.4 = (bf16[1024,128]{1,0:T(8,128)(2,1)S(1)}, bf16[1024,128]{1,0:T(8,128)(2,1)S(1)}, u32[]{:S(2)}, u32[]{:S(2)}) collective-permute-start(bf16[1024,128]{1,0:T(8,128)(2,1)S(1)} %get-tuple-element.48), channel_id=1, source_target_pairs={{0,8},{2,10},{4,12},{6,14},{8,0},{10,2},{12,4},{14,6},{16,24},{18,... | collective-permute-start | bytes 786440 | tf_op jit(solution)/shard_map/ppermute | solution.py:35
  19.4 16.9 %collective-permute-start.3 = (bf16[1024,128]{1,0:T(8,128)(2,1)S(1)}, bf16[1024,128]{1,0:T(8,128)(2,1)S(1)}, u32[]{:S(2)}, u32[]{:S(2)}) collective-permute-start(bf16[1024,128]{1,0:T(8,128)(2,1)S(1)} %get-tuple-element.48), channel_id=1, source_target_pairs={{0,4},{2,6},{4,0},{6,2},{8,12},{10,14},{12,8},{14,10},{16,20},{18,... | collective-permute-start | bytes 786440 | tf_op jit(solution)/shard_map/ppermute | solution.py:35
  21.3 4.4 %collective-permute-start.1 = (bf16[1024,128]{1,0:T(8,128)(2,1)S(1)}, bf16[1024,128]{1,0:T(8,128)(2,1)S(1)}, u32[]{:S(2)}, u32[]{:S(2)}) collective-permute-start(bf16[1024,128]{1,0:T(8,128)(2,1)S(1)} %get-tuple-element.48), channel_id=1, source_target_pairs={{0,2},{2,0},{4,6},{6,4},{8,10},{10,8},{12,14},{14,12},{16,18},{18,... | collective-permute-start | bytes 786440 | tf_op jit(solution)/shard_map/ppermute | solution.py:35
  25.3 16.7 %collective-permute-start.8 = (bf16[256,512]{1,0:T(8,128)(2,1)S(1)}, bf16[256,512]{1,0:T(8,128)(2,1)S(1)}, u32[]{:S(2)}, u32[]{:S(2)}) collective-permute-start(bf16[256,512]{1,0:T(8,128)(2,1)S(1)} %get-tuple-element.57), channel_id=1, source_target_pairs={{0,8},{2,10},{4,12},{6,14},{8,0},{10,2},{12,4},{14,6},{16,24},{18,... | collective-permute-start | bytes 786440 | tf_op jit(solution)/shard_map/ppermute | solution.py:35
  25.8 16.2 %collective-permute-start.9 = (bf16[256,512]{1,0:T(8,128)(2,1)S(1)}, bf16[256,512]{1,0:T(8,128)(2,1)S(1)}, u32[]{:S(2)}, u32[]{:S(2)}) collective-permute-start(bf16[256,512]{1,0:T(8,128)(2,1)S(1)} %get-tuple-element.58), channel_id=1, source_target_pairs={{0,16},{2,18},{4,20},{6,22},{8,24},{10,26},{12,28},{14,30},{16,0},... | collective-permute-start | bytes 786440 | tf_op jit(solution)/shard_map/ppermute | solution.py:35
  30.5 11.5 %collective-permute-start.10 = (bf16[256,512]{1,0:T(8,128)(2,1)S(1)}, bf16[256,512]{1,0:T(8,128)(2,1)S(1)}, u32[]{:S(2)}, u32[]{:S(2)}) collective-permute-start(bf16[256,512]{1,0:T(8,128)(2,1)S(1)} %get-tuple-element.59), channel_id=1, source_target_pairs={{0,4},{2,6},{4,0},{6,2},{8,12},{10,14},{12,8},{14,10},{16,20},{18,... | collective-permute-start | bytes 786440 | tf_op jit(solution)/shard_map/ppermute | solution.py:35
  41.0 12.0 %collective-permute-start.12 = (bf16[256,512]{1,0:T(8,128)(2,1)}, bf16[256,512]{1,0:T(8,128)(2,1)S(1)}, u32[]{:S(2)}, u32[]{:S(2)}) collective-permute-start(bf16[256,512]{1,0:T(8,128)(2,1)} %get-tuple-element.63), channel_id=1, source_target_pairs={{0,8},{2,10},{4,12},{6,14},{8,0},{10,2},{12,4},{14,6},{16,24},{18,... | collective-permute-start | bytes 786440 | tf_op jit(solution)/shard_map/ppermute | solution.py:35
  41.0 13.2 %collective-permute-start.13 = (bf16[256,512]{1,0:T(8,128)(2,1)}, bf16[256,512]{1,0:T(8,128)(2,1)S(1)}, u32[]{:S(2)}, u32[]{:S(2)}) collective-permute-start(bf16[256,512]{1,0:T(8,128)(2,1)} %get-tuple-element.64), channel_id=1, source_target_pairs={{0,16},{2,18},{4,20},{6,22},{8,24},{10,26},{12,28},{14,30},{16,0},... | collective-permute-start | bytes 786440 | tf_op jit(solution)/shard_map/ppermute | solution.py:35
  42.0 7.0 %collective-permute-start.11 = (bf16[256,512]{1,0:T(8,128)(2,1)S(1)}, bf16[256,512]{1,0:T(8,128)(2,1)S(1)}, u32[]{:S(2)}, u32[]{:S(2)}) collective-permute-start(bf16[256,512]{1,0:T(8,128)(2,1)S(1)} %get-tuple-element.61), channel_id=1, source_target_pairs={{0,2},{2,0},{4,6},{6,4},{8,10},{10,8},{12,14},{14,12},{16,18},{18,... | collective-permute-start | bytes 786440 | tf_op jit(solution)/shard_map/ppermute | solution.py:35
  42.0 12.3 %collective-permute-start.14 = (bf16[256,512]{1,0:T(8,128)(2,1)}, bf16[256,512]{1,0:T(8,128)(2,1)S(1)}, u32[]{:S(2)}, u32[]{:S(2)}) collective-permute-start(bf16[256,512]{1,0:T(8,128)(2,1)} %get-tuple-element.66), channel_id=1, source_target_pairs={{0,2},{2,0},{4,6},{6,4},{8,10},{10,8},{12,14},{14,12},{16,18},{18,... | collective-permute-start | bytes 786440 | tf_op jit(solution)/shard_map/ppermute | solution.py:35
  42.5 11.8 %collective-permute-start.15 = (bf16[256,512]{1,0:T(8,128)(2,1)}, bf16[256,512]{1,0:T(8,128)(2,1)S(1)}, u32[]{:S(2)}, u32[]{:S(2)}) collective-permute-start(bf16[256,512]{1,0:T(8,128)(2,1)} %get-tuple-element.68), channel_id=1, source_target_pairs={{0,4},{2,6},{4,0},{6,2},{8,12},{10,14},{12,8},{14,10},{16,20},{18,... | collective-permute-start | bytes 786440 | tf_op jit(solution)/shard_map/ppermute | solution.py:35
  44.1 12.2 %all-to-all-start = ((f32[32,1,128]{2,1,0:T(1,128)}), f32[32,1,128]{2,1,0:T(1,128)S(1)}, u32[]{:S(2)}, u32[]{:S(2)}) async-start(f32[32,1,128]{2,1,0:T(1,128)} %get-tuple-element.71), calls=%async_computation | async-start | bytes 32768 | tf_op jit(solution)/shard_map/all_to_all | solution.py:477

commit v7 on v6

--- a/solution.py
+++ b/solution.py
@@ -18,6 +18,7 @@
 BUCKET_LANE = 112
 MASKED = -1e30
 TABLE_ROWS = 32
+TABLE_HEADS = 4
 UNROLL = 4
 VMEM_LIMIT = 16 * 2**20
 FLOPS = 2 * 10**10
@@ -282,10 +283,10 @@
             start = (2 * s + part) * count
             masked.append((wide[start : start + count] * hot).astype(BF16))
     rows = jnp.concatenate([row_hot] * (2 * section_count), axis=0)
-    return contract(rows, jnp.concatenate(masked, axis=0), 0, 0)
-
-
-def table_body(section_count, gathered_ref, table_ref, scratch, total):
+    return rows, jnp.concatenate(masked, axis=0)
+
+
+def table_body(section_count, gathered_ref, table_ref, scratch, total, staged, sems):
     count = gathered_ref.shape[0]
 
     def copy_row(row, carry):
@@ -294,19 +295,37 @@
 
     lax.fori_loop(0, count, copy_row, 0, unroll=8)
     if count <= TABLE_ROWS:
-        table = table_part(section_count, scratch[...])
+        rows, spread = table_part(section_count, scratch[...])
+
+        def columns(window):
+            return contract(rows, spread[:, window], 0, 0)
+
     else:
         total[...] = jnp.zeros_like(total)
 
         def add_part(step, carry):
             start = pl.multiple_of(step * TABLE_ROWS, TABLE_ROWS)
-            total[...] += table_part(section_count, scratch[pl.ds(start, TABLE_ROWS), :])
+            rows, spread = table_part(section_count, scratch[pl.ds(start, TABLE_ROWS), :])
+            total[...] += contract(rows, spread, 0, 0)
             return carry
 
         lax.fori_loop(0, count // TABLE_ROWS, add_part, 0)
-        table = total[...]
-    for head in range(H):
-        table_ref[head] = table[:, head * NB : (head + 1) * NB]
+
+        def columns(window):
+            return total[:, window]
+
+    copies = []
+    for group in range(H // TABLE_HEADS):
+        part = columns(slice(group * TABLE_HEADS * NB, (group + 1) * TABLE_HEADS * NB))
+        heads = pl.ds(group * TABLE_HEADS, TABLE_HEADS)
+        for head in range(TABLE_HEADS):
+            staged[group * TABLE_HEADS + head] = part[:, head * NB : (head + 1) * NB]
+        copies.append(
+            pltpu.make_async_copy(staged.at[heads], table_ref.at[heads], sems.at[group])
+        )
+        copies[-1].start()
+    for copy in copies:
+        copy.wait()
 
 
 def table_of(gathered, section_count):
@@ -314,11 +333,13 @@
     return pl.pallas_call(
         functools.partial(table_body, section_count),
         in_specs=[vmem],
-        out_specs=vmem,
+        out_specs=pl.BlockSpec(memory_space=pltpu.HBM),
         out_shape=jax.ShapeDtypeStruct((H, NB, NB), F32),
         scratch_shapes=[
             pltpu.VMEM((gathered.shape[0], LANES), F32),
             pltpu.VMEM((NB, H * NB), F32),
+            pltpu.VMEM((H, NB, NB), F32),
+            pltpu.SemaphoreType.DMA((H // TABLE_HEADS,)),
         ],
         compiler_params=pltpu.CompilerParams(vmem_limit_bytes=VMEM_LIMIT),
         name="table",
@@ -330,10 +351,9 @@
 
 
 def pack_body(*refs):
-    mask_hbm, bucket_hbm, seg_hbm, key_hbm, value_hbm = refs[:5]
-    first_ref, seg_ref, param_ref, mask_ref, bucket_ref, sems = refs[5:]
+    bucket_hbm, seg_hbm, key_hbm, value_hbm, first_ref, seg_ref, bucket_ref, sems = refs
     pairs = (first_ref.shape[0] - INFO) // (2 * BLK)
-    small = [(mask_hbm, mask_ref), (bucket_hbm, bucket_ref), (seg_hbm, seg_ref)]
+    small = [(bucket_hbm, bucket_ref), (seg_hbm, seg_ref)]
     copies = [
         pltpu.make_async_copy(source, target, sems.at[i]) for i, (source, target) in enumerate(small)
     ]
@@ -354,41 +374,35 @@
     bucket = jnp.broadcast_to(bucket_ref[...], (INFO, LANES))
     info = jnp.where(top, seg_ref[...], bucket).astype(F32).astype(BF16)
     first_ref[pairs * 2 * BLK : pairs * 2 * BLK + INFO, :] = info
-    lines = row_iota((2 * INFO, LANES))
-    params = jnp.where(lines == INFO, bucket_ref[...].astype(F32), 0.0)
-    for s in range(1, mask_ref.shape[1]):
-        shut = jnp.where(mask_ref[:, s : s + 1] != 0, 0.0, MASKED)
-        params = jnp.where(lines == s, shut, params)
-    param_ref[...] = params
     for copy in copies[len(small) :]:
         copy.wait()
 
 
-def pack(mask, bucket, seg, keys, values):
+def pack(bucket, seg, keys, values):
     pairs = keys.shape[1] // HALVES // PAIR_LANES
     vmem = pl.BlockSpec(memory_space=pltpu.VMEM)
     hbm = pl.BlockSpec(memory_space=pltpu.HBM)
     return pl.pallas_call(
         pack_body,
-        in_specs=[hbm, pl.BlockSpec(memory_space=pl.ANY), hbm, hbm, hbm],
-        out_specs=[vmem] * 3,
+        in_specs=[pl.BlockSpec(memory_space=pl.ANY), hbm, hbm, hbm],
+        out_specs=[vmem] * 2,
         out_shape=[
             jax.ShapeDtypeStruct((pairs * 2 * BLK + INFO, PAIR_LANES), BF16),
             jax.ShapeDtypeStruct(seg.shape, jnp.int32),
-            jax.ShapeDtypeStruct((2 * INFO, LANES), F32),
         ],
         scratch_shapes=[
-            pltpu.VMEM(mask.shape, jnp.int32),
             pltpu.VMEM(bucket.shape, jnp.int32),
-            pltpu.SemaphoreType.DMA((3 + 2 * pairs,)),
+            pltpu.SemaphoreType.DMA((2 + 2 * pairs,)),
         ],
         compiler_params=pltpu.CompilerParams(vmem_limit_bytes=VMEM_LIMIT),
         name="pack",
-    )(*[bucket if a is bucket else in_hbm(a) for a in (mask, bucket, seg, keys, values)])
+    )(bucket, *[in_hbm(a) for a in (seg, keys, values)])
 
 
 def load_body(first_ref, *refs):
-    sources, targets, sems = refs[:5], refs[5:10], refs[10]
+    mask_hbm, *sources = refs[:6]
+    param_ref, *targets = refs[6:12]
+    mask_ref, sems = refs[12:]
     whole_ref, second_ref = targets[:2]
     pairs = second_ref.shape[0] // (2 * BLK)
     copies = []
@@ -397,6 +411,7 @@
         copies.append(pltpu.make_async_copy(source, target, sems.at[len(copies)]))
         copies[-1].start()
 
+    add(mask_hbm, mask_ref)
     for row, source in ((0, sources[0]), (BLK, sources[1])):
         for pair in range(pairs):
             window = pl.ds((pairs + pair) * PAIR_LANES, PAIR_LANES)
@@ -404,28 +419,40 @@
         add(source, whole_ref.at[pl.ds(row, BLK), :])
     for source, target in zip(sources[2:], targets[2:]):
         add(source, target)
-    for copy in copies:
+    copies[0].wait()
+    lines = row_iota((2 * INFO, LANES))
+    bucket = first_ref[pairs * 2 * BLK : pairs * 2 * BLK + INFO, :].astype(F32)[1:2]
+    params = jnp.where(lines == INFO, bucket, 0.0)
+    for s in range(1, mask_ref.shape[1]):
+        shut = jnp.where(mask_ref[:, s : s + 1] != 0, 0.0, MASKED)
+        params = jnp.where(lines == s, shut, params)
+    param_ref[...] = params
+    for copy in copies[1:]:
         copy.wait()
 
 
-def load(first, keys, values, *arrays):
+def load(first, mask, keys, values, *arrays):
     row_count, feature_count = keys.shape
     pairs = feature_count // HALVES // PAIR_LANES
     vmem = pl.BlockSpec(memory_space=pltpu.VMEM)
     out_shape = [
+        jax.ShapeDtypeStruct((2 * INFO, LANES), F32),
         jax.ShapeDtypeStruct((2 * row_count, feature_count), BF16),
         jax.ShapeDtypeStruct((pairs * 2 * BLK, PAIR_LANES), BF16),
         *[jax.ShapeDtypeStruct(a.shape, a.dtype) for a in arrays],
     ]
     return pl.pallas_call(
         load_body,
-        in_specs=[vmem] + [pl.BlockSpec(memory_space=pltpu.HBM)] * 5,
-        out_specs=[vmem] * 5,
+        in_specs=[vmem] + [pl.BlockSpec(memory_space=pltpu.HBM)] * 6,
+        out_specs=[vmem] * 6,
         out_shape=out_shape,
-        scratch_shapes=[pltpu.SemaphoreType.DMA((2 + 2 * pairs + len(arrays),))],
+        scratch_shapes=[
+            pltpu.VMEM(mask.shape, jnp.int32),
+            pltpu.SemaphoreType.DMA((3 + 2 * pairs + len(arrays),)),
+        ],
         compiler_params=pltpu.CompilerParams(vmem_limit_bytes=VMEM_LIMIT),
         name="load",
-    )(first, *[in_hbm(a) for a in (keys, values, *arrays)])
+    )(first, *[in_hbm(a) for a in (mask, keys, values, *arrays)])
 
 
 def after(value, *earlier):
@@ -444,12 +471,17 @@
     def send(value, level):
         return from_partner(value, "seq", 1 << level)
 
-    first, *scalars = pack(
-        block_mask.reshape(1, -1), block_bucket, segment_ids, keys[0], values[0]
+    first, seg = pack(block_bucket, segment_ids, keys[0], values[0])
+    params, whole, second, query_rows, grad_rows, table_rows = load(
+        first,
+        block_mask.reshape(1, -1),
+        keys[0],
+        values[0],
+        queries[0],
+        d_out[0],
+        bias_table.reshape(H * NB, NB),
     )
-    whole, second, query_rows, grad_rows, table_rows = load(
-        first, keys[0], values[0], queries[0], d_out[0], bias_table.reshape(H * NB, NB)
-    )
+    scalars = (seg, params)
     rows = [query_rows, grad_rows, whole]
     far = [{}, {}]
     for level in reversed(far_levels):

time: 58 us -> 57.9 us (level)
  no operation moved by 1% of the time
where the time goes in v7:
time: 57.9 us; the launch traced here: 57.6 us
  starting transfers between devices  23 us (40%)
  waiting for transfers between devices  19.7 us (34%)
  Pallas kernels  13.6 us (23%)
  between operations  1.38 us (2%)
    ppermute x16, waiting for transfers between devices, from_partner(): return lax.ppermute(value, axis, pairs)  18.6 us
    ppermute x16, starting transfers between devices, from_partner(): return lax.ppermute(value, axis, pairs)  18.1 us
    pallas_call x2, Pallas kernels, attention_half(): pl.pallas_call(functools.partial(attention_body, near_count, far_count, h...  8.7 us
    all_to_all x1, starting transfers between devices, local(): gathered = lax.all_to_all(block, ('dp', 'seq'), 0, 0, tiled=True)  4.87 us
    pallas_call x1, Pallas kernels, load(): pl.pallas_call(load_body, in_specs=[vmem] + [pl.BlockSpec(memory_space=pl...  1.55 us
    pallas_call x1, Pallas kernels, table_of(): pl.pallas_call(functools.partial(table_body, section_count), in_specs=[vm...  1.3 us
  transfers between devices with their start and end apart: 17, of which 8 were waited for; matrix products, arithmetic and copies ran while one was open for 0% of the time, Pallas kernels for 20%

profile of v7, /device:TPU:0, one launch (start us, length us, event | category | flops | bytes accessed | tf_op | source)
XLA Modules:
  0.0 57.6 jit_solution(1776844860455775807)
XLA Ops:
  1.3 1.0 %pack.1 = (bf16[1032,128]{1,0:T(8,128)(2,1)S(1)}, s32[1,128]{1,0:T(1,128)S(1)}) custom-call(s32[1,1]{1,0:T(1,128)S(6)} %copy.13.refs_0_, s32[1,128]{1,0:T(1,128)} %refs_1_.1, bf16[128,1024]{1,0:T(8,128)(2,1)} %bitcast.10, bf16[128,1024]{1,0:T(8,128)(2,1)} %bitcast.12), custom_call_target="tpu_custom_call" | custom-call | tf_op jit(solution)/shard_map/pack/pallas_call | solution.py:385
  2.3 0.5 collective-permute-start.2
  2.8 3.7 %collective-permute-start = (bf16[1032,128]{1,0:T(8,128)(2,1)S(1)}, bf16[1032,128]{1,0:T(8,128)(2,1)S(1)}, u32[]{:S(2)}, u32[]{:S(2)}) collective-permute-start(bf16[1032,128]{1,0:T(8,128)(2,1)S(1)} %get-tuple-element.40.first_ref), channel_id=1, source_target_pairs={{0,16},{2,18},{4,20},{6,22},{8,24},{10,26},{12,28},{14,30},{16,0},... | collective-permute-start | bytes 792584 | tf_op jit(solution)/shard_map/ppermute | solution.py:36
  6.5 1.6 %collective-permute-start.7 = (bf16[1032,128]{1,0:T(8,128)(2,1)S(1)}, bf16[1032,128]{1,0:T(8,128)(2,1)S(1)}, u32[]{:S(2)}, u32[]{:S(2)}) collective-permute-start(bf16[1032,128]{1,0:T(8,128)(2,1)S(1)} %get-tuple-element.40.first_ref), channel_id=1, source_target_pairs={{0,8},{2,10},{4,12},{6,14},{8,0},{10,2},{12,4},{14,6},{16,24},{18,... | collective-permute-start | bytes 792584 | tf_op jit(solution)/shard_map/ppermute | solution.py:36
  8.0 1.5 %collective-permute-start.6 = (bf16[1032,128]{1,0:T(8,128)(2,1)S(1)}, bf16[1032,128]{1,0:T(8,128)(2,1)S(1)}, u32[]{:S(2)}, u32[]{:S(2)}) collective-permute-start(bf16[1032,128]{1,0:T(8,128)(2,1)S(1)} %get-tuple-element.40.first_ref), channel_id=1, source_target_pairs={{0,4},{2,6},{4,0},{6,2},{8,12},{10,14},{12,8},{14,10},{16,20},{18,... | collective-permute-start | bytes 792584 | tf_op jit(solution)/shard_map/ppermute | solution.py:36
  9.5 1.5 %load.1 = (f32[16,128]{1,0:T(8,128)S(1)}, bf16[256,1024]{1,0:T(8,128)(2,1)S(1)}, bf16[1024,128]{1,0:T(8,128)(2,1)S(1)}, bf16[128,1024]{1,0:T(8,128)(2,1)S(1)}, b...) custom-call(bf16[1032,128]{1,0:T(8,128)(2,1)S(1)} %get-tuple-element.40.first_ref, s32[1,5]{1,0:T(1,128)} %bitcast.17, ...), custom_call_target="tpu_custom_call" | custom-call | tf_op jit(solution)/shard_map/load/pallas_call | solution.py:444
  11.1 0.0 collective-permute-done.2.refs_6_
  11.1 0.4 collective-permute-start.5
  11.5 0.4 collective-permute-start.4
  12.0 7.4 %collective-permute-done.refs_9_ = bf16[1032,128]{1,0:T(8,128)(2,1)S(1)} collective-permute-done((bf16[1032,128]{1,0:T(8,128)(2,1)S(1)}, bf16[1032,128]{1,0:T(8,128)(2,1)S(1)}, u32[]{:S(2)}, u32[]{:S(2)}) %collective-permute-start) | collective-permute-done | bytes 264224 | tf_op jit(solution)/shard_map/ppermute | solution.py:36
  19.4 1.8 %collective-permute-start.3 = (bf16[1024,128]{1,0:T(8,128)(2,1)S(1)}, bf16[1024,128]{1,0:T(8,128)(2,1)S(1)}, u32[]{:S(2)}, u32[]{:S(2)}) collective-permute-start(bf16[1024,128]{1,0:T(8,128)(2,1)S(1)} %get-tuple-element.48), channel_id=1, source_target_pairs={{0,4},{2,6},{4,0},{6,2},{8,12},{10,14},{12,8},{14,10},{16,20},{18,... | collective-permute-start | bytes 786440 | tf_op jit(solution)/shard_map/ppermute | solution.py:36
  21.2 0.1 collective-permute-done.7.refs_8_
  21.3 4.0 %attention.2 = (bf16[128,512]{1,0:T(8,128)(2,1)S(1)}, bf16[128,512]{1,0:T(8,128)(2,1)S(1)}, f32[256,512]{1,0:T(8,128)S(1)}, bf16[256,512]{1,0:T(8,128)(2,1)S(1)}...) custom-call(s32[1,128]{1,0:T(1,128)S(1)} %get-tuple-element.39.refs_, ...), custom_call_target="tpu_custom_call" | custom-call | flops 20000000000 | bytes 4194304 | tf_op jit(solution)/shard_map/attention/pallas_call | solution.py:203
  25.3 0.4 collective-permute-start.8
  25.7 0.0 collective-permute-done.1.refs_6_
  25.7 3.6 %collective-permute-start.9 = (bf16[256,512]{1,0:T(8,128)(2,1)S(1)}, bf16[256,512]{1,0:T(8,128)(2,1)S(1)}, u32[]{:S(2)}, u32[]{:S(2)}) collective-permute-start(bf16[256,512]{1,0:T(8,128)(2,1)S(1)} %get-tuple-element.58), channel_id=1, source_target_pairs={{0,16},{2,18},{4,20},{6,22},{8,24},{10,26},{12,28},{14,30},{16,0},... | collective-permute-start | bytes 786440 | tf_op jit(solution)/shard_map/ppermute | solution.py:36
  29.3 1.1 %collective-permute-done.5.refs_9_ = bf16[1024,128]{1,0:T(8,128)(2,1)S(1)} collective-permute-done((bf16[1024,128]{1,0:T(8,128)(2,1)S(1)}, bf16[1024,128]{1,0:T(8,128)(2,1)S(1)}, u32[]{:S(2)}, u32[]{:S(2)}) %collective-permute-start.5) | collective-permute-done | bytes 262176 | tf_op jit(solution)/shard_map/ppermute | solution.py:36
  30.4 2.0 %collective-permute-start.10 = (bf16[256,512]{1,0:T(8,128)(2,1)S(1)}, bf16[256,512]{1,0:T(8,128)(2,1)S(1)}, u32[]{:S(2)}, u32[]{:S(2)}) collective-permute-start(bf16[256,512]{1,0:T(8,128)(2,1)S(1)} %get-tuple-element.59), channel_id=1, source_target_pairs={{0,4},{2,6},{4,0},{6,2},{8,12},{10,14},{12,8},{14,10},{16,20},{18,... | collective-permute-start | bytes 786440 | tf_op jit(solution)/shard_map/ppermute | solution.py:36
  32.5 3.8 %collective-permute-done.4.refs_8_ = bf16[1024,128]{1,0:T(8,128)(2,1)S(1)} collective-permute-done((bf16[1024,128]{1,0:T(8,128)(2,1)S(1)}, bf16[1024,128]{1,0:T(8,128)(2,1)S(1)}, u32[]{:S(2)}, u32[]{:S(2)}) %collective-permute-start.4) | collective-permute-done | bytes 262176 | tf_op jit(solution)/shard_map/ppermute | solution.py:36
  36.3 4.7 %attention.3 = (bf16[128,1024]{1,0:T(8,128)(2,1)}, bf16[128,1024]{1,0:T(8,128)(2,1)}, f32[256,512]{1,0:T(8,128)S(1)}, bf16[256,512]{1,0:T(8,128)(2,1)}, bf16[256...) custom-call(s32[1,128]{1,0:T(1,128)S(1)} %get-tuple-element.39.refs_0_, ...), custom_call_target="tpu_custom_call" | custom-call | flops 20000000000 | bytes 4194304 | tf_op jit(solution)/shard_map/attention/pallas_call | solution.py:203
  41.0 0.0 collective-permute-start.12
  41.0 0.9 %collective-permute-done.8.refs_1_ = bf16[256,512]{1,0:T(8,128)(2,1)S(1)} collective-permute-done((bf16[256,512]{1,0:T(8,128)(2,1)S(1)}, bf16[256,512]{1,0:T(8,128)(2,1)S(1)}, u32[]{:S(2)}, u32[]{:S(2)}) %collective-permute-start.8) | collective-permute-done | bytes 262176 | tf_op jit(solution)/shard_map/ppermute | solution.py:36
  42.0 0.5 collective-permute-start.14
  42.5 1.6 %collective-permute-start.15 = (bf16[256,512]{1,0:T(8,128)(2,1)}, bf16[256,512]{1,0:T(8,128)(2,1)S(1)}, u32[]{:S(2)}, u32[]{:S(2)}) collective-permute-start(bf16[256,512]{1,0:T(8,128)(2,1)} %get-tuple-element.68), channel_id=1, source_target_pairs={{0,4},{2,6},{4,0},{6,2},{8,12},{10,14},{12,8},{14,10},{16,20},{18,... | collective-permute-start | bytes 786440 | tf_op jit(solution)/shard_map/ppermute | solution.py:36
  44.1 4.9 %all-to-all-start = ((f32[32,1,128]{2,1,0:T(1,128)}), f32[32,1,128]{2,1,0:T(1,128)S(1)}, u32[]{:S(2)}, u32[]{:S(2)}) async-start(f32[32,1,128]{2,1,0:T(1,128)} %get-tuple-element.71), calls=%async_computation | async-start | bytes 32768 | tf_op jit(solution)/shard_map/all_to_all | solution.py:509
  49.0 0.1 gather.2.refs_0_
  49.2 3.9 %collective-permute-done.12.refs_1_ = bf16[256,512]{1,0:T(8,128)(2,1)S(1)} collective-permute-done((bf16[256,512]{1,0:T(8,128)(2,1)}, bf16[256,512]{1,0:T(8,128)(2,1)S(1)}, u32[]{:S(2)}, u32[]{:S(2)}) %collective-permute-start.12) | collective-permute-done | bytes 262176 | tf_op jit(solution)/shard_map/ppermute | solution.py:36
  53.0 1.2 %collective-permute-done.13.refs_2_ = bf16[256,512]{1,0:T(8,128)(2,1)S(1)} collective-permute-done((bf16[256,512]{1,0:T(8,128)(2,1)}, bf16[256,512]{1,0:T(8,128)(2,1)S(1)}, u32[]{:S(2)}, u32[]{:S(2)}) %collective-permute-start.13) | collective-permute-done | bytes 262176 | tf_op jit(solution)/shard_map/ppermute | solution.py:36
  54.2 0.1 gather.3.refs_1_
  54.3 0.9 %finish.1 = (bf16[128,1024]{1,0:T(8,128)(2,1)}, bf16[128,1024]{1,0:T(8,128)(2,1)}) custom-call(f32[256,512]{1,0:T(8,128)S(1)} %gather.2.refs_0_, f32[256,512]{1,0:T(8,128)S(1)} %gather.3.refs_1_, bf16[256,512]{1,0:T(8,128)(2,1)S(1)} %collective-permute-done.14.refs_2_, bf16[256,512]{1,0:T(8,128)(2,1)S(1)} %collective-permute-done.15.refs_3_), custom_call_target="tpu_custom_call" | custom-call | flops 524288 | bytes 2097152 | tf_op jit(solution)/shard_map/finish/pallas_call | solution.py:250
  55.2 1.1 %all-to-all-done.gathered_ref = f32[32,1,128]{2,1,0:T(1,128)S(1)} async-done(((f32[32,1,128]{2,1,0:T(1,128)}), f32[32,1,128]{2,1,0:T(1,128)S(1)}, u32[]{:S(2)}, u32[]{:S(2)}) %all-to-all-start) | async-done | bytes 16416 | tf_op jit(solution)/shard_map/all_to_all | solution.py:509
  56.3 1.3 %table.1 = f32[16,64,64]{2,1,0:T(8,128)} custom-call(f32[32,1,128]{2,1,0:T(1,128)S(1)} %all-to-all-done.gathered_ref), custom_call_target="tpu_custom_call" | custom-call | tf_op jit(solution)/shard_map/table/pallas_call | solution.py:333
  (10 shorter events, 0.0 us)
Async XLA Ops:
  2.3 8.8 %collective-permute-start.2 = (bf16[1032,128]{1,0:T(8,128)(2,1)S(1)}, bf16[1032,128]{1,0:T(8,128)(2,1)S(1)}, u32[]{:S(2)}, u32[]{:S(2)}) collective-permute-start(bf16[1032,128]{1,0:T(8,128)(2,1)S(1)} %get-tuple-element.40.first_ref), channel_id=1, source_target_pairs={{0,2},{2,0},{4,6},{6,4},{8,10},{10,8},{12,14},{14,12},{16,18},{18,... | collective-permute-start | bytes 792584 | tf_op jit(solution)/shard_map/ppermute | solution.py:36
  2.8 16.6 %collective-permute-start = (bf16[1032,128]{1,0:T(8,128)(2,1)S(1)}, bf16[1032,128]{1,0:T(8,128)(2,1)S(1)}, u32[]{:S(2)}, u32[]{:S(2)}) collective-permute-start(bf16[1032,128]{1,0:T(8,128)(2,1)S(1)} %get-tuple-element.40.first_ref), channel_id=1, source_target_pairs={{0,16},{2,18},{4,20},{6,22},{8,24},{10,26},{12,28},{14,30},{16,0},... | collective-permute-start | bytes 792584 | tf_op jit(solution)/shard_map/ppermute | solution.py:36
  6.5 14.9 %collective-permute-start.7 = (bf16[1032,128]{1,0:T(8,128)(2,1)S(1)}, bf16[1032,128]{1,0:T(8,128)(2,1)S(1)}, u32[]{:S(2)}, u32[]{:S(2)}) collective-permute-start(bf16[1032,128]{1,0:T(8,128)(2,1)S(1)} %get-tuple-element.40.first_ref), channel_id=1, source_target_pairs={{0,8},{2,10},{4,12},{6,14},{8,0},{10,2},{12,4},{14,6},{16,24},{18,... | collective-permute-start | bytes 792584 | tf_op jit(solution)/shard_map/ppermute | solution.py:36
  8.0 13.3 %collective-permute-start.6 = (bf16[1032,128]{1,0:T(8,128)(2,1)S(1)}, bf16[1032,128]{1,0:T(8,128)(2,1)S(1)}, u32[]{:S(2)}, u32[]{:S(2)}) collective-permute-start(bf16[1032,128]{1,0:T(8,128)(2,1)S(1)} %get-tuple-element.40.first_ref), channel_id=1, source_target_pairs={{0,4},{2,6},{4,0},{6,2},{8,12},{10,14},{12,8},{14,10},{16,20},{18,... | collective-permute-start | bytes 792584 | tf_op jit(solution)/shard_map/ppermute | solution.py:36
  11.1 19.3 %collective-permute-start.5 = (bf16[1024,128]{1,0:T(8,128)(2,1)S(1)}, bf16[1024,128]{1,0:T(8,128)(2,1)S(1)}, u32[]{:S(2)}, u32[]{:S(2)}) collective-permute-start(bf16[1024,128]{1,0:T(8,128)(2,1)S(1)} %get-tuple-element.48), channel_id=1, source_target_pairs={{0,16},{2,18},{4,20},{6,22},{8,24},{10,26},{12,28},{14,30},{16,0},... | collective-permute-start | bytes 786440 | tf_op jit(solution)/shard_map/ppermute | solution.py:36
  11.5 24.8 %collective-permute-start.4 = (bf16[1024,128]{1,0:T(8,128)(2,1)S(1)}, bf16[1024,128]{1,0:T(8,128)(2,1)S(1)}, u32[]{:S(2)}, u32[]{:S(2)}) collective-permute-start(bf16[1024,128]{1,0:T(8,128)(2,1)S(1)} %get-tuple-element.48), channel_id=1, source_target_pairs={{0,8},{2,10},{4,12},{6,14},{8,0},{10,2},{12,4},{14,6},{16,24},{18,... | collective-permute-start | bytes 786440 | tf_op jit(solution)/shard_map/ppermute | solution.py:36
  19.4 16.9 %collective-permute-start.3 = (bf16[1024,128]{1,0:T(8,128)(2,1)S(1)}, bf16[1024,128]{1,0:T(8,128)(2,1)S(1)}, u32[]{:S(2)}, u32[]{:S(2)}) collective-permute-start(bf16[1024,128]{1,0:T(8,128)(2,1)S(1)} %get-tuple-element.48), channel_id=1, source_target_pairs={{0,4},{2,6},{4,0},{6,2},{8,12},{10,14},{12,8},{14,10},{16,20},{18,... | collective-permute-start | bytes 786440 | tf_op jit(solution)/shard_map/ppermute | solution.py:36
  21.3 4.4 %collective-permute-start.1 = (bf16[1024,128]{1,0:T(8,128)(2,1)S(1)}, bf16[1024,128]{1,0:T(8,128)(2,1)S(1)}, u32[]{:S(2)}, u32[]{:S(2)}) collective-permute-start(bf16[1024,128]{1,0:T(8,128)(2,1)S(1)} %get-tuple-element.48), channel_id=1, source_target_pairs={{0,2},{2,0},{4,6},{6,4},{8,10},{10,8},{12,14},{14,12},{16,18},{18,... | collective-permute-start | bytes 786440 | tf_op jit(solution)/shard_map/ppermute | solution.py:36
  25.3 16.7 %collective-permute-start.8 = (bf16[256,512]{1,0:T(8,128)(2,1)S(1)}, bf16[256,512]{1,0:T(8,128)(2,1)S(1)}, u32[]{:S(2)}, u32[]{:S(2)}) collective-permute-start(bf16[256,512]{1,0:T(8,128)(2,1)S(1)} %get-tuple-element.57), channel_id=1, source_target_pairs={{0,8},{2,10},{4,12},{6,14},{8,0},{10,2},{12,4},{14,6},{16,24},{18,... | collective-permute-start | bytes 786440 | tf_op jit(solution)/shard_map/ppermute | solution.py:36
  25.7 16.2 %collective-permute-start.9 = (bf16[256,512]{1,0:T(8,128)(2,1)S(1)}, bf16[256,512]{1,0:T(8,128)(2,1)S(1)}, u32[]{:S(2)}, u32[]{:S(2)}) collective-permute-start(bf16[256,512]{1,0:T(8,128)(2,1)S(1)} %get-tuple-element.58), channel_id=1, source_target_pairs={{0,16},{2,18},{4,20},{6,22},{8,24},{10,26},{12,28},{14,30},{16,0},... | collective-permute-start | bytes 786440 | tf_op jit(solution)/shard_map/ppermute | solution.py:36
  30.4 11.5 %collective-permute-start.10 = (bf16[256,512]{1,0:T(8,128)(2,1)S(1)}, bf16[256,512]{1,0:T(8,128)(2,1)S(1)}, u32[]{:S(2)}, u32[]{:S(2)}) collective-permute-start(bf16[256,512]{1,0:T(8,128)(2,1)S(1)} %get-tuple-element.59), channel_id=1, source_target_pairs={{0,4},{2,6},{4,0},{6,2},{8,12},{10,14},{12,8},{14,10},{16,20},{18,... | collective-permute-start | bytes 786440 | tf_op jit(solution)/shard_map/ppermute | solution.py:36
  41.0 12.0 %collective-permute-start.12 = (bf16[256,512]{1,0:T(8,128)(2,1)}, bf16[256,512]{1,0:T(8,128)(2,1)S(1)}, u32[]{:S(2)}, u32[]{:S(2)}) collective-permute-start(bf16[256,512]{1,0:T(8,128)(2,1)} %get-tuple-element.63), channel_id=1, source_target_pairs={{0,8},{2,10},{4,12},{6,14},{8,0},{10,2},{12,4},{14,6},{16,24},{18,... | collective-permute-start | bytes 786440 | tf_op jit(solution)/shard_map/ppermute | solution.py:36
  41.0 13.2 %collective-permute-start.13 = (bf16[256,512]{1,0:T(8,128)(2,1)}, bf16[256,512]{1,0:T(8,128)(2,1)S(1)}, u32[]{:S(2)}, u32[]{:S(2)}) collective-permute-start(bf16[256,512]{1,0:T(8,128)(2,1)} %get-tuple-element.64), channel_id=1, source_target_pairs={{0,16},{2,18},{4,20},{6,22},{8,24},{10,26},{12,28},{14,30},{16,0},... | collective-permute-start | bytes 786440 | tf_op jit(solution)/shard_map/ppermute | solution.py:36
  42.0 7.0 %collective-permute-start.11 = (bf16[256,512]{1,0:T(8,128)(2,1)S(1)}, bf16[256,512]{1,0:T(8,128)(2,1)S(1)}, u32[]{:S(2)}, u32[]{:S(2)}) collective-permute-start(bf16[256,512]{1,0:T(8,128)(2,1)S(1)} %get-tuple-element.61), channel_id=1, source_target_pairs={{0,2},{2,0},{4,6},{6,4},{8,10},{10,8},{12,14},{14,12},{16,18},{18,... | collective-permute-start | bytes 786440 | tf_op jit(solution)/shard_map/ppermute | solution.py:36
  42.0 12.3 %collective-permute-start.14 = (bf16[256,512]{1,0:T(8,128)(2,1)}, bf16[256,512]{1,0:T(8,128)(2,1)S(1)}, u32[]{:S(2)}, u32[]{:S(2)}) collective-permute-start(bf16[256,512]{1,0:T(8,128)(2,1)} %get-tuple-element.66), channel_id=1, source_target_pairs={{0,2},{2,0},{4,6},{6,4},{8,10},{10,8},{12,14},{14,12},{16,18},{18,... | collective-permute-start | bytes 786440 | tf_op jit(solution)/shard_map/ppermute | solution.py:36
  42.5 11.8 %collective-permute-start.15 = (bf16[256,512]{1,0:T(8,128)(2,1)}, bf16[256,512]{1,0:T(8,128)(2,1)S(1)}, u32[]{:S(2)}, u32[]{:S(2)}) collective-permute-start(bf16[256,512]{1,0:T(8,128)(2,1)} %get-tuple-element.68), channel_id=1, source_target_pairs={{0,4},{2,6},{4,0},{6,2},{8,12},{10,14},{12,8},{14,10},{16,20},{18,... | collective-permute-start | bytes 786440 | tf_op jit(solution)/shard_map/ppermute | solution.py:36
  44.1 12.2 %all-to-all-start = ((f32[32,1,128]{2,1,0:T(1,128)}), f32[32,1,128]{2,1,0:T(1,128)S(1)}, u32[]{:S(2)}, u32[]{:S(2)}) async-start(f32[32,1,128]{2,1,0:T(1,128)} %get-tuple-element.71), calls=%async_computation | async-start | bytes 32768 | tf_op jit(solution)/shard_map/all_to_all | solution.py:509

commit v8 on v7

--- a/solution.py
+++ b/solution.py
@@ -20,7 +20,7 @@
 TABLE_ROWS = 32
 TABLE_HEADS = 4
 UNROLL = 4
-VMEM_LIMIT = 16 * 2**20
+VMEM_LIMIT = 10 * 2**20
 FLOPS = 2 * 10**10
 
 F32 = jnp.float32

time: 57.9 us -> 57.9 us (level)
  no operation moved by 1% of the time
where the time goes in v8:
time: 57.9 us; the launch traced here: 57.6 us
  starting transfers between devices  23 us (40%)
  waiting for transfers between devices  19.7 us (34%)
  Pallas kernels  13.6 us (23%)
  between operations  1.38 us (2%)
    ppermute x16, waiting for transfers between devices, from_partner(): return lax.ppermute(value, axis, pairs)  18.6 us
    ppermute x16, starting transfers between devices, from_partner(): return lax.ppermute(value, axis, pairs)  18.1 us
    pallas_call x2, Pallas kernels, attention_half(): pl.pallas_call(functools.partial(attention_body, near_count, far_count, h...  8.7 us
    all_to_all x1, starting transfers between devices, local(): gathered = lax.all_to_all(block, ('dp', 'seq'), 0, 0, tiled=True)  4.87 us
    pallas_call x1, Pallas kernels, load(): pl.pallas_call(load_body, in_specs=[vmem] + [pl.BlockSpec(memory_space=pl...  1.55 us
    pallas_call x1, Pallas kernels, table_of(): pl.pallas_call(functools.partial(table_body, section_count), in_specs=[vm...  1.3 us
  transfers between devices with their start and end apart: 17, of which 8 were waited for; matrix products, arithmetic and copies ran while one was open for 0% of the time, Pallas kernels for 20%

profile of v8, /device:TPU:0, one launch (start us, length us, event | category | flops | bytes accessed | tf_op | source)
XLA Modules:
  0.0 57.6 jit_solution(8032195611410230447)
XLA Ops:
  1.3 1.0 %pack.1 = (bf16[1032,128]{1,0:T(8,128)(2,1)S(1)}, s32[1,128]{1,0:T(1,128)S(1)}) custom-call(s32[1,1]{1,0:T(1,128)S(6)} %copy.13.refs_0_, s32[1,128]{1,0:T(1,128)} %refs_1_.1, bf16[128,1024]{1,0:T(8,128)(2,1)} %bitcast.10, bf16[128,1024]{1,0:T(8,128)(2,1)} %bitcast.12), custom_call_target="tpu_custom_call" | custom-call | tf_op jit(solution)/shard_map/pack/pallas_call | solution.py:385
  2.3 0.5 collective-permute-start.2
  2.8 3.7 %collective-permute-start = (bf16[1032,128]{1,0:T(8,128)(2,1)S(1)}, bf16[1032,128]{1,0:T(8,128)(2,1)S(1)}, u32[]{:S(2)}, u32[]{:S(2)}) collective-permute-start(bf16[1032,128]{1,0:T(8,128)(2,1)S(1)} %get-tuple-element.40.first_ref), channel_id=1, source_target_pairs={{0,16},{2,18},{4,20},{6,22},{8,24},{10,26},{12,28},{14,30},{16,0},... | collective-permute-start | bytes 792584 | tf_op jit(solution)/shard_map/ppermute | solution.py:36
  6.5 1.6 %collective-permute-start.7 = (bf16[1032,128]{1,0:T(8,128)(2,1)S(1)}, bf16[1032,128]{1,0:T(8,128)(2,1)S(1)}, u32[]{:S(2)}, u32[]{:S(2)}) collective-permute-start(bf16[1032,128]{1,0:T(8,128)(2,1)S(1)} %get-tuple-element.40.first_ref), channel_id=1, source_target_pairs={{0,8},{2,10},{4,12},{6,14},{8,0},{10,2},{12,4},{14,6},{16,24},{18,... | collective-permute-start | bytes 792584 | tf_op jit(solution)/shard_map/ppermute | solution.py:36
  8.0 1.5 %collective-permute-start.6 = (bf16[1032,128]{1,0:T(8,128)(2,1)S(1)}, bf16[1032,128]{1,0:T(8,128)(2,1)S(1)}, u32[]{:S(2)}, u32[]{:S(2)}) collective-permute-start(bf16[1032,128]{1,0:T(8,128)(2,1)S(1)} %get-tuple-element.40.first_ref), channel_id=1, source_target_pairs={{0,4},{2,6},{4,0},{6,2},{8,12},{10,14},{12,8},{14,10},{16,20},{18,... | collective-permute-start | bytes 792584 | tf_op jit(solution)/shard_map/ppermute | solution.py:36
  9.5 1.5 %load.1 = (f32[16,128]{1,0:T(8,128)S(1)}, bf16[256,1024]{1,0:T(8,128)(2,1)S(1)}, bf16[1024,128]{1,0:T(8,128)(2,1)S(1)}, bf16[128,1024]{1,0:T(8,128)(2,1)S(1)}, b...) custom-call(bf16[1032,128]{1,0:T(8,128)(2,1)S(1)} %get-tuple-element.40.first_ref, s32[1,5]{1,0:T(1,128)} %bitcast.17, ...), custom_call_target="tpu_custom_call" | custom-call | tf_op jit(solution)/shard_map/load/pallas_call | solution.py:444
  11.1 0.0 collective-permute-done.2.refs_6_
  11.1 0.4 collective-permute-start.5
  11.5 0.4 collective-permute-start.4
  12.0 7.4 %collective-permute-done.refs_9_ = bf16[1032,128]{1,0:T(8,128)(2,1)S(1)} collective-permute-done((bf16[1032,128]{1,0:T(8,128)(2,1)S(1)}, bf16[1032,128]{1,0:T(8,128)(2,1)S(1)}, u32[]{:S(2)}, u32[]{:S(2)}) %collective-permute-start) | collective-permute-done | bytes 264224 | tf_op jit(solution)/shard_map/ppermute | solution.py:36
  19.4 1.8 %collective-permute-start.3 = (bf16[1024,128]{1,0:T(8,128)(2,1)S(1)}, bf16[1024,128]{1,0:T(8,128)(2,1)S(1)}, u32[]{:S(2)}, u32[]{:S(2)}) collective-permute-start(bf16[1024,128]{1,0:T(8,128)(2,1)S(1)} %get-tuple-element.48), channel_id=1, source_target_pairs={{0,4},{2,6},{4,0},{6,2},{8,12},{10,14},{12,8},{14,10},{16,20},{18,... | collective-permute-start | bytes 786440 | tf_op jit(solution)/shard_map/ppermute | solution.py:36
  21.2 0.1 collective-permute-done.7.refs_8_
  21.3 4.0 %attention.2 = (bf16[128,512]{1,0:T(8,128)(2,1)S(1)}, bf16[128,512]{1,0:T(8,128)(2,1)S(1)}, f32[256,512]{1,0:T(8,128)S(1)}, bf16[256,512]{1,0:T(8,128)(2,1)S(1)}...) custom-call(s32[1,128]{1,0:T(1,128)S(1)} %get-tuple-element.39.refs_, ...), custom_call_target="tpu_custom_call" | custom-call | flops 20000000000 | bytes 4194304 | tf_op jit(solution)/shard_map/attention/pallas_call | solution.py:203
  25.3 0.4 collective-permute-start.8
  25.7 0.0 collective-permute-done.1.refs_6_
  25.7 3.6 %collective-permute-start.9 = (bf16[256,512]{1,0:T(8,128)(2,1)S(1)}, bf16[256,512]{1,0:T(8,128)(2,1)S(1)}, u32[]{:S(2)}, u32[]{:S(2)}) collective-permute-start(bf16[256,512]{1,0:T(8,128)(2,1)S(1)} %get-tuple-element.58), channel_id=1, source_target_pairs={{0,16},{2,18},{4,20},{6,22},{8,24},{10,26},{12,28},{14,30},{16,0},... | collective-permute-start | bytes 786440 | tf_op jit(solution)/shard_map/ppermute | solution.py:36
  29.3 1.1 %collective-permute-done.5.refs_9_ = bf16[1024,128]{1,0:T(8,128)(2,1)S(1)} collective-permute-done((bf16[1024,128]{1,0:T(8,128)(2,1)S(1)}, bf16[1024,128]{1,0:T(8,128)(2,1)S(1)}, u32[]{:S(2)}, u32[]{:S(2)}) %collective-permute-start.5) | collective-permute-done | bytes 262176 | tf_op jit(solution)/shard_map/ppermute | solution.py:36
  30.4 2.0 %collective-permute-start.10 = (bf16[256,512]{1,0:T(8,128)(2,1)S(1)}, bf16[256,512]{1,0:T(8,128)(2,1)S(1)}, u32[]{:S(2)}, u32[]{:S(2)}) collective-permute-start(bf16[256,512]{1,0:T(8,128)(2,1)S(1)} %get-tuple-element.59), channel_id=1, source_target_pairs={{0,4},{2,6},{4,0},{6,2},{8,12},{10,14},{12,8},{14,10},{16,20},{18,... | collective-permute-start | bytes 786440 | tf_op jit(solution)/shard_map/ppermute | solution.py:36
  32.5 3.8 %collective-permute-done.4.refs_8_ = bf16[1024,128]{1,0:T(8,128)(2,1)S(1)} collective-permute-done((bf16[1024,128]{1,0:T(8,128)(2,1)S(1)}, bf16[1024,128]{1,0:T(8,128)(2,1)S(1)}, u32[]{:S(2)}, u32[]{:S(2)}) %collective-permute-start.4) | collective-permute-done | bytes 262176 | tf_op jit(solution)/shard_map/ppermute | solution.py:36
  36.3 4.7 %attention.3 = (bf16[128,1024]{1,0:T(8,128)(2,1)}, bf16[128,1024]{1,0:T(8,128)(2,1)}, f32[256,512]{1,0:T(8,128)S(1)}, bf16[256,512]{1,0:T(8,128)(2,1)}, bf16[256...) custom-call(s32[1,128]{1,0:T(1,128)S(1)} %get-tuple-element.39.refs_0_, ...), custom_call_target="tpu_custom_call" | custom-call | flops 20000000000 | bytes 4194304 | tf_op jit(solution)/shard_map/attention/pallas_call | solution.py:203
  41.0 0.0 collective-permute-start.12
  41.0 0.9 %collective-permute-done.8.refs_1_ = bf16[256,512]{1,0:T(8,128)(2,1)S(1)} collective-permute-done((bf16[256,512]{1,0:T(8,128)(2,1)S(1)}, bf16[256,512]{1,0:T(8,128)(2,1)S(1)}, u32[]{:S(2)}, u32[]{:S(2)}) %collective-permute-start.8) | collective-permute-done | bytes 262176 | tf_op jit(solution)/shard_map/ppermute | solution.py:36
  42.0 0.5 collective-permute-start.14
  42.5 1.6 %collective-permute-start.15 = (bf16[256,512]{1,0:T(8,128)(2,1)}, bf16[256,512]{1,0:T(8,128)(2,1)S(1)}, u32[]{:S(2)}, u32[]{:S(2)}) collective-permute-start(bf16[256,512]{1,0:T(8,128)(2,1)} %get-tuple-element.68), channel_id=1, source_target_pairs={{0,4},{2,6},{4,0},{6,2},{8,12},{10,14},{12,8},{14,10},{16,20},{18,... | collective-permute-start | bytes 786440 | tf_op jit(solution)/shard_map/ppermute | solution.py:36
  44.1 4.9 %all-to-all-start = ((f32[32,1,128]{2,1,0:T(1,128)}), f32[32,1,128]{2,1,0:T(1,128)S(1)}, u32[]{:S(2)}, u32[]{:S(2)}) async-start(f32[32,1,128]{2,1,0:T(1,128)} %get-tuple-element.71), calls=%async_computation | async-start | bytes 32768 | tf_op jit(solution)/shard_map/all_to_all | solution.py:509
  49.0 0.1 gather.2.refs_0_
  49.2 3.9 %collective-permute-done.12.refs_1_ = bf16[256,512]{1,0:T(8,128)(2,1)S(1)} collective-permute-done((bf16[256,512]{1,0:T(8,128)(2,1)}, bf16[256,512]{1,0:T(8,128)(2,1)S(1)}, u32[]{:S(2)}, u32[]{:S(2)}) %collective-permute-start.12) | collective-permute-done | bytes 262176 | tf_op jit(solution)/shard_map/ppermute | solution.py:36
  53.0 1.2 %collective-permute-done.13.refs_2_ = bf16[256,512]{1,0:T(8,128)(2,1)S(1)} collective-permute-done((bf16[256,512]{1,0:T(8,128)(2,1)}, bf16[256,512]{1,0:T(8,128)(2,1)S(1)}, u32[]{:S(2)}, u32[]{:S(2)}) %collective-permute-start.13) | collective-permute-done | bytes 262176 | tf_op jit(solution)/shard_map/ppermute | solution.py:36
  54.2 0.1 gather.3.refs_1_
  54.3 0.9 %finish.1 = (bf16[128,1024]{1,0:T(8,128)(2,1)}, bf16[128,1024]{1,0:T(8,128)(2,1)}) custom-call(f32[256,512]{1,0:T(8,128)S(1)} %gather.2.refs_0_, f32[256,512]{1,0:T(8,128)S(1)} %gather.3.refs_1_, bf16[256,512]{1,0:T(8,128)(2,1)S(1)} %collective-permute-done.14.refs_2_, bf16[256,512]{1,0:T(8,128)(2,1)S(1)} %collective-permute-done.15.refs_3_), custom_call_target="tpu_custom_call" | custom-call | flops 524288 | bytes 2097152 | tf_op jit(solution)/shard_map/finish/pallas_call | solution.py:250
  55.2 1.1 %all-to-all-done.gathered_ref = f32[32,1,128]{2,1,0:T(1,128)S(1)} async-done(((f32[32,1,128]{2,1,0:T(1,128)}), f32[32,1,128]{2,1,0:T(1,128)S(1)}, u32[]{:S(2)}, u32[]{:S(2)}) %all-to-all-start) | async-done | bytes 16416 | tf_op jit(solution)/shard_map/all_to_all | solution.py:509
  56.3 1.3 %table.1 = f32[16,64,64]{2,1,0:T(8,128)} custom-call(f32[32,1,128]{2,1,0:T(1,128)S(1)} %all-to-all-done.gathered_ref), custom_call_target="tpu_custom_call" | custom-call | tf_op jit(solution)/shard_map/table/pallas_call | solution.py:333
  (10 shorter events, 0.0 us)
Async XLA Ops:
  2.3 8.8 %collective-permute-start.2 = (bf16[1032,128]{1,0:T(8,128)(2,1)S(1)}, bf16[1032,128]{1,0:T(8,128)(2,1)S(1)}, u32[]{:S(2)}, u32[]{:S(2)}) collective-permute-start(bf16[1032,128]{1,0:T(8,128)(2,1)S(1)} %get-tuple-element.40.first_ref), channel_id=1, source_target_pairs={{0,2},{2,0},{4,6},{6,4},{8,10},{10,8},{12,14},{14,12},{16,18},{18,... | collective-permute-start | bytes 792584 | tf_op jit(solution)/shard_map/ppermute | solution.py:36
  2.8 16.6 %collective-permute-start = (bf16[1032,128]{1,0:T(8,128)(2,1)S(1)}, bf16[1032,128]{1,0:T(8,128)(2,1)S(1)}, u32[]{:S(2)}, u32[]{:S(2)}) collective-permute-start(bf16[1032,128]{1,0:T(8,128)(2,1)S(1)} %get-tuple-element.40.first_ref), channel_id=1, source_target_pairs={{0,16},{2,18},{4,20},{6,22},{8,24},{10,26},{12,28},{14,30},{16,0},... | collective-permute-start | bytes 792584 | tf_op jit(solution)/shard_map/ppermute | solution.py:36
  6.5 14.9 %collective-permute-start.7 = (bf16[1032,128]{1,0:T(8,128)(2,1)S(1)}, bf16[1032,128]{1,0:T(8,128)(2,1)S(1)}, u32[]{:S(2)}, u32[]{:S(2)}) collective-permute-start(bf16[1032,128]{1,0:T(8,128)(2,1)S(1)} %get-tuple-element.40.first_ref), channel_id=1, source_target_pairs={{0,8},{2,10},{4,12},{6,14},{8,0},{10,2},{12,4},{14,6},{16,24},{18,... | collective-permute-start | bytes 792584 | tf_op jit(solution)/shard_map/ppermute | solution.py:36
  8.0 13.3 %collective-permute-start.6 = (bf16[1032,128]{1,0:T(8,128)(2,1)S(1)}, bf16[1032,128]{1,0:T(8,128)(2,1)S(1)}, u32[]{:S(2)}, u32[]{:S(2)}) collective-permute-start(bf16[1032,128]{1,0:T(8,128)(2,1)S(1)} %get-tuple-element.40.first_ref), channel_id=1, source_target_pairs={{0,4},{2,6},{4,0},{6,2},{8,12},{10,14},{12,8},{14,10},{16,20},{18,... | collective-permute-start | bytes 792584 | tf_op jit(solution)/shard_map/ppermute | solution.py:36
  11.1 19.3 %collective-permute-start.5 = (bf16[1024,128]{1,0:T(8,128)(2,1)S(1)}, bf16[1024,128]{1,0:T(8,128)(2,1)S(1)}, u32[]{:S(2)}, u32[]{:S(2)}) collective-permute-start(bf16[1024,128]{1,0:T(8,128)(2,1)S(1)} %get-tuple-element.48), channel_id=1, source_target_pairs={{0,16},{2,18},{4,20},{6,22},{8,24},{10,26},{12,28},{14,30},{16,0},... | collective-permute-start | bytes 786440 | tf_op jit(solution)/shard_map/ppermute | solution.py:36
  11.5 24.8 %collective-permute-start.4 = (bf16[1024,128]{1,0:T(8,128)(2,1)S(1)}, bf16[1024,128]{1,0:T(8,128)(2,1)S(1)}, u32[]{:S(2)}, u32[]{:S(2)}) collective-permute-start(bf16[1024,128]{1,0:T(8,128)(2,1)S(1)} %get-tuple-element.48), channel_id=1, source_target_pairs={{0,8},{2,10},{4,12},{6,14},{8,0},{10,2},{12,4},{14,6},{16,24},{18,... | collective-permute-start | bytes 786440 | tf_op jit(solution)/shard_map/ppermute | solution.py:36
  19.4 16.9 %collective-permute-start.3 = (bf16[1024,128]{1,0:T(8,128)(2,1)S(1)}, bf16[1024,128]{1,0:T(8,128)(2,1)S(1)}, u32[]{:S(2)}, u32[]{:S(2)}) collective-permute-start(bf16[1024,128]{1,0:T(8,128)(2,1)S(1)} %get-tuple-element.48), channel_id=1, source_target_pairs={{0,4},{2,6},{4,0},{6,2},{8,12},{10,14},{12,8},{14,10},{16,20},{18,... | collective-permute-start | bytes 786440 | tf_op jit(solution)/shard_map/ppermute | solution.py:36
  21.3 4.4 %collective-permute-start.1 = (bf16[1024,128]{1,0:T(8,128)(2,1)S(1)}, bf16[1024,128]{1,0:T(8,128)(2,1)S(1)}, u32[]{:S(2)}, u32[]{:S(2)}) collective-permute-start(bf16[1024,128]{1,0:T(8,128)(2,1)S(1)} %get-tuple-element.48), channel_id=1, source_target_pairs={{0,2},{2,0},{4,6},{6,4},{8,10},{10,8},{12,14},{14,12},{16,18},{18,... | collective-permute-start | bytes 786440 | tf_op jit(solution)/shard_map/ppermute | solution.py:36
  25.3 16.7 %collective-permute-start.8 = (bf16[256,512]{1,0:T(8,128)(2,1)S(1)}, bf16[256,512]{1,0:T(8,128)(2,1)S(1)}, u32[]{:S(2)}, u32[]{:S(2)}) collective-permute-start(bf16[256,512]{1,0:T(8,128)(2,1)S(1)} %get-tuple-element.57), channel_id=1, source_target_pairs={{0,8},{2,10},{4,12},{6,14},{8,0},{10,2},{12,4},{14,6},{16,24},{18,... | collective-permute-start | bytes 786440 | tf_op jit(solution)/shard_map/ppermute | solution.py:36
  25.7 16.2 %collective-permute-start.9 = (bf16[256,512]{1,0:T(8,128)(2,1)S(1)}, bf16[256,512]{1,0:T(8,128)(2,1)S(1)}, u32[]{:S(2)}, u32[]{:S(2)}) collective-permute-start(bf16[256,512]{1,0:T(8,128)(2,1)S(1)} %get-tuple-element.58), channel_id=1, source_target_pairs={{0,16},{2,18},{4,20},{6,22},{8,24},{10,26},{12,28},{14,30},{16,0},... | collective-permute-start | bytes 786440 | tf_op jit(solution)/shard_map/ppermute | solution.py:36
  30.4 11.5 %collective-permute-start.10 = (bf16[256,512]{1,0:T(8,128)(2,1)S(1)}, bf16[256,512]{1,0:T(8,128)(2,1)S(1)}, u32[]{:S(2)}, u32[]{:S(2)}) collective-permute-start(bf16[256,512]{1,0:T(8,128)(2,1)S(1)} %get-tuple-element.59), channel_id=1, source_target_pairs={{0,4},{2,6},{4,0},{6,2},{8,12},{10,14},{12,8},{14,10},{16,20},{18,... | collective-permute-start | bytes 786440 | tf_op jit(solution)/shard_map/ppermute | solution.py:36
  41.0 12.0 %collective-permute-start.12 = (bf16[256,512]{1,0:T(8,128)(2,1)}, bf16[256,512]{1,0:T(8,128)(2,1)S(1)}, u32[]{:S(2)}, u32[]{:S(2)}) collective-permute-start(bf16[256,512]{1,0:T(8,128)(2,1)} %get-tuple-element.63), channel_id=1, source_target_pairs={{0,8},{2,10},{4,12},{6,14},{8,0},{10,2},{12,4},{14,6},{16,24},{18,... | collective-permute-start | bytes 786440 | tf_op jit(solution)/shard_map/ppermute | solution.py:36
  41.0 13.2 %collective-permute-start.13 = (bf16[256,512]{1,0:T(8,128)(2,1)}, bf16[256,512]{1,0:T(8,128)(2,1)S(1)}, u32[]{:S(2)}, u32[]{:S(2)}) collective-permute-start(bf16[256,512]{1,0:T(8,128)(2,1)} %get-tuple-element.64), channel_id=1, source_target_pairs={{0,16},{2,18},{4,20},{6,22},{8,24},{10,26},{12,28},{14,30},{16,0},... | collective-permute-start | bytes 786440 | tf_op jit(solution)/shard_map/ppermute | solution.py:36
  42.0 7.0 %collective-permute-start.11 = (bf16[256,512]{1,0:T(8,128)(2,1)S(1)}, bf16[256,512]{1,0:T(8,128)(2,1)S(1)}, u32[]{:S(2)}, u32[]{:S(2)}) collective-permute-start(bf16[256,512]{1,0:T(8,128)(2,1)S(1)} %get-tuple-element.61), channel_id=1, source_target_pairs={{0,2},{2,0},{4,6},{6,4},{8,10},{10,8},{12,14},{14,12},{16,18},{18,... | collective-permute-start | bytes 786440 | tf_op jit(solution)/shard_map/ppermute | solution.py:36
  42.0 12.3 %collective-permute-start.14 = (bf16[256,512]{1,0:T(8,128)(2,1)}, bf16[256,512]{1,0:T(8,128)(2,1)S(1)}, u32[]{:S(2)}, u32[]{:S(2)}) collective-permute-start(bf16[256,512]{1,0:T(8,128)(2,1)} %get-tuple-element.66), channel_id=1, source_target_pairs={{0,2},{2,0},{4,6},{6,4},{8,10},{10,8},{12,14},{14,12},{16,18},{18,... | collective-permute-start | bytes 786440 | tf_op jit(solution)/shard_map/ppermute | solution.py:36
  42.5 11.8 %collective-permute-start.15 = (bf16[256,512]{1,0:T(8,128)(2,1)}, bf16[256,512]{1,0:T(8,128)(2,1)S(1)}, u32[]{:S(2)}, u32[]{:S(2)}) collective-permute-start(bf16[256,512]{1,0:T(8,128)(2,1)} %get-tuple-element.68), channel_id=1, source_target_pairs={{0,4},{2,6},{4,0},{6,2},{8,12},{10,14},{12,8},{14,10},{16,20},{18,... | collective-permute-start | bytes 786440 | tf_op jit(solution)/shard_map/ppermute | solution.py:36
  44.1 12.2 %all-to-all-start = ((f32[32,1,128]{2,1,0:T(1,128)}), f32[32,1,128]{2,1,0:T(1,128)S(1)}, u32[]{:S(2)}, u32[]{:S(2)}) async-start(f32[32,1,128]{2,1,0:T(1,128)} %get-tuple-element.71), calls=%async_computation | async-start | bytes 32768 | tf_op jit(solution)/shard_map/all_to_all | solution.py:509
